TPU v7x, 128 devices: a whole 4x4x4 slice. The times are simulated.
128 devices in a mesh: queue: 4 (over y), dp: 32 (over x, z, core).
Axes of the slice: x: 4, y: 4, z: 4, core: 2. Of those that a mesh axis runs over, the one named last changes fastest.
Arguments:
- features: bfloat16 [4096, 49, 2048], P(('queue', 'dp')), may hold values from -40 to 40
- shuffle: int32 [4, 1024], P('queue'), may hold values from 0 to 1023, as said below
- positive: int32 [4096], P(('queue', 'dp')), may hold values from 0 to 1023, as said below
- queries: bfloat16 [4096, 128], P(('queue', 'dp')), may hold values from -8 to 8
- queue_keys: bfloat16 [65536, 128], P('queue'), may hold values from -8 to 8
- reduce_weight: bfloat16 [2048, 512], replicated, may hold values from -0.125 to 0.125
- gain_one: float32 [512], replicated, may hold values from 0.1 to 1.9
- shift_one: float32 [512], replicated, may hold values from -3 to 3
- w_spatial: bfloat16 [9, 512, 512], replicated, may hold values from -0.09375 to 0.09375
- gain_two: float32 [512], replicated, may hold values from 0.1 to 1.9
- shift_two: float32 [512], replicated, may hold values from -3 to 3
- w_expand: bfloat16 [512, 2048], replicated, may hold values from -0.25 to 0.25
- gain_three: float32 [2048], replicated, may hold values from 0.1 to 1.9
- shift_three: float32 [2048], replicated, may hold values from -3 to 3
- w_project: bfloat16 [2048, 128], replicated, may hold values from -0.125 to 0.125
Outputs:
- loss_vals: float32 [4096], P(('queue', 'dp'))
- key_rows: bfloat16 [4096, 128], P(('queue', 'dp'))
Inputs may be any that keep to these rules, and one draw needn't show every extreme that they name: `shuffle`: each row is a permutation of 0 to 1023, and each block of 32 slots k * 32 to (k + 1) * 32 - 1 holds exactly one image from each block of 32 images. Within each queue group of 1024 queries, positive is a permutation of 0 to 1023.
All inputs are finite; a program needn't handle non-finite values.
Results may differ from a plain program's by a relative error of at most 0.0075.
Values may be sent and summed in bfloat16 or wider, within the bound.
No kernel may reach another device: no remote copies, remote signals or barrier semaphores. Data moves between devices by JAX's collectives and lax.ppermute only.
A program may use at most 128 MiB of HBM per device.

v0:
```python
import functools
import math

import jax
import jax.numpy as jnp
from jax import lax
from jax.experimental import pallas as pl
from jax.experimental.pallas import tpu as pltpu
from jax.sharding import PartitionSpec as P


SIDE = 7
EPS = 1e-05
UNIT_EPS = 1e-06
TEMP = 0.2
F32 = jnp.float32
BF16 = jnp.bfloat16
VMEM = pl.BlockSpec(memory_space=pltpu.VMEM)
SMEM = pl.BlockSpec(memory_space=pltpu.SMEM)


def params(limit_mib):
    return pltpu.CompilerParams(
        dimension_semantics=("arbitrary",), vmem_limit_bytes=limit_mib * 1024 * 1024
    )


def dot32(a, b):
    return jnp.dot(a, b, preferred_element_type=F32)


def pieces(values):
    high = values.astype(BF16)
    rest = values - high.astype(F32)
    middle = rest.astype(BF16)
    low = (rest - middle.astype(F32)).astype(BF16)
    return jnp.concatenate([high, middle, low], 0)


def set_onehots(me, shuffle, count):
    total = shuffle.shape[1]
    image = lax.broadcasted_iota(jnp.int32, (count, total), 0) + me * count
    here = (shuffle == image).astype(F32)
    slot = lax.broadcasted_iota(jnp.int32, (total, total // count), 0)
    low = lax.broadcasted_iota(jnp.int32, (total, total // count), 1) * count
    inside = jnp.logical_and(slot >= low, slot < low + count)
    by_image = dot32(here.astype(BF16), inside.astype(F32).astype(BF16))
    by_set = jnp.transpose(by_image, (1, 0))
    return [jnp.concatenate([p] * 3, 1).astype(BF16) for p in (by_set, by_image)]


def reorder(onehot, values):
    return dot32(onehot, pieces(values))


def split_halves(core, values, keep_ref, send_ref, start):
    half = values.shape[1] // 2
    low, high = values[:, :half], values[:, half:]
    keep_ref[:, start : start + half] = jnp.where(core == 0, low, high)
    send_ref[:, start : start + half] = jnp.where(core == 0, high, low)


def join_halves(core, mine, other):
    low = jnp.where(core == 0, mine, other)
    high = jnp.where(core == 0, other, mine)
    return jnp.concatenate([low, high], 1)


CHUNKS = ((0, 7), (7, 14), (21, 28))


def reduce_kernel(
    me_ref,
    x_hbm,
    w_hbm,
    shuffle_hbm,
    y_ref,
    keep_ref,
    send_ref,
    by_set_ref,
    by_image_ref,
    x_ref,
    w_ref,
    shuffle_ref,
    sems,
):
    _, count, channels = x_ref.shape
    mid = w_ref.shape[1]
    weight_copy = pltpu.make_async_copy(w_hbm, w_ref, sems.at[0])
    weight_copy.start()
    copies = []
    for n, (first, size) in enumerate(CHUNKS):
        part = pl.ds(first, size)
        copies.append(pltpu.make_async_copy(x_hbm.at[part], x_ref.at[part], sems.at[n + 1]))
        copies[-1].start()
    shuffle_copy = pltpu.make_async_copy(shuffle_hbm, shuffle_ref, sems.at[len(CHUNKS) + 1])
    shuffle_copy.start()
    shuffle_copy.wait()
    by_set, by_image = set_onehots(me_ref[0], shuffle_ref[...], count)
    by_set_ref[...] = by_set
    by_image_ref[...] = by_image
    weight_copy.wait()
    s1 = jnp.zeros((count, mid), F32)
    s2 = jnp.zeros((count, mid), F32)
    for (first, size), copy in zip(CHUNKS, copies):
        copy.wait()
        part = pl.ds(first, size)
        y = dot32(x_ref[part].reshape(size * count, channels), w_ref[...])
        y = y.reshape(size, count, mid)
        y_ref[part] = y
        s1 += jnp.sum(y, 0)
        s2 += jnp.sum(y * y, 0)
    core = jnp.bitwise_and(me_ref[0], 1)
    split_halves(core, reorder(by_set, s1), keep_ref, send_ref, 0)
    split_halves(core, reorder(by_set, s2), keep_ref, send_ref, mid // 2)


def reduce_stage(me, x, weight, shuffle):
    places, count, channels = x.shape
    mid = weight.shape[1]
    sets = shuffle.shape[1] // count
    hbm = pl.BlockSpec(memory_space=pltpu.HBM)
    return pl.pallas_call(
        reduce_kernel,
        name="reduce",
        in_specs=[SMEM, hbm, hbm, hbm],
        out_specs=[VMEM] * 6,
        out_shape=[
            jax.ShapeDtypeStruct((places, count, mid), F32),
            jax.ShapeDtypeStruct((count, mid), F32),
            jax.ShapeDtypeStruct((count, mid), F32),
            jax.ShapeDtypeStruct((sets, 3 * count), BF16),
            jax.ShapeDtypeStruct((count, 3 * sets), BF16),
            jax.ShapeDtypeStruct(x.shape, x.dtype),
        ],
        scratch_shapes=[
            pltpu.VMEM(weight.shape, weight.dtype),
            pltpu.VMEM(shuffle.shape, shuffle.dtype),
            pltpu.SemaphoreType.DMA((len(CHUNKS) + 2,)),
        ],
        compiler_params=pltpu.CompilerParams(vmem_limit_bytes=24 * 1024 * 1024),
        cost_estimate=pl.CostEstimate(
            flops=2 * places * count * channels * mid,
            bytes_accessed=2 * x.size + 4 * places * count * mid,
            transcendentals=0,
        ),
    )(me, *[pltpu.with_memory_space_constraint(v, pltpu.HBM) for v in (x, weight, shuffle)])


def scale_shift(core, mine, other, onehot, gain, shift, rows):
    half = mine.shape[1] // 2
    total1 = join_halves(core, mine[:, :half], other[:, :half])
    total2 = join_halves(core, mine[:, half:], other[:, half:])
    average = total1 / rows
    spread = total2 / rows - average * average
    scale = lax.rsqrt(spread + EPS) * gain
    return reorder(onehot, scale), reorder(onehot, shift - average * scale)


def conv_kernel(
    rows,
    core_ref,
    y_ref,
    mine_ref,
    other_ref,
    by_set_ref,
    by_image_ref,
    gain_ref,
    shift_ref,
    w_ref,
    z_ref,
    keep_ref,
    send_ref,
    act,
    scale_s,
    shift_s,
    s1,
    s2,
):
    step = pl.program_id(0)
    side = SIDE
    _, count, mid = y_ref.shape

    def norm(row):
        a = y_ref[pl.ds(row * side, side)] * scale_s[...][None] + shift_s[...][None]
        act[row] = jnp.maximum(a, 0.0).astype(BF16)

    def conv_row(row, dys):
        for dx in (0, -1, 1):
            lo, hi = max(0, -dx), side - max(0, dx)
            window = [act[row + dy, lo + dx : hi + dx].reshape((hi - lo) * count, mid) for dy in dys]
            weight = [w_ref[3 * (dy + 1) + dx + 1] for dy in dys]
            part = dot32(jnp.concatenate(window, 1), jnp.concatenate(weight, 0))
            part = part.reshape(hi - lo, count, mid)
            if dx == 0:
                z_ref[pl.ds(row * side, side)] = part
            else:
                z_ref[pl.ds(row * side + lo, hi - lo)] += part
        z = z_ref[pl.ds(row * side, side)]
        s1[...] += jnp.sum(z, 0)
        s2[...] += jnp.sum(z * z, 0)

    @pl.when(step == 0)
    def _():
        scale, shift = scale_shift(
            core_ref[0],
            mine_ref[...],
            other_ref[...],
            by_image_ref[...],
            gain_ref[...],
            shift_ref[...],
            rows,
        )
        scale_s[...] = scale
        shift_s[...] = shift
        s1[...] = jnp.zeros_like(s1)
        s2[...] = jnp.zeros_like(s2)
        norm(0)
        norm(1)
        conv_row(0, (0, 1))
        norm(2)

    @pl.when(jnp.logical_and(step > 0, step < side - 1))
    def _():
        conv_row(step, (-1, 0, 1))
        norm(jnp.minimum(step + 2, side - 1))

    @pl.when(step == side - 1)
    def _():
        conv_row(side - 1, (-1, 0))
        core = core_ref[0]
        by_set = by_set_ref[...]
        split_halves(core, reorder(by_set, s1[...]), keep_ref, send_ref, 0)
        split_halves(core, reorder(by_set, s2[...]), keep_ref, send_ref, mid // 2)


def conv_stage(rows, core, y, mine, other, by_set, by_image, gain, shift, weight):
    places, count, mid = y.shape
    return pl.pallas_call(
        functools.partial(conv_kernel, rows),
        name="conv",
        grid=(SIDE,),
        in_specs=[SMEM] + [VMEM] * 8,
        out_specs=[VMEM] * 3,
        out_shape=[
            jax.ShapeDtypeStruct((places, count, mid), F32),
            jax.ShapeDtypeStruct((count, mid), F32),
            jax.ShapeDtypeStruct((count, mid), F32),
        ],
        scratch_shapes=[
            pltpu.VMEM((SIDE, SIDE, count, mid), BF16),
            pltpu.VMEM((count, mid), F32),
            pltpu.VMEM((count, mid), F32),
            pltpu.VMEM((count, mid), F32),
            pltpu.VMEM((count, mid), F32),
        ],
        compiler_params=params(16),
        cost_estimate=pl.CostEstimate(
            flops=2 * 361 * count * mid * mid,
            bytes_accessed=8 * places * count * mid + 2 * weight.size,
            transcendentals=0,
        ),
    )(core, y, mine, other, by_set, by_image, gain, shift, weight)


COLUMNS = 256


def center_kernel(gain_ref, shift_ref, w_ref, act_center_ref, center_ref):
    gain, shift = gain_ref[...], shift_ref[...]
    ratio = jnp.abs(shift) / gain
    value = jnp.maximum(shift, 0.0) + 0.4 * gain * jnp.exp(-ratio * (1.1 + 0.45 * ratio))
    value = value.astype(BF16)
    act_center_ref[...] = value.astype(F32)
    wide = dot32(jnp.broadcast_to(value, (16, value.shape[1])), w_ref[...])
    center_ref[...] = wide[:1]


def center_stage(gain, shift, weight):
    return pl.pallas_call(
        center_kernel,
        name="center",
        in_specs=[VMEM] * 3,
        out_specs=[VMEM] * 2,
        out_shape=[
            jax.ShapeDtypeStruct(gain.shape, F32),
            jax.ShapeDtypeStruct((1, weight.shape[1]), F32),
        ],
        compiler_params=pltpu.CompilerParams(vmem_limit_bytes=8 * 1024 * 1024),
        cost_estimate=pl.CostEstimate(
            flops=32 * weight.size, bytes_accessed=2 * weight.size, transcendentals=gain.size
        ),
    )(gain, shift, weight)


def expand_kernel(
    rows,
    core_ref,
    z_ref,
    mine_ref,
    other_ref,
    by_set_ref,
    by_image_ref,
    gain_ref,
    shift_ref,
    act_center_ref,
    center_ref,
    w_ref,
    e_ref,
    keep_ref,
    send_ref,
    act,
    sq_s,
):
    places, count, mid = z_ref.shape
    wide = w_ref.shape[1]
    core = core_ref[0]
    by_set = by_set_ref[...]
    scale, shift = scale_shift(
        core,
        mine_ref[...],
        other_ref[...],
        by_image_ref[...],
        gain_ref[...],
        shift_ref[...],
        rows,
    )
    total = jnp.zeros((count, mid), F32)
    for row in range(0, places, SIDE):
        a = z_ref[row : row + SIDE] * scale[None] + shift[None]
        a = jnp.maximum(a, 0.0).astype(BF16)
        act[row : row + SIDE] = a
        total += jnp.sum(a.astype(F32), 0)
    flat = act[...].reshape(places * count, mid)
    for j in range(0, wide, COLUMNS):
        e = dot32(flat, w_ref[:, j : j + COLUMNS]).reshape(places, count, COLUMNS)
        e_ref[:, :, j : j + COLUMNS] = e
        d = e - center_ref[:, j : j + COLUMNS][None]
        sq_s[:, j : j + COLUMNS] = jnp.sum(d * d, 0)
    total = total - places * act_center_ref[...]
    split_halves(core, reorder(by_set, total), keep_ref, send_ref, 0)
    split_halves(core, reorder(by_set, sq_s[...]), keep_ref, send_ref, mid // 2)


def expand_stage(
    rows, core, z, mine, other, by_set, by_image, gain, shift, act_center, center, weight
):
    places, count, mid = z.shape
    wide = weight.shape[1]
    sums = (mid + wide) // 2
    return pl.pallas_call(
        functools.partial(expand_kernel, rows),
        name="expand",
        in_specs=[SMEM] + [VMEM] * 10,
        out_specs=[VMEM] * 3,
        out_shape=[
            jax.ShapeDtypeStruct((places, count, wide), F32),
            jax.ShapeDtypeStruct((count, sums), F32),
            jax.ShapeDtypeStruct((count, sums), F32),
        ],
        scratch_shapes=[
            pltpu.VMEM((places, count, mid), BF16),
            pltpu.VMEM((count, wide), F32),
        ],
        compiler_params=pltpu.CompilerParams(vmem_limit_bytes=16 * 1024 * 1024),
        cost_estimate=pl.CostEstimate(
            flops=2 * places * count * mid * wide,
            bytes_accessed=4 * places * count * (mid + wide),
            transcendentals=0,
        ),
    )(core, z, mine, other, by_set, by_image, gain, shift, act_center, center, weight)


def merge_kernel(
    rows,
    core_ref,
    e_ref,
    x_ref,
    mine_ref,
    other_ref,
    by_image_ref,
    gain_ref,
    shift_ref,
    act_center_ref,
    center_ref,
    w_ref,
    proj_ref,
    key_ref,
    copies_ref,
    scale_s,
    shift_s,
    pool,
):
    places, count, wide = e_ref.shape
    core, by_image = core_ref[0], by_image_ref[...]
    mine, other = mine_ref[...], other_ref[...]
    cut = w_ref.shape[0] // 2
    sums = join_halves(core, mine[:, :cut], other[:, :cut]) + rows * act_center_ref[...]
    squares = join_halves(core, mine[:, cut:], other[:, cut:])
    three = dot32(pieces(sums), w_ref[...])
    sets = sums.shape[0]
    average = (three[:sets] + (three[sets : 2 * sets] + three[2 * sets :])) / rows
    away = average - center_ref[...]
    spread = squares / rows - away * away
    scale = lax.rsqrt(spread + EPS) * gain_ref[...]
    scale_s[...] = reorder(by_image, scale)
    shift_s[...] = reorder(by_image, shift_ref[...] - average * scale)
    for j in range(0, wide, COLUMNS):
        cols = slice(j, j + COLUMNS)
        sc, sh = scale_s[:, cols], shift_s[:, cols]
        total = jnp.zeros((count, COLUMNS), F32)
        for place in range(places):
            y = e_ref[place, :, cols] * sc + sh + x_ref[place, :, cols].astype(F32)
            total += jnp.maximum(y, 0.0)
        pool[:, cols] = total
    pooled = (pool[...] / places).astype(BF16)
    u = dot32(pooled, proj_ref[...])
    key = (u * lax.rsqrt(jnp.sum(u * u, 1, keepdims=True) + UNIT_EPS)).astype(BF16)
    key_ref[...] = key
    copies_ref[...] = jnp.broadcast_to(key[None], copies_ref.shape)


def merge_stage(
    rows, core, peers, e, x, mine, other, by_image, gain, shift, act_center, center, weight, proj
):
    places, count, wide = e.shape
    feat = proj.shape[1]
    return pl.pallas_call(
        functools.partial(merge_kernel, rows),
        name="merge",
        in_specs=[SMEM] + [VMEM] * 11,
        out_specs=[VMEM] * 2,
        out_shape=[
            jax.ShapeDtypeStruct((count, feat), BF16),
            jax.ShapeDtypeStruct((peers, count, feat), BF16),
        ],
        scratch_shapes=[
            pltpu.VMEM((count, wide), F32),
            pltpu.VMEM((count, wide), F32),
            pltpu.VMEM((count, wide), F32),
        ],
        compiler_params=pltpu.CompilerParams(vmem_limit_bytes=16 * 1024 * 1024),
        cost_estimate=pl.CostEstimate(
            flops=8 * places * count * wide,
            bytes_accessed=2 * x.size + 4 * e.size,
            transcendentals=0,
        ),
    )(core, e, x, mine, other, by_image, gain, shift, act_center, center, weight, proj)


def negative_kernel(factor, q_ref, k_ref, out_ref):
    @pl.when(pl.program_id(0) == 0)
    def _():
        out_ref[...] = jnp.zeros_like(out_ref)

    keys = k_ref[...]
    wide = keys.astype(F32)
    norm = lax.rsqrt(jnp.sum(wide * wide, 1, keepdims=True) + UNIT_EPS) * factor
    score = lax.dot_general(
        keys, q_ref[...], (((1,), (1,)), ((), ())), preferred_element_type=F32
    )
    out_ref[...] += jnp.sum(jnp.exp2(score * norm), 0, keepdims=True)


def negative_stage(queries, keys, part, parts):
    count, feat = queries.shape
    total = keys.shape[0] // parts
    block = math.gcd(total, 2048)
    steps = total // block
    return pl.pallas_call(
        functools.partial(negative_kernel, math.log2(math.e) / TEMP),
        name="negative",
        grid=(steps,),
        in_specs=[VMEM, pl.BlockSpec((block, feat), lambda i: (i + part * steps, 0))],
        out_specs=pl.BlockSpec((1, count), lambda i: (0, 0)),
        out_shape=jax.ShapeDtypeStruct((1, count), F32),
        compiler_params=params(8),
        cost_estimate=pl.CostEstimate(
            flops=2 * total * count * feat,
            bytes_accessed=2 * total * feat,
            transcendentals=total * count,
        ),
    )(queries, pltpu.with_memory_space_constraint(keys, pltpu.HBM))


def loss_kernel(table_ref, u_ref, pos_ref, neg_ref, loss_ref):
    logits = lax.dot_general(
        table_ref[...], u_ref[...], (((1,), (1,)), ((), ())), preferred_element_type=F32
    )
    row = lax.broadcasted_iota(jnp.int32, logits.shape, 0)
    picked = jnp.sum(jnp.where(row == pos_ref[...], logits, 0.0), 0, keepdims=True) / TEMP
    loss_ref[...] = jnp.log(jnp.exp(picked) + neg_ref[...]) - picked


def loss_stage(table, units, positive, negatives):
    return pl.pallas_call(
        loss_kernel,
        name="loss",
        in_specs=[VMEM] * 4,
        out_specs=VMEM,
        out_shape=jax.ShapeDtypeStruct(positive.shape, F32),
        compiler_params=pltpu.CompilerParams(vmem_limit_bytes=8 * 1024 * 1024),
    )(table, units, positive, negatives)


def unit_rows(values):
    as_float = values.astype(F32)
    return (
        as_float * lax.rsqrt(jnp.sum(as_float * as_float, -1, keepdims=True) + UNIT_EPS)
    ).astype(BF16)


RING = 4


def swap_core():
    return [(i, i ^ 1) for i in range(2 * RING * RING)]


def ring_swap(k, flip):
    pairs = []
    for i in range(2 * RING * RING):
        x, z, c = i // (2 * RING), (i // 2) % RING, i % 2
        if (c == 1) != flip:
            x = x ^ k
        else:
            z = z ^ k
        pairs.append((i, (x * RING + z) * 2 + c))
    return pairs


def queue_swap(values, k):
    return lax.ppermute(values, "queue", [(i, i ^ k) for i in range(RING)])


def reduce_sets(keep, send, side_work, side_input, wire):
    total = keep + lax.ppermute(send, "dp", swap_core())
    for turn, work in enumerate(side_work):
        parts = []
        sent = total.astype(wire)
        for k in (1, 2, 3):
            parts.append(lax.ppermute(sent, "dp", ring_swap(k, turn == 1)).astype(F32))
        held, free = work(lax.optimization_barrier((side_input, total))[0])
        parts, held = lax.optimization_barrier((parts, held))
        side_input = (held, free)
        total = (total + parts[0]) + (parts[1] + parts[2])
    return total, lax.ppermute(total, "dp", swap_core()), side_input


def on_device(
    features,
    shuffle,
    positive,
    queries,
    queue_keys,
    reduce_weight,
    gain_one,
    shift_one,
    w_spatial,
    gain_two,
    shift_two,
    w_expand,
    gain_three,
    shift_three,
    w_project,
):
    count, places, _ = features.shape
    peers = lax.axis_size("dp")
    me = lax.axis_index("dp").astype(jnp.int32).reshape(1)
    core = jnp.bitwise_and(me, 1)
    rows = count * places
    x = jnp.transpose(features, (1, 0, 2))
    units = unit_rows(queries)
    gain_two, shift_two = gain_two[None], shift_two[None]

    def gather_one(own):
        return None, (own, queue_swap(own, 1))

    def gather_two(state):
        pair = jnp.concatenate(state[1], 0)
        return None, (pair, queue_swap(pair, 3))

    def negative_one(state):
        here, gain, shift = state
        centers = center_stage(gain, shift, w_expand)
        return (here, negative_stage(here, queue_keys, 0, 2), centers), None

    def negative_two(state):
        here, sums, centers = state[0]
        sums = sums + negative_stage(here, queue_keys, 1, 2)
        return (sums, centers), queue_swap(sums[:, 2 * count :], 3)

    def return_two(state):
        sums = state[0] + state[1]
        return None, (sums[:, :count], queue_swap(sums[:, count:], 1))

    def return_done(state):
        return sum(state[1]), None

    y, keep, send, by_set, by_image, x = reduce_stage(me, x, reduce_weight, shuffle)
    mine, other, (_, asked) = reduce_sets(keep, send, (gather_one, gather_two), units, F32)
    asked = jnp.concatenate(asked, 0)
    z, keep, send = conv_stage(
        rows, core, y, mine, other, by_set, by_image, gain_one[None], shift_one[None], w_spatial
    )
    mine, other, ((sums, centers), told) = reduce_sets(
        keep, send, (negative_one, negative_two), (asked, gain_two, shift_two), F32
    )
    e, keep, send = expand_stage(
        rows, core, z, mine, other, by_set, by_image, gain_two, shift_two, *centers, w_expand
    )
    mine, other, (negatives, _) = reduce_sets(
        keep, send, (return_two, return_done), (sums[:, : 2 * count], told), BF16
    )
    key_rows, copies = merge_stage(
        rows,
        core,
        peers,
        e,
        x,
        mine,
        other,
        by_image,
        gain_three[None],
        shift_three[None],
        *centers,
        w_expand,
        w_project,
    )
    table = lax.all_to_all(copies, "dp", split_axis=0, concat_axis=0, tiled=True)
    table = table.reshape(peers * count, -1)
    loss_vals = loss_stage(table, units, positive.reshape(1, count), negatives)
    return (loss_vals.reshape(count), key_rows)


def solution(mesh):
    placed = (
        P(("queue", "dp"), None, None),
        P("queue", None),
        P(("queue", "dp")),
        P(("queue", "dp"), None),
        P("queue", None),
    ) + (P(),) * 10
    return jax.shard_map(
        on_device,
        mesh=mesh,
        in_specs=placed,
        out_specs=(P(("queue", "dp")), P(("queue", "dp"), None)),
        check_vma=False,
    )
```

profile of v0, /device:TPU:0, one launch (start us, length us, event | category | flops | bytes accessed | tf_op | source)
XLA Modules:
  0.0 106.2 jit_solution(7326435459902780382)
XLA Ops:
  0.7 7.8 %reduce.1 = (f32[49,32,512]{2,1,0:T(8,128)S(1)}, f32[32,512]{1,0:T(8,128)S(1)}, f32[32,512]{1,0:T(8,128)S(1)}, bf16[32,96]{1,0:T(8,128)(2,1)S(1)}, bf16[32,96]{1...) custom-call(s32[1]{0:T(128)} %bitcast.me_ref, bf16[49,32,2048]{2,1,0:T(8,128)(2,1)} %bitcast.23, ...), custom_call_target="tpu_custom_call" | custom-call | flops 3288334336 | bytes 9633792 | tf_op jit(solution)/shard_map/reduce/pallas_call | solution.py:123
  8.4 0.1 collective-permute-start
  8.5 1.2 %collective-permute-done = f32[32,512]{1,0:T(8,128)S(1)} collective-permute-done((f32[32,512]{1,0:T(8,128)S(1)}, f32[32,512]{1,0:T(8,128)S(1)}, u32[]{:S(2)}, u32[]{:S(2)}) %collective-permute-start) | collective-permute-done | bytes 65568 | tf_op jit(solution)/shard_map/ppermute | solution.py:537
  9.8 2.1 %collective-permute-start.1 = (f32[32,512]{1,0:T(8,128)S(1)}, f32[32,512]{1,0:T(8,128)S(1)}, u32[]{:S(2)}, u32[]{:S(2)}) collective-permute-start(f32[32,512]{1,0:T(8,128)S(1)} %add.83), channel_id=1, source_target_pairs={{0,2},{1,9},{2,0},{3,11},{4,6},{5,13},{6,4},{7,15},{8,10},{9,1},{1... | collective-permute-start | bytes 196616 | tf_op jit(solution)/shard_map/ppermute | solution.py:542
  11.9 3.6 %collective-permute-start.2 = (f32[32,512]{1,0:T(8,128)S(1)}, f32[32,512]{1,0:T(8,128)S(1)}, u32[]{:S(2)}, u32[]{:S(2)}) collective-permute-start(f32[32,512]{1,0:T(8,128)S(1)} %add.83), channel_id=1, source_target_pairs={{0,4},{1,17},{2,6},{3,19},{4,0},{5,21},{6,2},{7,23},{8,12},{9,25},... | collective-permute-start | bytes 196616 | tf_op jit(solution)/shard_map/ppermute | solution.py:542
  15.5 0.1 fusion
  15.6 0.0 collective-permute-done.1
  15.6 2.8 %collective-permute-done.2 = f32[32,512]{1,0:T(8,128)S(1)} collective-permute-done((f32[32,512]{1,0:T(8,128)S(1)}, f32[32,512]{1,0:T(8,128)S(1)}, u32[]{:S(2)}, u32[]{:S(2)}) %collective-permute-start.2) | collective-permute-done | bytes 65568 | tf_op jit(solution)/shard_map/ppermute | solution.py:542
  18.4 2.5 %collective-permute-done.3 = f32[32,512]{1,0:T(8,128)S(1)} collective-permute-done((f32[32,512]{1,0:T(8,128)S(1)}, f32[32,512]{1,0:T(8,128)S(1)}, u32[]{:S(2)}, u32[]{:S(2)}) %collective-permute-start.3) | collective-permute-done | bytes 65568 | tf_op jit(solution)/shard_map/ppermute | solution.py:542
  21.0 1.6 %collective-permute-start.4 = (f32[32,512]{1,0:T(8,128)S(1)}, f32[32,512]{1,0:T(8,128)S(1)}, u32[]{:S(2)}, u32[]{:S(2)}) collective-permute-start(f32[32,512]{1,0:T(8,128)S(1)} %add_add_fusion.5), channel_id=1, source_target_pairs={{0,8},{1,3},{2,10},{3,1},{4,12},{5,7},{6,14},{7,5},{8,0},{9,11},{1... | collective-permute-start | bytes 196616 | tf_op jit(solution)/shard_map/ppermute | solution.py:542
  22.6 2.7 %collective-permute-start.5 = (f32[32,512]{1,0:T(8,128)S(1)}, f32[32,512]{1,0:T(8,128)S(1)}, u32[]{:S(2)}, u32[]{:S(2)}) collective-permute-start(f32[32,512]{1,0:T(8,128)S(1)} %add_add_fusion.5), channel_id=1, source_target_pairs={{0,16},{1,5},{2,18},{3,7},{4,20},{5,1},{6,22},{7,3},{8,24},{9,13},... | collective-permute-start | bytes 196616 | tf_op jit(solution)/shard_map/ppermute | solution.py:542
  25.3 0.5 collective-permute-start.6
  25.8 0.0 collective-permute-done.4
  25.8 2.6 %collective-permute-done.5 = f32[32,512]{1,0:T(8,128)S(1)} collective-permute-done((f32[32,512]{1,0:T(8,128)S(1)}, f32[32,512]{1,0:T(8,128)S(1)}, u32[]{:S(2)}, u32[]{:S(2)}) %collective-permute-start.5) | collective-permute-done | bytes 65568 | tf_op jit(solution)/shard_map/ppermute | solution.py:542
  28.3 2.4 %collective-permute-done.6 = f32[32,512]{1,0:T(8,128)S(1)} collective-permute-done((f32[32,512]{1,0:T(8,128)S(1)}, f32[32,512]{1,0:T(8,128)S(1)}, u32[]{:S(2)}, u32[]{:S(2)}) %collective-permute-start.6) | collective-permute-done | bytes 65568 | tf_op jit(solution)/shard_map/ppermute | solution.py:542
  30.8 0.1 collective-permute-start.7
  30.9 0.1 fusion.1.u_ref
  30.9 1.6 %collective-permute-start.12 = (bf16[32,128]{1,0:T(8,128)(2,1)S(1)}, bf16[32,128]{1,0:T(8,128)(2,1)S(1)}, u32[]{:S(2)}, u32[]{:S(2)}) collective-permute-start(bf16[32,128]{1,0:T(8,128)(2,1)S(1)} %fusion.1.u_ref), channel_id=1, source_target_pairs={{0,32},{32,0},{64,96},{96,64},{1,33},{33,1},{65,97},{97,65},{2,34}... | collective-permute-start | bytes 24584 | tf_op jit(solution)/shard_map/ppermute | solution.py:533
  32.5 2.1 %collective-permute-done.12 = bf16[32,128]{1,0:T(8,128)(2,1)S(1)} collective-permute-done((bf16[32,128]{1,0:T(8,128)(2,1)S(1)}, bf16[32,128]{1,0:T(8,128)(2,1)S(1)}, u32[]{:S(2)}, u32[]{:S(2)}) %collective-permute-start.12) | collective-permute-done | bytes 8224 | tf_op jit(solution)/shard_map/ppermute | solution.py:533
  34.6 0.0 copy-start
  34.7 0.0 copy-start.4
  34.7 0.0 copy-start.5
  34.7 8.0 %conv.1 = (f32[49,32,512]{2,1,0:T(8,128)S(1)}, f32[32,512]{1,0:T(8,128)S(1)}, f32[32,512]{1,0:T(8,128)S(1)}) custom-call(s32[1]{0:T(128)S(6)} %and.4.core_ref, f32[49,32,512]{2,1,0:T(8,128)S(1)} %get-tuple-element.58.y_ref, f32[32,512]{1,0:T(8,128)S(1)} %add_add_fusion.4.mine_ref, f32[32,512]{1,0:T(8,128)S(1)} %collective-permute-done.7.other_ref, ...), custom_call_target="tpu_custom_call" | custom-call | flops 6056574976 | bytes 11141120 | tf_op jit(solution)/shard_map/conv/pallas_call | solution.py:239
  42.7 0.1 collective-permute-start.8
  42.8 3.1 %collective-permute-start.13 = (bf16[64,128]{1,0:T(8,128)(2,1)S(1)}, bf16[64,128]{1,0:T(8,128)(2,1)S(1)}, u32[]{:S(2)}, u32[]{:S(2)}) collective-permute-start(bf16[64,128]{1,0:T(8,128)(2,1)S(1)} %pad_maximum_fusion.1), channel_id=1, source_target_pairs={{0,96},{32,64},{64,32},{96,0},{1,97},{33,65},{65,33},{97,1},{2,98}... | collective-permute-start | bytes 49160 | tf_op jit(solution)/shard_map/ppermute | solution.py:533
  45.9 0.4 collective-permute-start.10
  46.3 1.0 collective-permute-start.11
  47.3 2.2 %collective-permute-start.9 = (f32[32,512]{1,0:T(8,128)S(1)}, f32[32,512]{1,0:T(8,128)S(1)}, u32[]{:S(2)}, u32[]{:S(2)}) collective-permute-start(f32[32,512]{1,0:T(8,128)S(1)} %add.90), channel_id=1, source_target_pairs={{0,2},{1,9},{2,0},{3,11},{4,6},{5,13},{6,4},{7,15},{8,10},{9,1},{1... | collective-permute-start | bytes 196616 | tf_op jit(solution)/shard_map/ppermute | solution.py:542
  49.5 0.0 collective-permute-done.13
  49.5 0.4 center.1
  49.9 3.5 %negative.2 = f32[1,128]{1,0:T(1,128)S(1)} custom-call(bf16[128,128]{1,0:T(8,128)(2,1)S(1)} %pad_maximum_fusion.q_ref, bf16[16384,128]{1,0:T(8,128)(2,1)} %k_ref.3), custom_call_target="tpu_custom_call" | custom-call | flops 268435456 | bytes 2097152 | tf_op jit(solution)/shard_map/negative/pallas_call | solution.py:470
  53.4 0.0 collective-permute-done.11
  53.5 0.0 collective-permute-done.9
  53.5 0.1 collective-permute-start.14
  53.6 1.9 %collective-permute-start.15 = (f32[32,512]{1,0:T(8,128)S(1)}, f32[32,512]{1,0:T(8,128)S(1)}, u32[]{:S(2)}, u32[]{:S(2)}) collective-permute-start(f32[32,512]{1,0:T(8,128)S(1)} %add_add_fusion.3), channel_id=1, source_target_pairs={{0,16},{1,5},{2,18},{3,7},{4,20},{5,1},{6,22},{7,3},{8,24},{9,13},... | collective-permute-start | bytes 196616 | tf_op jit(solution)/shard_map/ppermute | solution.py:542
  55.5 2.8 %collective-permute-start.16 = (f32[32,512]{1,0:T(8,128)S(1)}, f32[32,512]{1,0:T(8,128)S(1)}, u32[]{:S(2)}, u32[]{:S(2)}) collective-permute-start(f32[32,512]{1,0:T(8,128)S(1)} %add_add_fusion.3), channel_id=1, source_target_pairs={{0,24},{1,7},{2,26},{3,5},{4,28},{5,3},{6,30},{7,1},{8,16},{9,15},... | collective-permute-start | bytes 196616 | tf_op jit(solution)/shard_map/ppermute | solution.py:542
  58.3 3.5 %negative.3 = f32[1,128]{1,0:T(1,128)S(1)} custom-call(bf16[128,128]{1,0:T(8,128)(2,1)S(1)} %pad_maximum_fusion.q_ref, bf16[16384,128]{1,0:T(8,128)(2,1)} %k_ref.3), custom_call_target="tpu_custom_call" | custom-call | flops 268435456 | bytes 2097152 | tf_op jit(solution)/shard_map/negative/pallas_call | solution.py:470
  61.8 0.0 collective-permute-done.14
  61.8 0.0 collective-permute-done.16
  61.9 0.3 collective-permute-start.17
  62.1 1.2 %collective-permute-done.17.other_ref = f32[32,512]{1,0:T(8,128)S(1)} collective-permute-done((f32[32,512]{1,0:T(8,128)S(1)}, f32[32,512]{1,0:T(8,128)S(1)}, u32[]{:S(2)}, u32[]{:S(2)}) %collective-permute-start.17) | collective-permute-done | bytes 65568 | tf_op jit(solution)/shard_map/ppermute | solution.py:547
  63.4 3.9 %expand.1 = (f32[49,32,2048]{2,1,0:T(8,128)S(1)}, f32[32,1280]{1,0:T(8,128)S(1)}, f32[32,1280]{1,0:T(8,128)S(1)}) custom-call(s32[1]{0:T(128)S(6)} %and.4.core_ref, f32[49,32,512]{2,1,0:T(8,128)S(1)} %get-tuple-element.69.z_ref, f32[32,512]{1,0:T(8,128)S(1)} %add_add_fusion.2.mine_ref, f32[32,512]{1,0:T(8,128)S(1)} %collective-permute-done.17.other_ref, ...), custom_call_target="tpu_custom_call" | custom-call | flops 3288334336 | bytes 16056320 | tf_op jit(solution)/shard_map/expand/pallas_call | solution.py:351
  67.3 0.2 collective-permute-start.18
  67.5 1.2 %collective-permute-done.18 = f32[32,1280]{1,0:T(8,128)S(1)} collective-permute-done((f32[32,1280]{1,0:T(8,128)S(1)}, f32[32,1280]{1,0:T(8,128)S(1)}, u32[]{:S(2)}, u32[]{:S(2)}) %collective-permute-start.18) | collective-permute-done | bytes 163872 | tf_op jit(solution)/shard_map/ppermute | solution.py:537
  68.8 0.4 collective-permute-start.19
  69.2 1.8 %collective-permute-start.20 = (bf16[32,1280]{1,0:T(8,128)(2,1)S(1)}, bf16[32,1280]{1,0:T(8,128)(2,1)S(1)}, u32[]{:S(2)}, u32[]{:S(2)}) collective-permute-start(bf16[32,1280]{1,0:T(8,128)(2,1)S(1)} %get-tuple-element.116), channel_id=1, source_target_pairs={{0,4},{1,17},{2,6},{3,19},{4,0},{5,21},{6,2},{7,23},{8,12},{9,25},... | collective-permute-start | bytes 245768 | tf_op jit(solution)/shard_map/ppermute | solution.py:542
  70.9 2.6 %collective-permute-start.21 = (bf16[32,1280]{1,0:T(8,128)(2,1)S(1)}, bf16[32,1280]{1,0:T(8,128)(2,1)S(1)}, u32[]{:S(2)}, u32[]{:S(2)}) collective-permute-start(bf16[32,1280]{1,0:T(8,128)(2,1)S(1)} %get-tuple-element.116), channel_id=1, source_target_pairs={{0,6},{1,25},{2,4},{3,27},{4,2},{5,29},{6,0},{7,31},{8,14},{9,17},... | collective-permute-start | bytes 245768 | tf_op jit(solution)/shard_map/ppermute | solution.py:542
  73.6 0.1 slice.13
  73.6 1.4 %collective-permute-start.25 = (f32[1,64]{1,0:T(1,128)S(1)}, f32[1,64]{1,0:T(1,128)S(1)}, u32[]{:S(2)}, u32[]{:S(2)}) collective-permute-start(f32[1,64]{1,0:T(1,128)S(1)} %slice.13), channel_id=1, source_target_pairs={{0,96},{32,64},{64,32},{96,0},{1,97},{33,65},{65,33},{97,1},{2,98}... | collective-permute-start | bytes 776 | tf_op jit(solution)/shard_map/ppermute | solution.py:533
  75.0 3.4 %collective-permute-done.25 = f32[1,64]{1,0:T(1,128)S(1)} collective-permute-done((f32[1,64]{1,0:T(1,128)S(1)}, f32[1,64]{1,0:T(1,128)S(1)}, u32[]{:S(2)}, u32[]{:S(2)}) %collective-permute-start.25) | collective-permute-done | bytes 288 | tf_op jit(solution)/shard_map/ppermute | solution.py:533
  78.4 0.0 collective-permute-done.19
  78.5 0.1 collective-permute-start.22
  78.6 3.4 %collective-permute-start.23 = (bf16[32,1280]{1,0:T(8,128)(2,1)S(1)}, bf16[32,1280]{1,0:T(8,128)(2,1)S(1)}, u32[]{:S(2)}, u32[]{:S(2)}) collective-permute-start(bf16[32,1280]{1,0:T(8,128)(2,1)S(1)} %get-tuple-element.114), channel_id=1, source_target_pairs={{0,16},{1,5},{2,18},{3,7},{4,20},{5,1},{6,22},{7,3},{8,24},{9,13},... | collective-permute-start | bytes 245768 | tf_op jit(solution)/shard_map/ppermute | solution.py:542
  82.0 1.3 %collective-permute-start.24 = (bf16[32,1280]{1,0:T(8,128)(2,1)S(1)}, bf16[32,1280]{1,0:T(8,128)(2,1)S(1)}, u32[]{:S(2)}, u32[]{:S(2)}) collective-permute-start(bf16[32,1280]{1,0:T(8,128)(2,1)S(1)} %get-tuple-element.114), channel_id=1, source_target_pairs={{0,24},{1,7},{2,26},{3,5},{4,28},{5,3},{6,30},{7,1},{8,16},{9,15},... | collective-permute-start | bytes 245768 | tf_op jit(solution)/shard_map/ppermute | solution.py:542
  83.3 0.1 fusion.4
  83.4 3.6 %collective-permute-done.26 = f32[1,32]{1,0:T(1,128)S(1)} collective-permute-done((f32[1,32]{1,0:T(1,128)S(1)}, f32[1,32]{1,0:T(1,128)S(1)}, u32[]{:S(2)}, u32[]{:S(2)}) %collective-permute-start.26) | collective-permute-done | bytes 160 | tf_op jit(solution)/shard_map/ppermute | solution.py:533
  87.0 0.6 collective-permute-done.24
  87.7 0.1 add_add_fusion.mine_ref
  87.7 0.1 collective-permute-start.27
  87.8 1.4 %collective-permute-done.27.other_ref = f32[32,1280]{1,0:T(8,128)S(1)} collective-permute-done((f32[32,1280]{1,0:T(8,128)S(1)}, f32[32,1280]{1,0:T(8,128)S(1)}, u32[]{:S(2)}, u32[]{:S(2)}) %collective-permute-start.27) | collective-permute-done | bytes 163872 | tf_op jit(solution)/shard_map/ppermute | solution.py:547
  89.2 0.0 copy-start.6
  89.2 4.3 %merge.1 = (bf16[32,128]{1,0:T(8,128)(2,1)}, bf16[32,32,128]{2,1,0:T(8,128)(2,1)S(1)}) custom-call(s32[1]{0:T(128)S(6)} %and.4.core_ref, f32[49,32,2048]{2,1,0:T(8,128)S(1)} %get-tuple-element.96.e_ref, bf16[49,32,2048]{2,1,0:T(8,128)(2,1)S(1)} %get-tuple-element.97.x_ref, f32[32,1280]{1,0:T(8,128)S(1)} %add_add_fusion.mine_ref, ...), custom_call_target="tpu_custom_call" | custom-call | flops 25690112 | bytes 19267584 | tf_op jit(solution)/shard_map/merge/pallas_call | solution.py:428
  93.5 11.9 %all_to_all.5 = bf16[32,32,128]{2,1,0:T(8,128)(2,1)S(1)} all-to-all(bf16[32,32,128]{2,1,0:T(8,128)(2,1)S(1)} %get-tuple-element.111), channel_id=1, replica_groups=mesh['queue'=4,'dp'=32] {'dp'}, dimensions={0} | all-to-all | bytes 524288 | tf_op jit(solution)/shard_map/all_to_all | solution.py:630
  105.4 0.8 loss.1
  (48 shorter events, 0.3 us)
Async XLA Ops:
  0.6 14.8 %copy-start.10 = (bf16[32,128]{1,0:T(8,128)(2,1)S(1)}, bf16[32,128]{1,0:T(8,128)(2,1)}, u32[]{:S(2)}) copy-start(bf16[32,128]{1,0:T(8,128)(2,1)} %param.18) | copy-start | bytes 24580
  0.6 34.0 %copy-start.7 = (bf16[9,512,512]{2,1,0:T(8,128)(2,1)S(1)}, bf16[9,512,512]{2,1,0:T(8,128)(2,1)}, u32[]{:S(2)}) copy-start(bf16[9,512,512]{2,1,0:T(8,128)(2,1)} %w_ref.4) | copy-start | bytes 14155780
  0.7 34.0 %copy-start.8 = (f32[512]{0:T(512)S(1)}, f32[512]{0:T(512)}, u32[]{:S(2)}) copy-start(f32[512]{0:T(512)} %param.21) | copy-start | bytes 6148
  0.7 34.0 %copy-start.9 = (f32[512]{0:T(512)S(1)}, f32[512]{0:T(512)}, u32[]{:S(2)}) copy-start(f32[512]{0:T(512)} %param.22) | copy-start | bytes 6148
  8.4 1.3 %collective-permute-start = (f32[32,512]{1,0:T(8,128)S(1)}, f32[32,512]{1,0:T(8,128)S(1)}, u32[]{:S(2)}, u32[]{:S(2)}) collective-permute-start(f32[32,512]{1,0:T(8,128)S(1)} %get-tuple-element.60), channel_id=1, source_target_pairs={{0,1},{1,0},{2,3},{3,2},{4,5},{5,4},{6,7},{7,6},{8,9},{9,8},{10,11... | collective-permute-start | bytes 196616 | tf_op jit(solution)/shard_map/ppermute | solution.py:537
  9.8 5.8 %collective-permute-start.1 = (f32[32,512]{1,0:T(8,128)S(1)}, f32[32,512]{1,0:T(8,128)S(1)}, u32[]{:S(2)}, u32[]{:S(2)}) collective-permute-start(f32[32,512]{1,0:T(8,128)S(1)} %add.83), channel_id=1, source_target_pairs={{0,2},{1,9},{2,0},{3,11},{4,6},{5,13},{6,4},{7,15},{8,10},{9,1},{1... | collective-permute-start | bytes 196616 | tf_op jit(solution)/shard_map/ppermute | solution.py:542
  11.9 6.5 %collective-permute-start.2 = (f32[32,512]{1,0:T(8,128)S(1)}, f32[32,512]{1,0:T(8,128)S(1)}, u32[]{:S(2)}, u32[]{:S(2)}) collective-permute-start(f32[32,512]{1,0:T(8,128)S(1)} %add.83), channel_id=1, source_target_pairs={{0,4},{1,17},{2,6},{3,19},{4,0},{5,21},{6,2},{7,23},{8,12},{9,25},... | collective-permute-start | bytes 196616 | tf_op jit(solution)/shard_map/ppermute | solution.py:542
  15.5 5.5 %collective-permute-start.3 = (f32[32,512]{1,0:T(8,128)S(1)}, f32[32,512]{1,0:T(8,128)S(1)}, u32[]{:S(2)}, u32[]{:S(2)}) collective-permute-start(f32[32,512]{1,0:T(8,128)S(1)} %add.83), channel_id=1, source_target_pairs={{0,6},{1,25},{2,4},{3,27},{4,2},{5,29},{6,0},{7,31},{8,14},{9,17},... | collective-permute-start | bytes 196616 | tf_op jit(solution)/shard_map/ppermute | solution.py:542
  21.0 4.8 %collective-permute-start.4 = (f32[32,512]{1,0:T(8,128)S(1)}, f32[32,512]{1,0:T(8,128)S(1)}, u32[]{:S(2)}, u32[]{:S(2)}) collective-permute-start(f32[32,512]{1,0:T(8,128)S(1)} %add_add_fusion.5), channel_id=1, source_target_pairs={{0,8},{1,3},{2,10},{3,1},{4,12},{5,7},{6,14},{7,5},{8,0},{9,11},{1... | collective-permute-start | bytes 196616 | tf_op jit(solution)/shard_map/ppermute | solution.py:542
  22.6 5.8 %collective-permute-start.5 = (f32[32,512]{1,0:T(8,128)S(1)}, f32[32,512]{1,0:T(8,128)S(1)}, u32[]{:S(2)}, u32[]{:S(2)}) collective-permute-start(f32[32,512]{1,0:T(8,128)S(1)} %add_add_fusion.5), channel_id=1, source_target_pairs={{0,16},{1,5},{2,18},{3,7},{4,20},{5,1},{6,22},{7,3},{8,24},{9,13},... | collective-permute-start | bytes 196616 | tf_op jit(solution)/shard_map/ppermute | solution.py:542
  25.3 5.5 %collective-permute-start.6 = (f32[32,512]{1,0:T(8,128)S(1)}, f32[32,512]{1,0:T(8,128)S(1)}, u32[]{:S(2)}, u32[]{:S(2)}) collective-permute-start(f32[32,512]{1,0:T(8,128)S(1)} %add_add_fusion.5), channel_id=1, source_target_pairs={{0,24},{1,7},{2,26},{3,5},{4,28},{5,3},{6,30},{7,1},{8,16},{9,15},... | collective-permute-start | bytes 196616 | tf_op jit(solution)/shard_map/ppermute | solution.py:542
  30.8 3.8 %collective-permute-start.7 = (f32[32,512]{1,0:T(8,128)S(1)}, f32[32,512]{1,0:T(8,128)S(1)}, u32[]{:S(2)}, u32[]{:S(2)}) collective-permute-start(f32[32,512]{1,0:T(8,128)S(1)} %add_add_fusion.4.mine_ref), channel_id=1, source_target_pairs={{0,1},{1,0},{2,3},{3,2},{4,5},{5,4},{6,7},{7,6},{8,9},{9,8},{10,11... | collective-permute-start | bytes 196616 | tf_op jit(solution)/shard_map/ppermute | solution.py:547
  30.9 3.7 %collective-permute-start.12 = (bf16[32,128]{1,0:T(8,128)(2,1)S(1)}, bf16[32,128]{1,0:T(8,128)(2,1)S(1)}, u32[]{:S(2)}, u32[]{:S(2)}) collective-permute-start(bf16[32,128]{1,0:T(8,128)(2,1)S(1)} %fusion.1.u_ref), channel_id=1, source_target_pairs={{0,32},{32,0},{64,96},{96,64},{1,33},{33,1},{65,97},{97,65},{2,34}... | collective-permute-start | bytes 24584 | tf_op jit(solution)/shard_map/ppermute | solution.py:533
  34.6 14.9 %copy-start = (bf16[512,2048]{1,0:T(8,128)(2,1)S(1)}, bf16[512,2048]{1,0:T(8,128)(2,1)}, u32[]{:S(2)}) copy-start(bf16[512,2048]{1,0:T(8,128)(2,1)} %w_ref.7) | copy-start | bytes 6291460
  34.7 14.9 %copy-start.4 = (f32[512]{0:T(512)S(1)}, f32[512]{0:T(512)}, u32[]{:S(2)}) copy-start(f32[512]{0:T(512)} %param.24) | copy-start | bytes 6148
  34.7 14.9 %copy-start.5 = (f32[512]{0:T(512)S(1)}, f32[512]{0:T(512)}, u32[]{:S(2)}) copy-start(f32[512]{0:T(512)} %param.25) | copy-start | bytes 6148
  42.7 3.2 %collective-permute-start.8 = (f32[32,512]{1,0:T(8,128)S(1)}, f32[32,512]{1,0:T(8,128)S(1)}, u32[]{:S(2)}, u32[]{:S(2)}) collective-permute-start(f32[32,512]{1,0:T(8,128)S(1)} %get-tuple-element.71), channel_id=1, source_target_pairs={{0,1},{1,0},{2,3},{3,2},{4,5},{5,4},{6,7},{7,6},{8,9},{9,8},{10,11... | collective-permute-start | bytes 196616 | tf_op jit(solution)/shard_map/ppermute | solution.py:537
  42.8 6.7 %collective-permute-start.13 = (bf16[64,128]{1,0:T(8,128)(2,1)S(1)}, bf16[64,128]{1,0:T(8,128)(2,1)S(1)}, u32[]{:S(2)}, u32[]{:S(2)}) collective-permute-start(bf16[64,128]{1,0:T(8,128)(2,1)S(1)} %pad_maximum_fusion.1), channel_id=1, source_target_pairs={{0,96},{32,64},{64,32},{96,0},{1,97},{33,65},{65,33},{97,1},{2,98}... | collective-permute-start | bytes 49160 | tf_op jit(solution)/shard_map/ppermute | solution.py:533
  45.9 7.5 %collective-permute-start.10 = (f32[32,512]{1,0:T(8,128)S(1)}, f32[32,512]{1,0:T(8,128)S(1)}, u32[]{:S(2)}, u32[]{:S(2)}) collective-permute-start(f32[32,512]{1,0:T(8,128)S(1)} %add.90), channel_id=1, source_target_pairs={{0,4},{1,17},{2,6},{3,19},{4,0},{5,21},{6,2},{7,23},{8,12},{9,25},... | collective-permute-start | bytes 196616 | tf_op jit(solution)/shard_map/ppermute | solution.py:542
  46.3 7.1 %collective-permute-start.11 = (f32[32,512]{1,0:T(8,128)S(1)}, f32[32,512]{1,0:T(8,128)S(1)}, u32[]{:S(2)}, u32[]{:S(2)}) collective-permute-start(f32[32,512]{1,0:T(8,128)S(1)} %add.90), channel_id=1, source_target_pairs={{0,6},{1,25},{2,4},{3,27},{4,2},{5,29},{6,0},{7,31},{8,14},{9,17},... | collective-permute-start | bytes 196616 | tf_op jit(solution)/shard_map/ppermute | solution.py:542
  47.3 6.2 %collective-permute-start.9 = (f32[32,512]{1,0:T(8,128)S(1)}, f32[32,512]{1,0:T(8,128)S(1)}, u32[]{:S(2)}, u32[]{:S(2)}) collective-permute-start(f32[32,512]{1,0:T(8,128)S(1)} %add.90), channel_id=1, source_target_pairs={{0,2},{1,9},{2,0},{3,11},{4,6},{5,13},{6,4},{7,15},{8,10},{9,1},{1... | collective-permute-start | bytes 196616 | tf_op jit(solution)/shard_map/ppermute | solution.py:542
  53.5 8.3 %collective-permute-start.14 = (f32[32,512]{1,0:T(8,128)S(1)}, f32[32,512]{1,0:T(8,128)S(1)}, u32[]{:S(2)}, u32[]{:S(2)}) collective-permute-start(f32[32,512]{1,0:T(8,128)S(1)} %add_add_fusion.3), channel_id=1, source_target_pairs={{0,8},{1,3},{2,10},{3,1},{4,12},{5,7},{6,14},{7,5},{8,0},{9,11},{1... | collective-permute-start | bytes 196616 | tf_op jit(solution)/shard_map/ppermute | solution.py:542
  53.6 8.2 %collective-permute-start.15 = (f32[32,512]{1,0:T(8,128)S(1)}, f32[32,512]{1,0:T(8,128)S(1)}, u32[]{:S(2)}, u32[]{:S(2)}) collective-permute-start(f32[32,512]{1,0:T(8,128)S(1)} %add_add_fusion.3), channel_id=1, source_target_pairs={{0,16},{1,5},{2,18},{3,7},{4,20},{5,1},{6,22},{7,3},{8,24},{9,13},... | collective-permute-start | bytes 196616 | tf_op jit(solution)/shard_map/ppermute | solution.py:542
  55.5 6.3 %collective-permute-start.16 = (f32[32,512]{1,0:T(8,128)S(1)}, f32[32,512]{1,0:T(8,128)S(1)}, u32[]{:S(2)}, u32[]{:S(2)}) collective-permute-start(f32[32,512]{1,0:T(8,128)S(1)} %add_add_fusion.3), channel_id=1, source_target_pairs={{0,24},{1,7},{2,26},{3,5},{4,28},{5,3},{6,30},{7,1},{8,16},{9,15},... | collective-permute-start | bytes 196616 | tf_op jit(solution)/shard_map/ppermute | solution.py:542
  61.9 1.5 %collective-permute-start.17 = (f32[32,512]{1,0:T(8,128)S(1)}, f32[32,512]{1,0:T(8,128)S(1)}, u32[]{:S(2)}, u32[]{:S(2)}) collective-permute-start(f32[32,512]{1,0:T(8,128)S(1)} %add_add_fusion.2.mine_ref), channel_id=1, source_target_pairs={{0,1},{1,0},{2,3},{3,2},{4,5},{5,4},{6,7},{7,6},{8,9},{9,8},{10,11... | collective-permute-start | bytes 196616 | tf_op jit(solution)/shard_map/ppermute | solution.py:547
  63.4 25.8 %copy-start.1 = (bf16[2048,128]{1,0:T(8,128)(2,1)S(1)}, bf16[2048,128]{1,0:T(8,128)(2,1)}, u32[]{:S(2)}) copy-start(bf16[2048,128]{1,0:T(8,128)(2,1)} %proj_ref.1) | copy-start | bytes 1572868
  63.4 25.8 %copy-start.2 = (f32[2048]{0:T(1024)S(1)}, f32[2048]{0:T(1024)}, u32[]{:S(2)}) copy-start(f32[2048]{0:T(1024)} %param.27) | copy-start | bytes 24580
  63.4 25.8 %copy-start.3 = (f32[2048]{0:T(1024)S(1)}, f32[2048]{0:T(1024)}, u32[]{:S(2)}) copy-start(f32[2048]{0:T(1024)} %param.28) | copy-start | bytes 24580
  67.3 1.5 %collective-permute-start.18 = (f32[32,1280]{1,0:T(8,128)S(1)}, f32[32,1280]{1,0:T(8,128)S(1)}, u32[]{:S(2)}, u32[]{:S(2)}) collective-permute-start(f32[32,1280]{1,0:T(8,128)S(1)} %get-tuple-element.99), channel_id=1, source_target_pairs={{0,1},{1,0},{2,3},{3,2},{4,5},{5,4},{6,7},{7,6},{8,9},{9,8},{10,11... | collective-permute-start | bytes 491528 | tf_op jit(solution)/shard_map/ppermute | solution.py:537
  68.8 9.6 %collective-permute-start.19 = (bf16[32,1280]{1,0:T(8,128)(2,1)S(1)}, bf16[32,1280]{1,0:T(8,128)(2,1)S(1)}, u32[]{:S(2)}, u32[]{:S(2)}) collective-permute-start(bf16[32,1280]{1,0:T(8,128)(2,1)S(1)} %get-tuple-element.116), channel_id=1, source_target_pairs={{0,2},{1,9},{2,0},{3,11},{4,6},{5,13},{6,4},{7,15},{8,10},{9,1},{1... | collective-permute-start | bytes 245768 | tf_op jit(solution)/shard_map/ppermute | solution.py:542
  69.2 9.3 %collective-permute-start.20 = (bf16[32,1280]{1,0:T(8,128)(2,1)S(1)}, bf16[32,1280]{1,0:T(8,128)(2,1)S(1)}, u32[]{:S(2)}, u32[]{:S(2)}) collective-permute-start(bf16[32,1280]{1,0:T(8,128)(2,1)S(1)} %get-tuple-element.116), channel_id=1, source_target_pairs={{0,4},{1,17},{2,6},{3,19},{4,0},{5,21},{6,2},{7,23},{8,12},{9,25},... | collective-permute-start | bytes 245768 | tf_op jit(solution)/shard_map/ppermute | solution.py:542
  70.9 7.5 %collective-permute-start.21 = (bf16[32,1280]{1,0:T(8,128)(2,1)S(1)}, bf16[32,1280]{1,0:T(8,128)(2,1)S(1)}, u32[]{:S(2)}, u32[]{:S(2)}) collective-permute-start(bf16[32,1280]{1,0:T(8,128)(2,1)S(1)} %get-tuple-element.116), channel_id=1, source_target_pairs={{0,6},{1,25},{2,4},{3,27},{4,2},{5,29},{6,0},{7,31},{8,14},{9,17},... | collective-permute-start | bytes 245768 | tf_op jit(solution)/shard_map/ppermute | solution.py:542
  73.6 4.8 %collective-permute-start.25 = (f32[1,64]{1,0:T(1,128)S(1)}, f32[1,64]{1,0:T(1,128)S(1)}, u32[]{:S(2)}, u32[]{:S(2)}) collective-permute-start(f32[1,64]{1,0:T(1,128)S(1)} %slice.13), channel_id=1, source_target_pairs={{0,96},{32,64},{64,32},{96,0},{1,97},{33,65},{65,33},{97,1},{2,98}... | collective-permute-start | bytes 776 | tf_op jit(solution)/shard_map/ppermute | solution.py:533
  78.5 8.4 %collective-permute-start.22 = (bf16[32,1280]{1,0:T(8,128)(2,1)S(1)}, bf16[32,1280]{1,0:T(8,128)(2,1)S(1)}, u32[]{:S(2)}, u32[]{:S(2)}) collective-permute-start(bf16[32,1280]{1,0:T(8,128)(2,1)S(1)} %get-tuple-element.114), channel_id=1, source_target_pairs={{0,8},{1,3},{2,10},{3,1},{4,12},{5,7},{6,14},{7,5},{8,0},{9,11},{1... | collective-permute-start | bytes 245768 | tf_op jit(solution)/shard_map/ppermute | solution.py:542
  78.6 8.4 %collective-permute-start.23 = (bf16[32,1280]{1,0:T(8,128)(2,1)S(1)}, bf16[32,1280]{1,0:T(8,128)(2,1)S(1)}, u32[]{:S(2)}, u32[]{:S(2)}) collective-permute-start(bf16[32,1280]{1,0:T(8,128)(2,1)S(1)} %get-tuple-element.114), channel_id=1, source_target_pairs={{0,16},{1,5},{2,18},{3,7},{4,20},{5,1},{6,22},{7,3},{8,24},{9,13},... | collective-permute-start | bytes 245768 | tf_op jit(solution)/shard_map/ppermute | solution.py:542
  82.0 5.7 %collective-permute-start.24 = (bf16[32,1280]{1,0:T(8,128)(2,1)S(1)}, bf16[32,1280]{1,0:T(8,128)(2,1)S(1)}, u32[]{:S(2)}, u32[]{:S(2)}) collective-permute-start(bf16[32,1280]{1,0:T(8,128)(2,1)S(1)} %get-tuple-element.114), channel_id=1, source_target_pairs={{0,24},{1,7},{2,26},{3,5},{4,28},{5,3},{6,30},{7,1},{8,16},{9,15},... | collective-permute-start | bytes 245768 | tf_op jit(solution)/shard_map/ppermute | solution.py:542
  83.4 3.6 %collective-permute-start.26 = (f32[1,32]{1,0:T(1,128)S(1)}, f32[1,32]{1,0:T(1,128)S(1)}, u32[]{:S(2)}, u32[]{:S(2)}) collective-permute-start(f32[1,32]{1,0:T(1,128)S(1)} %get-tuple-element.118), channel_id=1, source_target_pairs={{0,32},{32,0},{64,96},{96,64},{1,33},{33,1},{65,97},{97,65},{2,34}... | collective-permute-start | bytes 392 | tf_op jit(solution)/shard_map/ppermute | solution.py:533
  87.7 1.5 %collective-permute-start.27 = (f32[32,1280]{1,0:T(8,128)S(1)}, f32[32,1280]{1,0:T(8,128)S(1)}, u32[]{:S(2)}, u32[]{:S(2)}) collective-permute-start(f32[32,1280]{1,0:T(8,128)S(1)} %add_add_fusion.mine_ref), channel_id=1, source_target_pairs={{0,1},{1,0},{2,3},{3,2},{4,5},{5,4},{6,7},{7,6},{8,9},{9,8},{10,11... | collective-permute-start | bytes 491528 | tf_op jit(solution)/shard_map/ppermute | solution.py:547
  89.2 16.2 %copy-start.6 = (s32[32]{0:T(128)S(1)}, s32[32]{0:T(128)}, u32[]{:S(2)}) copy-start(s32[32]{0:T(128)} %param.17) | copy-start | bytes 388
where the time goes:
time: 108 us; the launch traced here: 106 us
  starting transfers between devices  35.3 us (33%)
  Pallas kernels  32.2 us (30%)
  waiting for transfers between devices  25.2 us (23%)
  blocking collectives  11.9 us (11%)
    ppermute x18, starting transfers between devices, reduce_sets(): parts.append(lax.ppermute(sent, 'dp', ring_swap(k, turn == 1)).astype(F32))  28.4 us
    all_to_all x1, blocking collectives, on_device(): lax.all_to_all(copies, 'dp', split_axis=0, concat_axis=0, tiled=True)  11.9 us
    ppermute x18, waiting for transfers between devices, reduce_sets(): parts.append(lax.ppermute(sent, 'dp', ring_swap(k, turn == 1)).astype(F32))  11 us
    ppermute x4, waiting for transfers between devices, queue_swap(): return lax.ppermute(values, 'queue', [(i, i ^ k) for i in range(RING)])  9.07 us
    pallas_call x1, Pallas kernels, conv_stage(): pl.pallas_call(functools.partial(conv_kernel, rows), name='conv', grid=(S...  8.03 us
    pallas_call x1, Pallas kernels, reduce_stage(): pl.pallas_call(reduce_kernel, name='reduce', in_specs=[SMEM, hbm, hbm, hb...  7.75 us
    pallas_call x2, Pallas kernels, negative_stage(): pl.pallas_call(functools.partial(negative_kernel, math.log2(math.e) / TEM...  7 us
    ppermute x4, starting transfers between devices, queue_swap(): return lax.ppermute(values, 'queue', [(i, i ^ k) for i in range(RING)])  6.05 us
  transfers between devices with their start and end apart: 28, of which 12 were waited for; matrix products, arithmetic and copies ran while one was open for 0% of the time, Pallas kernels for 7%

commit v1 on v0

--- a/solution.py
+++ b/solution.py
@@ -86,6 +86,8 @@
 ):
     _, count, channels = x_ref.shape
     mid = w_ref.shape[1]
+    shuffle_copy = pltpu.make_async_copy(shuffle_hbm, shuffle_ref, sems.at[len(CHUNKS) + 1])
+    shuffle_copy.start()
     weight_copy = pltpu.make_async_copy(w_hbm, w_ref, sems.at[0])
     weight_copy.start()
     copies = []
@@ -93,8 +95,6 @@
         part = pl.ds(first, size)
         copies.append(pltpu.make_async_copy(x_hbm.at[part], x_ref.at[part], sems.at[n + 1]))
         copies[-1].start()
-    shuffle_copy = pltpu.make_async_copy(shuffle_hbm, shuffle_ref, sems.at[len(CHUNKS) + 1])
-    shuffle_copy.start()
     shuffle_copy.wait()
     by_set, by_image = set_onehots(me_ref[0], shuffle_ref[...], count)
     by_set_ref[...] = by_set
@@ -480,7 +480,7 @@
             bytes_accessed=2 * total * feat,
             transcendentals=total * count,
         ),
-    )(queries, pltpu.with_memory_space_constraint(keys, pltpu.HBM))
+    )(queries, keys)
 
 
 def loss_kernel(table_ref, u_ref, pos_ref, neg_ref, loss_ref):
@@ -570,48 +570,39 @@
     core = jnp.bitwise_and(me, 1)
     rows = count * places
     x = jnp.transpose(features, (1, 0, 2))
-    units = unit_rows(queries)
     gain_two, shift_two = gain_two[None], shift_two[None]
-
-    def gather_one(own):
-        return None, (own, queue_swap(own, 1))
-
-    def gather_two(state):
-        pair = jnp.concatenate(state[1], 0)
-        return None, (pair, queue_swap(pair, 3))
 
     def negative_one(state):
         here, gain, shift = state
+        here = unit_rows(here)
         centers = center_stage(gain, shift, w_expand)
         return (here, negative_stage(here, queue_keys, 0, 2), centers), None
 
     def negative_two(state):
         here, sums, centers = state[0]
-        sums = sums + negative_stage(here, queue_keys, 1, 2)
-        return (sums, centers), queue_swap(sums[:, 2 * count :], 3)
-
-    def return_two(state):
-        sums = state[0] + state[1]
-        return None, (sums[:, :count], queue_swap(sums[:, count:], 1))
-
-    def return_done(state):
-        return sum(state[1]), None
-
+        return (here, sums + negative_stage(here, queue_keys, 1, 2), centers), None
+
+    def nothing(state):
+        return None, None
+
+    first = queue_swap(queries, 1)
     y, keep, send, by_set, by_image, x = reduce_stage(me, x, reduce_weight, shuffle)
-    mine, other, (_, asked) = reduce_sets(keep, send, (gather_one, gather_two), units, F32)
-    asked = jnp.concatenate(asked, 0)
+    pair = jnp.concatenate([queries, first], 0)
+    mine, other, _ = reduce_sets(keep, send, (nothing, nothing), None, F32)
+    asked = jnp.concatenate([pair, queue_swap(pair, 3)], 0)
     z, keep, send = conv_stage(
         rows, core, y, mine, other, by_set, by_image, gain_one[None], shift_one[None], w_spatial
     )
-    mine, other, ((sums, centers), told) = reduce_sets(
+    mine, other, ((units, sums, centers), _) = reduce_sets(
         keep, send, (negative_one, negative_two), (asked, gain_two, shift_two), F32
     )
+    told = queue_swap(sums[:, 2 * count :], 3)
     e, keep, send = expand_stage(
         rows, core, z, mine, other, by_set, by_image, gain_two, shift_two, *centers, w_expand
     )
-    mine, other, (negatives, _) = reduce_sets(
-        keep, send, (return_two, return_done), (sums[:, : 2 * count], told), BF16
-    )
+    mine, other, _ = reduce_sets(keep, send, (nothing, nothing), None, BF16)
+    sums = sums[:, : 2 * count] + told
+    told = queue_swap(sums[:, count:], 1)
     key_rows, copies = merge_stage(
         rows,
         core,
@@ -629,7 +620,8 @@
     )
     table = lax.all_to_all(copies, "dp", split_axis=0, concat_axis=0, tiled=True)
     table = table.reshape(peers * count, -1)
-    loss_vals = loss_stage(table, units, positive.reshape(1, count), negatives)
+    negatives = sums[:, :count] + told
+    loss_vals = loss_stage(table, units[:count], positive.reshape(1, count), negatives)
     return (loss_vals.reshape(count), key_rows)
 
 

time: 108 us -> 98.8 us (0.915)
  blocking collectives: 11.9 us -> 0 us
  waiting for transfers between devices: 25.2 us -> 30.5 us
  Pallas kernels: 32.2 us -> 27.1 us
  starting transfers between devices: 35.3 us -> 38.1 us
    all_to_all x1 -> x0, blocking collectives: 11.9 us -> none  [on_device(): lax.all_to_all(copies, 'dp', split_axis=0, concat_axis=0, tiled=True)]
    ppermute x18, waiting for transfers between devices: 11 us -> 16.8 us  [reduce_sets(): parts.append(lax.ppermute(sent, 'dp', ring_swap(k, turn == 1)).astype(F32))]
    ppermute x4, waiting for transfers between devices: 9.07 us -> 3.43 us  [queue_swap(): return lax.ppermute(values, 'queue', [(i, i ^ k) for i in range(RING)])]
    all_to_all x0 -> x1, waiting for transfers between devices: none -> 5.22 us  [on_device(): lax.all_to_all(copies, 'dp', split_axis=0, concat_axis=0, tiled=True)]
    all_to_all x0 -> x1, starting transfers between devices: none -> 5.09 us  [on_device(): lax.all_to_all(copies, 'dp', split_axis=0, concat_axis=0, tiled=True)]
    pallas_call x2, Pallas kernels: 7 us -> 3.66 us  [negative_stage(): pl.pallas_call(functools.partial(negative_kernel, math.log2(math.e) / TEM...]
    ppermute x18, starting transfers between devices: 28.4 us -> 26 us  [reduce_sets(): parts.append(lax.ppermute(sent, 'dp', ring_swap(k, turn == 1)).astype(F32))]
    pallas_call x1, Pallas kernels: 7.75 us -> 6 us  [reduce_stage(): pl.pallas_call(reduce_kernel, name='reduce', in_specs=[SMEM, hbm, hbm, hb...]
  transfers between devices with their start and end apart: 28 -> 29, of which waited for: 12 -> 16; matrix products, arithmetic and copies ran while one was open for 0% -> 0% of each run, Pallas kernels for 7% -> 17%
where the time goes in v1:
time: 98.8 us; the launch traced here: 97.4 us
  starting transfers between devices  38.1 us (39%)
  waiting for transfers between devices  30.5 us (31%)
  Pallas kernels  27.1 us (27%)
  between operations  1.01 us (1%)
    ppermute x18, starting transfers between devices, reduce_sets(): parts.append(lax.ppermute(sent, 'dp', ring_swap(k, turn == 1)).astype(F32))  26 us
    ppermute x18, waiting for transfers between devices, reduce_sets(): parts.append(lax.ppermute(sent, 'dp', ring_swap(k, turn == 1)).astype(F32))  16.8 us
    pallas_call x1, Pallas kernels, conv_stage(): pl.pallas_call(functools.partial(conv_kernel, rows), name='conv', grid=(S...  8.1 us
    pallas_call x1, Pallas kernels, reduce_stage(): pl.pallas_call(reduce_kernel, name='reduce', in_specs=[SMEM, hbm, hbm, hb...  6 us
    ppermute x4, starting transfers between devices, queue_swap(): return lax.ppermute(values, 'queue', [(i, i ^ k) for i in range(RING)])  5.99 us
    all_to_all x1, waiting for transfers between devices, on_device(): lax.all_to_all(copies, 'dp', split_axis=0, concat_axis=0, tiled=True)  5.22 us
    all_to_all x1, starting transfers between devices, on_device(): lax.all_to_all(copies, 'dp', split_axis=0, concat_axis=0, tiled=True)  5.09 us
    pallas_call x1, Pallas kernels, merge_stage(): pl.pallas_call(functools.partial(merge_kernel, rows), name='merge', in_sp...  4.23 us
  transfers between devices with their start and end apart: 29, of which 16 were waited for; matrix products, arithmetic and copies ran while one was open for 0% of the time, Pallas kernels for 17%

profile of v1, /device:TPU:0, one launch (start us, length us, event | category | flops | bytes accessed | tf_op | source)
XLA Modules:
  0.0 97.4 jit_solution(251268376927945256)
XLA Ops:
  0.7 6.0 %reduce.1 = (f32[49,32,512]{2,1,0:T(8,128)S(1)}, f32[32,512]{1,0:T(8,128)S(1)}, f32[32,512]{1,0:T(8,128)S(1)}, bf16[32,96]{1,0:T(8,128)(2,1)S(1)}, bf16[32,96]{1...) custom-call(s32[1]{0:T(128)} %bitcast.me_ref, bf16[49,32,2048]{2,1,0:T(8,128)(2,1)} %bitcast.22, ...), custom_call_target="tpu_custom_call" | custom-call | flops 3288334336 | bytes 9633792 | tf_op jit(solution)/shard_map/reduce/pallas_call | solution.py:123
  6.7 0.1 collective-permute-start
  6.8 1.2 %collective-permute-done = f32[32,512]{1,0:T(8,128)S(1)} collective-permute-done((f32[32,512]{1,0:T(8,128)S(1)}, f32[32,512]{1,0:T(8,128)S(1)}, u32[]{:S(2)}, u32[]{:S(2)}) %collective-permute-start) | collective-permute-done | bytes 65568 | tf_op jit(solution)/shard_map/ppermute | solution.py:537
  8.0 4.2 %collective-permute-start.3 = (f32[32,512]{1,0:T(8,128)S(1)}, f32[32,512]{1,0:T(8,128)S(1)}, u32[]{:S(2)}, u32[]{:S(2)}) collective-permute-start(f32[32,512]{1,0:T(8,128)S(1)} %add.83), channel_id=1, source_target_pairs={{0,6},{1,25},{2,4},{3,27},{4,2},{5,29},{6,0},{7,31},{8,14},{9,17},... | collective-permute-start | bytes 196616 | tf_op jit(solution)/shard_map/ppermute | solution.py:542
  12.3 0.0 collective-permute-start.2
  12.3 0.9 collective-permute-start.1
  13.2 1.6 %collective-permute-done.3 = f32[32,512]{1,0:T(8,128)S(1)} collective-permute-done((f32[32,512]{1,0:T(8,128)S(1)}, f32[32,512]{1,0:T(8,128)S(1)}, u32[]{:S(2)}, u32[]{:S(2)}) %collective-permute-start.3) | collective-permute-done | bytes 65568 | tf_op jit(solution)/shard_map/ppermute | solution.py:542
  14.8 3.3 %collective-permute-done.2 = f32[32,512]{1,0:T(8,128)S(1)} collective-permute-done((f32[32,512]{1,0:T(8,128)S(1)}, f32[32,512]{1,0:T(8,128)S(1)}, u32[]{:S(2)}, u32[]{:S(2)}) %collective-permute-start.2) | collective-permute-done | bytes 65568 | tf_op jit(solution)/shard_map/ppermute | solution.py:542
  18.0 0.0 collective-permute-done.1
  18.1 2.8 %collective-permute-start.6 = (f32[32,512]{1,0:T(8,128)S(1)}, f32[32,512]{1,0:T(8,128)S(1)}, u32[]{:S(2)}, u32[]{:S(2)}) collective-permute-start(f32[32,512]{1,0:T(8,128)S(1)} %add_add_fusion.5), channel_id=1, source_target_pairs={{0,24},{1,7},{2,26},{3,5},{4,28},{5,3},{6,30},{7,1},{8,16},{9,15},... | collective-permute-start | bytes 196616 | tf_op jit(solution)/shard_map/ppermute | solution.py:542
  20.9 0.8 collective-permute-start.5
  21.7 0.5 collective-permute-start.4
  22.2 1.6 %collective-permute-start.12 = (bf16[32,128]{1,0:T(8,128)(2,1)S(1)}, bf16[32,128]{1,0:T(8,128)(2,1)S(1)}, u32[]{:S(2)}, u32[]{:S(2)}) collective-permute-start(bf16[32,128]{1,0:T(8,128)(2,1)S(1)} %copy-done.11), channel_id=1, source_target_pairs={{0,32},{32,0},{64,96},{96,64},{1,33},{33,1},{65,97},{97,65},{2,34}... | collective-permute-start | bytes 24584 | tf_op jit(solution)/shard_map/ppermute | solution.py:533
  23.8 2.9 %collective-permute-done.5 = f32[32,512]{1,0:T(8,128)S(1)} collective-permute-done((f32[32,512]{1,0:T(8,128)S(1)}, f32[32,512]{1,0:T(8,128)S(1)}, u32[]{:S(2)}, u32[]{:S(2)}) %collective-permute-start.5) | collective-permute-done | bytes 65568 | tf_op jit(solution)/shard_map/ppermute | solution.py:542
  26.7 0.1 collective-permute-start.7
  26.8 3.1 %collective-permute-start.13 = (bf16[64,128]{1,0:T(8,128)(2,1)S(1)}, bf16[64,128]{1,0:T(8,128)(2,1)S(1)}, u32[]{:S(2)}, u32[]{:S(2)}) collective-permute-start(bf16[64,128]{1,0:T(8,128)(2,1)S(1)} %pad_maximum_fusion.1), channel_id=1, source_target_pairs={{0,96},{32,64},{64,32},{96,0},{1,97},{33,65},{65,33},{97,1},{2,98}... | collective-permute-start | bytes 49160 | tf_op jit(solution)/shard_map/ppermute | solution.py:533
  29.9 0.0 copy-start.1
  29.9 0.0 copy-start.5
  30.0 0.0 copy-start.6
  30.0 0.0 copy-start
  30.0 8.1 %conv.1 = (f32[49,32,512]{2,1,0:T(8,128)S(1)}, f32[32,512]{1,0:T(8,128)S(1)}, f32[32,512]{1,0:T(8,128)S(1)}) custom-call(s32[1]{0:T(128)S(6)} %and.4.core_ref, f32[49,32,512]{2,1,0:T(8,128)S(1)} %get-tuple-element.51.y_ref, f32[32,512]{1,0:T(8,128)S(1)} %add_add_fusion.4.mine_ref, f32[32,512]{1,0:T(8,128)S(1)} %collective-permute-done.7.other_ref, ...), custom_call_target="tpu_custom_call" | custom-call | flops 6056574976 | bytes 11141120 | tf_op jit(solution)/shard_map/conv/pallas_call | solution.py:239
  38.1 0.2 collective-permute-start.8
  38.3 1.1 %collective-permute-done.8 = f32[32,512]{1,0:T(8,128)S(1)} collective-permute-done((f32[32,512]{1,0:T(8,128)S(1)}, f32[32,512]{1,0:T(8,128)S(1)}, u32[]{:S(2)}, u32[]{:S(2)}) %collective-permute-start.8) | collective-permute-done | bytes 65568 | tf_op jit(solution)/shard_map/ppermute | solution.py:537
  39.4 1.3 %collective-permute-start.11 = (f32[32,512]{1,0:T(8,128)S(1)}, f32[32,512]{1,0:T(8,128)S(1)}, u32[]{:S(2)}, u32[]{:S(2)}) collective-permute-start(f32[32,512]{1,0:T(8,128)S(1)} %add.90), channel_id=1, source_target_pairs={{0,6},{1,25},{2,4},{3,27},{4,2},{5,29},{6,0},{7,31},{8,14},{9,17},... | collective-permute-start | bytes 196616 | tf_op jit(solution)/shard_map/ppermute | solution.py:542
  40.8 0.9 collective-permute-start.10
  41.6 2.0 %collective-permute-start.9 = (f32[32,512]{1,0:T(8,128)S(1)}, f32[32,512]{1,0:T(8,128)S(1)}, u32[]{:S(2)}, u32[]{:S(2)}) collective-permute-start(f32[32,512]{1,0:T(8,128)S(1)} %add.90), channel_id=1, source_target_pairs={{0,2},{1,9},{2,0},{3,11},{4,6},{5,13},{6,4},{7,15},{8,10},{9,1},{1... | collective-permute-start | bytes 196616 | tf_op jit(solution)/shard_map/ppermute | solution.py:542
  43.6 0.1 fusion
  43.7 0.1 fusion.1.q_ref
  43.9 0.4 center.1
  44.2 1.8 %negative.2 = f32[1,128]{1,0:T(1,128)S(1)} custom-call(bf16[128,128]{1,0:T(8,128)(2,1)S(1)} %fusion.1.q_ref, bf16[16384,128]{1,0:T(8,128)(2,1)S(1)} %copy-done), custom_call_target="tpu_custom_call" | custom-call | flops 268435456 | bytes 2097152 | tf_op jit(solution)/shard_map/negative/pallas_call | solution.py:470
  46.1 0.4 collective-permute-done.10
  46.5 0.0 collective-permute-done.9
  46.6 1.8 %collective-permute-start.16 = (f32[32,512]{1,0:T(8,128)S(1)}, f32[32,512]{1,0:T(8,128)S(1)}, u32[]{:S(2)}, u32[]{:S(2)}) collective-permute-start(f32[32,512]{1,0:T(8,128)S(1)} %add_add_fusion.3), channel_id=1, source_target_pairs={{0,24},{1,7},{2,26},{3,5},{4,28},{5,3},{6,30},{7,1},{8,16},{9,15},... | collective-permute-start | bytes 196616 | tf_op jit(solution)/shard_map/ppermute | solution.py:542
  48.4 0.8 collective-permute-start.15
  49.2 1.5 %collective-permute-start.14 = (f32[32,512]{1,0:T(8,128)S(1)}, f32[32,512]{1,0:T(8,128)S(1)}, u32[]{:S(2)}, u32[]{:S(2)}) collective-permute-start(f32[32,512]{1,0:T(8,128)S(1)} %add_add_fusion.3), channel_id=1, source_target_pairs={{0,8},{1,3},{2,10},{3,1},{4,12},{5,7},{6,14},{7,5},{8,0},{9,11},{1... | collective-permute-start | bytes 196616 | tf_op jit(solution)/shard_map/ppermute | solution.py:542
  50.8 1.8 %negative.3 = f32[1,128]{1,0:T(1,128)S(1)} custom-call(bf16[128,128]{1,0:T(8,128)(2,1)S(1)} %fusion.1.q_ref, bf16[16384,128]{1,0:T(8,128)(2,1)S(1)} %copy-done), custom_call_target="tpu_custom_call" | custom-call | flops 268435456 | bytes 2097152 | tf_op jit(solution)/shard_map/negative/pallas_call | solution.py:470
  52.6 1.6 %collective-permute-done.15 = f32[32,512]{1,0:T(8,128)S(1)} collective-permute-done((f32[32,512]{1,0:T(8,128)S(1)}, f32[32,512]{1,0:T(8,128)S(1)}, u32[]{:S(2)}, u32[]{:S(2)}) %collective-permute-start.15) | collective-permute-done | bytes 65568 | tf_op jit(solution)/shard_map/ppermute | solution.py:542
  54.2 0.3 collective-permute-start.17
  54.5 1.2 %collective-permute-done.17.other_ref = f32[32,512]{1,0:T(8,128)S(1)} collective-permute-done((f32[32,512]{1,0:T(8,128)S(1)}, f32[32,512]{1,0:T(8,128)S(1)}, u32[]{:S(2)}, u32[]{:S(2)}) %collective-permute-start.17) | collective-permute-done | bytes 65568 | tf_op jit(solution)/shard_map/ppermute | solution.py:547
  55.7 3.9 %expand.1 = (f32[49,32,2048]{2,1,0:T(8,128)S(1)}, f32[32,1280]{1,0:T(8,128)S(1)}, f32[32,1280]{1,0:T(8,128)S(1)}) custom-call(s32[1]{0:T(128)S(6)} %and.4.core_ref, f32[49,32,512]{2,1,0:T(8,128)S(1)} %get-tuple-element.62.z_ref, f32[32,512]{1,0:T(8,128)S(1)} %add_add_fusion.2.mine_ref, f32[32,512]{1,0:T(8,128)S(1)} %collective-permute-done.17.other_ref, ...), custom_call_target="tpu_custom_call" | custom-call | flops 3288334336 | bytes 16056320 | tf_op jit(solution)/shard_map/expand/pallas_call | solution.py:351
  59.6 0.2 collective-permute-start.18
  59.9 1.2 %collective-permute-done.18 = f32[32,1280]{1,0:T(8,128)S(1)} collective-permute-done((f32[32,1280]{1,0:T(8,128)S(1)}, f32[32,1280]{1,0:T(8,128)S(1)}, u32[]{:S(2)}, u32[]{:S(2)}) %collective-permute-start.18) | collective-permute-done | bytes 163872 | tf_op jit(solution)/shard_map/ppermute | solution.py:537
  61.1 2.1 %collective-permute-start.21 = (bf16[32,1280]{1,0:T(8,128)(2,1)S(1)}, bf16[32,1280]{1,0:T(8,128)(2,1)S(1)}, u32[]{:S(2)}, u32[]{:S(2)}) collective-permute-start(bf16[32,1280]{1,0:T(8,128)(2,1)S(1)} %get-tuple-element.102), channel_id=1, source_target_pairs={{0,6},{1,25},{2,4},{3,27},{4,2},{5,29},{6,0},{7,31},{8,14},{9,17},... | collective-permute-start | bytes 245768 | tf_op jit(solution)/shard_map/ppermute | solution.py:542
  63.2 1.4 %collective-permute-start.20 = (bf16[32,1280]{1,0:T(8,128)(2,1)S(1)}, bf16[32,1280]{1,0:T(8,128)(2,1)S(1)}, u32[]{:S(2)}, u32[]{:S(2)}) collective-permute-start(bf16[32,1280]{1,0:T(8,128)(2,1)S(1)} %get-tuple-element.102), channel_id=1, source_target_pairs={{0,4},{1,17},{2,6},{3,19},{4,0},{5,21},{6,2},{7,23},{8,12},{9,25},... | collective-permute-start | bytes 245768 | tf_op jit(solution)/shard_map/ppermute | solution.py:542
  64.6 0.7 collective-permute-start.19
  65.3 1.6 %collective-permute-done.21 = bf16[32,1280]{1,0:T(8,128)(2,1)S(1)} collective-permute-done((bf16[32,1280]{1,0:T(8,128)(2,1)S(1)}, bf16[32,1280]{1,0:T(8,128)(2,1)S(1)}, u32[]{:S(2)}, u32[]{:S(2)}) %collective-permute-start.21) | collective-permute-done | bytes 81952 | tf_op jit(solution)/shard_map/ppermute | solution.py:542
  66.9 2.2 %collective-permute-done.20 = bf16[32,1280]{1,0:T(8,128)(2,1)S(1)} collective-permute-done((bf16[32,1280]{1,0:T(8,128)(2,1)S(1)}, bf16[32,1280]{1,0:T(8,128)(2,1)S(1)}, u32[]{:S(2)}, u32[]{:S(2)}) %collective-permute-start.20) | collective-permute-done | bytes 81952 | tf_op jit(solution)/shard_map/ppermute | solution.py:542
  69.2 1.6 %collective-permute-start.24 = (bf16[32,1280]{1,0:T(8,128)(2,1)S(1)}, bf16[32,1280]{1,0:T(8,128)(2,1)S(1)}, u32[]{:S(2)}, u32[]{:S(2)}) collective-permute-start(bf16[32,1280]{1,0:T(8,128)(2,1)S(1)} %get-tuple-element.100), channel_id=1, source_target_pairs={{0,24},{1,7},{2,26},{3,5},{4,28},{5,3},{6,30},{7,1},{8,16},{9,15},... | collective-permute-start | bytes 245768 | tf_op jit(solution)/shard_map/ppermute | solution.py:542
  70.8 1.4 %collective-permute-start.23 = (bf16[32,1280]{1,0:T(8,128)(2,1)S(1)}, bf16[32,1280]{1,0:T(8,128)(2,1)S(1)}, u32[]{:S(2)}, u32[]{:S(2)}) collective-permute-start(bf16[32,1280]{1,0:T(8,128)(2,1)S(1)} %get-tuple-element.100), channel_id=1, source_target_pairs={{0,16},{1,5},{2,18},{3,7},{4,20},{5,1},{6,22},{7,3},{8,24},{9,13},... | collective-permute-start | bytes 245768 | tf_op jit(solution)/shard_map/ppermute | solution.py:542
  72.2 1.2 %collective-permute-start.22 = (bf16[32,1280]{1,0:T(8,128)(2,1)S(1)}, bf16[32,1280]{1,0:T(8,128)(2,1)S(1)}, u32[]{:S(2)}, u32[]{:S(2)}) collective-permute-start(bf16[32,1280]{1,0:T(8,128)(2,1)S(1)} %get-tuple-element.100), channel_id=1, source_target_pairs={{0,8},{1,3},{2,10},{3,1},{4,12},{5,7},{6,14},{7,5},{8,0},{9,11},{1... | collective-permute-start | bytes 245768 | tf_op jit(solution)/shard_map/ppermute | solution.py:542
  73.4 1.6 %collective-permute-done.24 = bf16[32,1280]{1,0:T(8,128)(2,1)S(1)} collective-permute-done((bf16[32,1280]{1,0:T(8,128)(2,1)S(1)}, bf16[32,1280]{1,0:T(8,128)(2,1)S(1)}, u32[]{:S(2)}, u32[]{:S(2)}) %collective-permute-start.24) | collective-permute-done | bytes 81952 | tf_op jit(solution)/shard_map/ppermute | solution.py:542
  75.0 1.8 %collective-permute-done.23 = bf16[32,1280]{1,0:T(8,128)(2,1)S(1)} collective-permute-done((bf16[32,1280]{1,0:T(8,128)(2,1)S(1)}, bf16[32,1280]{1,0:T(8,128)(2,1)S(1)}, u32[]{:S(2)}, u32[]{:S(2)}) %collective-permute-start.23) | collective-permute-done | bytes 81952 | tf_op jit(solution)/shard_map/ppermute | solution.py:542
  76.8 0.1 collective-permute-start.25
  76.9 0.1 slice.17
  77.0 1.1 %collective-permute-start.26 = (f32[1,64]{1,0:T(1,128)S(1)}, f32[1,64]{1,0:T(1,128)S(1)}, u32[]{:S(2)}, u32[]{:S(2)}) collective-permute-start(f32[1,64]{1,0:T(1,128)S(1)} %slice.17), channel_id=1, source_target_pairs={{0,96},{32,64},{64,32},{96,0},{1,97},{33,65},{65,33},{97,1},{2,98}... | collective-permute-start | bytes 776 | tf_op jit(solution)/shard_map/ppermute | solution.py:533
  78.1 0.2 collective-permute-done.25.other_ref
  78.3 0.0 copy-start.7
  78.3 4.2 %merge.1 = (bf16[32,128]{1,0:T(8,128)(2,1)}, bf16[32,32,128]{2,1,0:T(8,128)(2,1)}) custom-call(s32[1]{0:T(128)S(6)} %and.4.core_ref, f32[49,32,2048]{2,1,0:T(8,128)S(1)} %get-tuple-element.86.e_ref, bf16[49,32,2048]{2,1,0:T(8,128)(2,1)S(1)} %get-tuple-element.87.x_ref, f32[32,1280]{1,0:T(8,128)S(1)} %add_add_fusion.mine_ref, ...), custom_call_target="tpu_custom_call" | custom-call | flops 25690112 | bytes 19267584 | tf_op jit(solution)/shard_map/merge/pallas_call | solution.py:428
  82.6 5.1 %all-to-all-start = ((bf16[32,32,128]{2,1,0:T(8,128)(2,1)}), bf16[32,32,128]{2,1,0:T(8,128)(2,1)S(1)}, u32[]{:S(2)}, u32[]{:S(2)}) async-start(bf16[32,32,128]{2,1,0:T(8,128)(2,1)} %get-tuple-element.96), calls=%async_computation | async-start | bytes 524288 | tf_op jit(solution)/shard_map/all_to_all | solution.py:621
  87.7 0.1 slice.19
  87.8 0.2 collective-permute-start.27
  87.9 3.4 %collective-permute-done.27 = f32[1,32]{1,0:T(1,128)S(1)} collective-permute-done((f32[1,32]{1,0:T(1,128)S(1)}, f32[1,32]{1,0:T(1,128)S(1)}, u32[]{:S(2)}, u32[]{:S(2)}) %collective-permute-start.27) | collective-permute-done | bytes 160 | tf_op jit(solution)/shard_map/ppermute | solution.py:533
  91.3 5.2 %all-to-all-done = bf16[32,32,128]{2,1,0:T(8,128)(2,1)S(1)} async-done(((bf16[32,32,128]{2,1,0:T(8,128)(2,1)}), bf16[32,32,128]{2,1,0:T(8,128)(2,1)S(1)}, u32[]{:S(2)}, u32[]{:S(2)}) %all-to-all-start) | async-done | bytes 262176 | tf_op jit(solution)/shard_map/all_to_all | solution.py:621
  96.6 0.8 loss.1
  (52 shorter events, 0.4 us)
Async XLA Ops:
  0.6 21.6 %copy-start.11 = (bf16[32,128]{1,0:T(8,128)(2,1)S(1)}, bf16[32,128]{1,0:T(8,128)(2,1)}, u32[]{:S(2)}) copy-start(bf16[32,128]{1,0:T(8,128)(2,1)} %param.18) | copy-start | bytes 24580
  0.6 29.3 %copy-start.8 = (bf16[9,512,512]{2,1,0:T(8,128)(2,1)S(1)}, bf16[9,512,512]{2,1,0:T(8,128)(2,1)}, u32[]{:S(2)}) copy-start(bf16[9,512,512]{2,1,0:T(8,128)(2,1)} %w_ref.4) | copy-start | bytes 14155780
  0.7 29.3 %copy-start.9 = (f32[512]{0:T(512)S(1)}, f32[512]{0:T(512)}, u32[]{:S(2)}) copy-start(f32[512]{0:T(512)} %param.21) | copy-start | bytes 6148
  0.7 29.3 %copy-start.10 = (f32[512]{0:T(512)S(1)}, f32[512]{0:T(512)}, u32[]{:S(2)}) copy-start(f32[512]{0:T(512)} %param.22) | copy-start | bytes 6148
  6.7 1.3 %collective-permute-start = (f32[32,512]{1,0:T(8,128)S(1)}, f32[32,512]{1,0:T(8,128)S(1)}, u32[]{:S(2)}, u32[]{:S(2)}) collective-permute-start(f32[32,512]{1,0:T(8,128)S(1)} %get-tuple-element.53), channel_id=1, source_target_pairs={{0,1},{1,0},{2,3},{3,2},{4,5},{5,4},{6,7},{7,6},{8,9},{9,8},{10,11... | collective-permute-start | bytes 196616 | tf_op jit(solution)/shard_map/ppermute | solution.py:537
  8.0 6.7 %collective-permute-start.3 = (f32[32,512]{1,0:T(8,128)S(1)}, f32[32,512]{1,0:T(8,128)S(1)}, u32[]{:S(2)}, u32[]{:S(2)}) collective-permute-start(f32[32,512]{1,0:T(8,128)S(1)} %add.83), channel_id=1, source_target_pairs={{0,6},{1,25},{2,4},{3,27},{4,2},{5,29},{6,0},{7,31},{8,14},{9,17},... | collective-permute-start | bytes 196616 | tf_op jit(solution)/shard_map/ppermute | solution.py:542
  12.3 5.8 %collective-permute-start.2 = (f32[32,512]{1,0:T(8,128)S(1)}, f32[32,512]{1,0:T(8,128)S(1)}, u32[]{:S(2)}, u32[]{:S(2)}) collective-permute-start(f32[32,512]{1,0:T(8,128)S(1)} %add.83), channel_id=1, source_target_pairs={{0,4},{1,17},{2,6},{3,19},{4,0},{5,21},{6,2},{7,23},{8,12},{9,25},... | collective-permute-start | bytes 196616 | tf_op jit(solution)/shard_map/ppermute | solution.py:542
  12.3 5.8 %collective-permute-start.1 = (f32[32,512]{1,0:T(8,128)S(1)}, f32[32,512]{1,0:T(8,128)S(1)}, u32[]{:S(2)}, u32[]{:S(2)}) collective-permute-start(f32[32,512]{1,0:T(8,128)S(1)} %add.83), channel_id=1, source_target_pairs={{0,2},{1,9},{2,0},{3,11},{4,6},{5,13},{6,4},{7,15},{8,10},{9,1},{1... | collective-permute-start | bytes 196616 | tf_op jit(solution)/shard_map/ppermute | solution.py:542
  18.1 5.8 %collective-permute-start.6 = (f32[32,512]{1,0:T(8,128)S(1)}, f32[32,512]{1,0:T(8,128)S(1)}, u32[]{:S(2)}, u32[]{:S(2)}) collective-permute-start(f32[32,512]{1,0:T(8,128)S(1)} %add_add_fusion.5), channel_id=1, source_target_pairs={{0,24},{1,7},{2,26},{3,5},{4,28},{5,3},{6,30},{7,1},{8,16},{9,15},... | collective-permute-start | bytes 196616 | tf_op jit(solution)/shard_map/ppermute | solution.py:542
  20.9 5.8 %collective-permute-start.5 = (f32[32,512]{1,0:T(8,128)S(1)}, f32[32,512]{1,0:T(8,128)S(1)}, u32[]{:S(2)}, u32[]{:S(2)}) collective-permute-start(f32[32,512]{1,0:T(8,128)S(1)} %add_add_fusion.5), channel_id=1, source_target_pairs={{0,16},{1,5},{2,18},{3,7},{4,20},{5,1},{6,22},{7,3},{8,24},{9,13},... | collective-permute-start | bytes 196616 | tf_op jit(solution)/shard_map/ppermute | solution.py:542
  21.7 5.0 %collective-permute-start.4 = (f32[32,512]{1,0:T(8,128)S(1)}, f32[32,512]{1,0:T(8,128)S(1)}, u32[]{:S(2)}, u32[]{:S(2)}) collective-permute-start(f32[32,512]{1,0:T(8,128)S(1)} %add_add_fusion.5), channel_id=1, source_target_pairs={{0,8},{1,3},{2,10},{3,1},{4,12},{5,7},{6,14},{7,5},{8,0},{9,11},{1... | collective-permute-start | bytes 196616 | tf_op jit(solution)/shard_map/ppermute | solution.py:542
  22.2 4.6 %collective-permute-start.12 = (bf16[32,128]{1,0:T(8,128)(2,1)S(1)}, bf16[32,128]{1,0:T(8,128)(2,1)S(1)}, u32[]{:S(2)}, u32[]{:S(2)}) collective-permute-start(bf16[32,128]{1,0:T(8,128)(2,1)S(1)} %copy-done.11), channel_id=1, source_target_pairs={{0,32},{32,0},{64,96},{96,64},{1,33},{33,1},{65,97},{97,65},{2,34}... | collective-permute-start | bytes 24584 | tf_op jit(solution)/shard_map/ppermute | solution.py:533
  26.7 3.2 %collective-permute-start.7 = (f32[32,512]{1,0:T(8,128)S(1)}, f32[32,512]{1,0:T(8,128)S(1)}, u32[]{:S(2)}, u32[]{:S(2)}) collective-permute-start(f32[32,512]{1,0:T(8,128)S(1)} %add_add_fusion.4.mine_ref), channel_id=1, source_target_pairs={{0,1},{1,0},{2,3},{3,2},{4,5},{5,4},{6,7},{7,6},{8,9},{9,8},{10,11... | collective-permute-start | bytes 196616 | tf_op jit(solution)/shard_map/ppermute | solution.py:547
  26.8 11.5 %collective-permute-start.13 = (bf16[64,128]{1,0:T(8,128)(2,1)S(1)}, bf16[64,128]{1,0:T(8,128)(2,1)S(1)}, u32[]{:S(2)}, u32[]{:S(2)}) collective-permute-start(bf16[64,128]{1,0:T(8,128)(2,1)S(1)} %pad_maximum_fusion.1), channel_id=1, source_target_pairs={{0,96},{32,64},{64,32},{96,0},{1,97},{33,65},{65,33},{97,1},{2,98}... | collective-permute-start | bytes 49160 | tf_op jit(solution)/shard_map/ppermute | solution.py:533
  29.9 13.9 %copy-start.1 = (bf16[512,2048]{1,0:T(8,128)(2,1)S(1)}, bf16[512,2048]{1,0:T(8,128)(2,1)}, u32[]{:S(2)}) copy-start(bf16[512,2048]{1,0:T(8,128)(2,1)} %w_ref.7) | copy-start | bytes 6291460
  29.9 13.9 %copy-start.5 = (f32[512]{0:T(512)S(1)}, f32[512]{0:T(512)}, u32[]{:S(2)}) copy-start(f32[512]{0:T(512)} %param.24) | copy-start | bytes 6148
  30.0 13.9 %copy-start.6 = (f32[512]{0:T(512)S(1)}, f32[512]{0:T(512)}, u32[]{:S(2)}) copy-start(f32[512]{0:T(512)} %param.25) | copy-start | bytes 6148
  30.0 14.3 %copy-start = (bf16[16384,128]{1,0:T(8,128)(2,1)S(1)}, bf16[16384,128]{1,0:T(8,128)(2,1)}, u32[]{:S(2)}) copy-start(bf16[16384,128]{1,0:T(8,128)(2,1)} %k_ref.3) | copy-start | bytes 12582916
  38.1 1.3 %collective-permute-start.8 = (f32[32,512]{1,0:T(8,128)S(1)}, f32[32,512]{1,0:T(8,128)S(1)}, u32[]{:S(2)}, u32[]{:S(2)}) collective-permute-start(f32[32,512]{1,0:T(8,128)S(1)} %get-tuple-element.64), channel_id=1, source_target_pairs={{0,1},{1,0},{2,3},{3,2},{4,5},{5,4},{6,7},{7,6},{8,9},{9,8},{10,11... | collective-permute-start | bytes 196616 | tf_op jit(solution)/shard_map/ppermute | solution.py:537
  39.4 6.7 %collective-permute-start.11 = (f32[32,512]{1,0:T(8,128)S(1)}, f32[32,512]{1,0:T(8,128)S(1)}, u32[]{:S(2)}, u32[]{:S(2)}) collective-permute-start(f32[32,512]{1,0:T(8,128)S(1)} %add.90), channel_id=1, source_target_pairs={{0,6},{1,25},{2,4},{3,27},{4,2},{5,29},{6,0},{7,31},{8,14},{9,17},... | collective-permute-start | bytes 196616 | tf_op jit(solution)/shard_map/ppermute | solution.py:542
  40.8 5.8 %collective-permute-start.10 = (f32[32,512]{1,0:T(8,128)S(1)}, f32[32,512]{1,0:T(8,128)S(1)}, u32[]{:S(2)}, u32[]{:S(2)}) collective-permute-start(f32[32,512]{1,0:T(8,128)S(1)} %add.90), channel_id=1, source_target_pairs={{0,4},{1,17},{2,6},{3,19},{4,0},{5,21},{6,2},{7,23},{8,12},{9,25},... | collective-permute-start | bytes 196616 | tf_op jit(solution)/shard_map/ppermute | solution.py:542
  41.6 4.9 %collective-permute-start.9 = (f32[32,512]{1,0:T(8,128)S(1)}, f32[32,512]{1,0:T(8,128)S(1)}, u32[]{:S(2)}, u32[]{:S(2)}) collective-permute-start(f32[32,512]{1,0:T(8,128)S(1)} %add.90), channel_id=1, source_target_pairs={{0,2},{1,9},{2,0},{3,11},{4,6},{5,13},{6,4},{7,15},{8,10},{9,1},{1... | collective-permute-start | bytes 196616 | tf_op jit(solution)/shard_map/ppermute | solution.py:542
  46.6 6.0 %collective-permute-start.16 = (f32[32,512]{1,0:T(8,128)S(1)}, f32[32,512]{1,0:T(8,128)S(1)}, u32[]{:S(2)}, u32[]{:S(2)}) collective-permute-start(f32[32,512]{1,0:T(8,128)S(1)} %add_add_fusion.3), channel_id=1, source_target_pairs={{0,24},{1,7},{2,26},{3,5},{4,28},{5,3},{6,30},{7,1},{8,16},{9,15},... | collective-permute-start | bytes 196616 | tf_op jit(solution)/shard_map/ppermute | solution.py:542
  48.4 5.8 %collective-permute-start.15 = (f32[32,512]{1,0:T(8,128)S(1)}, f32[32,512]{1,0:T(8,128)S(1)}, u32[]{:S(2)}, u32[]{:S(2)}) collective-permute-start(f32[32,512]{1,0:T(8,128)S(1)} %add_add_fusion.3), channel_id=1, source_target_pairs={{0,16},{1,5},{2,18},{3,7},{4,20},{5,1},{6,22},{7,3},{8,24},{9,13},... | collective-permute-start | bytes 196616 | tf_op jit(solution)/shard_map/ppermute | solution.py:542
  49.2 5.0 %collective-permute-start.14 = (f32[32,512]{1,0:T(8,128)S(1)}, f32[32,512]{1,0:T(8,128)S(1)}, u32[]{:S(2)}, u32[]{:S(2)}) collective-permute-start(f32[32,512]{1,0:T(8,128)S(1)} %add_add_fusion.3), channel_id=1, source_target_pairs={{0,8},{1,3},{2,10},{3,1},{4,12},{5,7},{6,14},{7,5},{8,0},{9,11},{1... | collective-permute-start | bytes 196616 | tf_op jit(solution)/shard_map/ppermute | solution.py:542
  54.2 1.5 %collective-permute-start.17 = (f32[32,512]{1,0:T(8,128)S(1)}, f32[32,512]{1,0:T(8,128)S(1)}, u32[]{:S(2)}, u32[]{:S(2)}) collective-permute-start(f32[32,512]{1,0:T(8,128)S(1)} %add_add_fusion.2.mine_ref), channel_id=1, source_target_pairs={{0,1},{1,0},{2,3},{3,2},{4,5},{5,4},{6,7},{7,6},{8,9},{9,8},{10,11... | collective-permute-start | bytes 196616 | tf_op jit(solution)/shard_map/ppermute | solution.py:547
  55.7 22.6 %copy-start.2 = (bf16[2048,128]{1,0:T(8,128)(2,1)S(1)}, bf16[2048,128]{1,0:T(8,128)(2,1)}, u32[]{:S(2)}) copy-start(bf16[2048,128]{1,0:T(8,128)(2,1)} %proj_ref.1) | copy-start | bytes 1572868
  55.7 22.6 %copy-start.3 = (f32[2048]{0:T(1024)S(1)}, f32[2048]{0:T(1024)}, u32[]{:S(2)}) copy-start(f32[2048]{0:T(1024)} %param.27) | copy-start | bytes 24580
  55.7 22.6 %copy-start.4 = (f32[2048]{0:T(1024)S(1)}, f32[2048]{0:T(1024)}, u32[]{:S(2)}) copy-start(f32[2048]{0:T(1024)} %param.28) | copy-start | bytes 24580
  59.6 1.5 %collective-permute-start.18 = (f32[32,1280]{1,0:T(8,128)S(1)}, f32[32,1280]{1,0:T(8,128)S(1)}, u32[]{:S(2)}, u32[]{:S(2)}) collective-permute-start(f32[32,1280]{1,0:T(8,128)S(1)} %get-tuple-element.89), channel_id=1, source_target_pairs={{0,1},{1,0},{2,3},{3,2},{4,5},{5,4},{6,7},{7,6},{8,9},{9,8},{10,11... | collective-permute-start | bytes 491528 | tf_op jit(solution)/shard_map/ppermute | solution.py:537
  61.1 5.7 %collective-permute-start.21 = (bf16[32,1280]{1,0:T(8,128)(2,1)S(1)}, bf16[32,1280]{1,0:T(8,128)(2,1)S(1)}, u32[]{:S(2)}, u32[]{:S(2)}) collective-permute-start(bf16[32,1280]{1,0:T(8,128)(2,1)S(1)} %get-tuple-element.102), channel_id=1, source_target_pairs={{0,6},{1,25},{2,4},{3,27},{4,2},{5,29},{6,0},{7,31},{8,14},{9,17},... | collective-permute-start | bytes 245768 | tf_op jit(solution)/shard_map/ppermute | solution.py:542
  63.2 5.9 %collective-permute-start.20 = (bf16[32,1280]{1,0:T(8,128)(2,1)S(1)}, bf16[32,1280]{1,0:T(8,128)(2,1)S(1)}, u32[]{:S(2)}, u32[]{:S(2)}) collective-permute-start(bf16[32,1280]{1,0:T(8,128)(2,1)S(1)} %get-tuple-element.102), channel_id=1, source_target_pairs={{0,4},{1,17},{2,6},{3,19},{4,0},{5,21},{6,2},{7,23},{8,12},{9,25},... | collective-permute-start | bytes 245768 | tf_op jit(solution)/shard_map/ppermute | solution.py:542
  64.6 4.5 %collective-permute-start.19 = (bf16[32,1280]{1,0:T(8,128)(2,1)S(1)}, bf16[32,1280]{1,0:T(8,128)(2,1)S(1)}, u32[]{:S(2)}, u32[]{:S(2)}) collective-permute-start(bf16[32,1280]{1,0:T(8,128)(2,1)S(1)} %get-tuple-element.102), channel_id=1, source_target_pairs={{0,2},{1,9},{2,0},{3,11},{4,6},{5,13},{6,4},{7,15},{8,10},{9,1},{1... | collective-permute-start | bytes 245768 | tf_op jit(solution)/shard_map/ppermute | solution.py:542
  69.2 5.7 %collective-permute-start.24 = (bf16[32,1280]{1,0:T(8,128)(2,1)S(1)}, bf16[32,1280]{1,0:T(8,128)(2,1)S(1)}, u32[]{:S(2)}, u32[]{:S(2)}) collective-permute-start(bf16[32,1280]{1,0:T(8,128)(2,1)S(1)} %get-tuple-element.100), channel_id=1, source_target_pairs={{0,24},{1,7},{2,26},{3,5},{4,28},{5,3},{6,30},{7,1},{8,16},{9,15},... | collective-permute-start | bytes 245768 | tf_op jit(solution)/shard_map/ppermute | solution.py:542
  70.8 5.9 %collective-permute-start.23 = (bf16[32,1280]{1,0:T(8,128)(2,1)S(1)}, bf16[32,1280]{1,0:T(8,128)(2,1)S(1)}, u32[]{:S(2)}, u32[]{:S(2)}) collective-permute-start(bf16[32,1280]{1,0:T(8,128)(2,1)S(1)} %get-tuple-element.100), channel_id=1, source_target_pairs={{0,16},{1,5},{2,18},{3,7},{4,20},{5,1},{6,22},{7,3},{8,24},{9,13},... | collective-permute-start | bytes 245768 | tf_op jit(solution)/shard_map/ppermute | solution.py:542
  72.2 4.5 %collective-permute-start.22 = (bf16[32,1280]{1,0:T(8,128)(2,1)S(1)}, bf16[32,1280]{1,0:T(8,128)(2,1)S(1)}, u32[]{:S(2)}, u32[]{:S(2)}) collective-permute-start(bf16[32,1280]{1,0:T(8,128)(2,1)S(1)} %get-tuple-element.100), channel_id=1, source_target_pairs={{0,8},{1,3},{2,10},{3,1},{4,12},{5,7},{6,14},{7,5},{8,0},{9,11},{1... | collective-permute-start | bytes 245768 | tf_op jit(solution)/shard_map/ppermute | solution.py:542
  76.8 1.5 %collective-permute-start.25 = (f32[32,1280]{1,0:T(8,128)S(1)}, f32[32,1280]{1,0:T(8,128)S(1)}, u32[]{:S(2)}, u32[]{:S(2)}) collective-permute-start(f32[32,1280]{1,0:T(8,128)S(1)} %add_add_fusion.mine_ref), channel_id=1, source_target_pairs={{0,1},{1,0},{2,3},{3,2},{4,5},{5,4},{6,7},{7,6},{8,9},{9,8},{10,11... | collective-permute-start | bytes 491528 | tf_op jit(solution)/shard_map/ppermute | solution.py:547
  77.0 10.7 %collective-permute-start.26 = (f32[1,64]{1,0:T(1,128)S(1)}, f32[1,64]{1,0:T(1,128)S(1)}, u32[]{:S(2)}, u32[]{:S(2)}) collective-permute-start(f32[1,64]{1,0:T(1,128)S(1)} %slice.17), channel_id=1, source_target_pairs={{0,96},{32,64},{64,32},{96,0},{1,97},{33,65},{65,33},{97,1},{2,98}... | collective-permute-start | bytes 776 | tf_op jit(solution)/shard_map/ppermute | solution.py:533
  78.3 18.3 %copy-start.7 = (s32[32]{0:T(128)S(1)}, s32[32]{0:T(128)}, u32[]{:S(2)}) copy-start(s32[32]{0:T(128)} %param.17) | copy-start | bytes 388
  82.6 14.0 %all-to-all-start = ((bf16[32,32,128]{2,1,0:T(8,128)(2,1)}), bf16[32,32,128]{2,1,0:T(8,128)(2,1)S(1)}, u32[]{:S(2)}, u32[]{:S(2)}) async-start(bf16[32,32,128]{2,1,0:T(8,128)(2,1)} %get-tuple-element.96), calls=%async_computation | async-start | bytes 524288 | tf_op jit(solution)/shard_map/all_to_all | solution.py:621
  87.8 3.6 %collective-permute-start.27 = (f32[1,32]{1,0:T(1,128)S(1)}, f32[1,32]{1,0:T(1,128)S(1)}, u32[]{:S(2)}, u32[]{:S(2)}) collective-permute-start(f32[1,32]{1,0:T(1,128)S(1)} %slice.19), channel_id=1, source_target_pairs={{0,32},{32,0},{64,96},{96,64},{1,33},{33,1},{65,97},{97,65},{2,34}... | collective-permute-start | bytes 392 | tf_op jit(solution)/shard_map/ppermute | solution.py:533

commit v2 on v1

--- a/solution.py
+++ b/solution.py
@@ -71,6 +71,7 @@
 
 def reduce_kernel(
     me_ref,
+    core_ref,
     x_hbm,
     w_hbm,
     shuffle_hbm,
@@ -110,12 +111,12 @@
         y_ref[part] = y
         s1 += jnp.sum(y, 0)
         s2 += jnp.sum(y * y, 0)
-    core = jnp.bitwise_and(me_ref[0], 1)
+    core = core_ref[0]
     split_halves(core, reorder(by_set, s1), keep_ref, send_ref, 0)
     split_halves(core, reorder(by_set, s2), keep_ref, send_ref, mid // 2)
 
 
-def reduce_stage(me, x, weight, shuffle):
+def reduce_stage(me, core, x, weight, shuffle):
     places, count, channels = x.shape
     mid = weight.shape[1]
     sets = shuffle.shape[1] // count
@@ -123,7 +124,7 @@
     return pl.pallas_call(
         reduce_kernel,
         name="reduce",
-        in_specs=[SMEM, hbm, hbm, hbm],
+        in_specs=[SMEM, SMEM, hbm, hbm, hbm],
         out_specs=[VMEM] * 6,
         out_shape=[
             jax.ShapeDtypeStruct((places, count, mid), F32),
@@ -144,7 +145,7 @@
             bytes_accessed=2 * x.size + 4 * places * count * mid,
             transcendentals=0,
         ),
-    )(me, *[pltpu.with_memory_space_constraint(v, pltpu.HBM) for v in (x, weight, shuffle)])
+    )(me, core, *[pltpu.with_memory_space_constraint(v, pltpu.HBM) for v in (x, weight, shuffle)])
 
 
 def scale_shift(core, mine, other, onehot, gain, shift, rows):
@@ -517,15 +518,20 @@
     return [(i, i ^ 1) for i in range(2 * RING * RING)]
 
 
+def mixed(v):
+    return (v ^ (v >> 1)) & 1
+
+
 def ring_swap(k, flip):
     pairs = []
     for i in range(2 * RING * RING):
         x, z, c = i // (2 * RING), (i // 2) % RING, i % 2
-        if (c == 1) != flip:
+        half = c ^ mixed(x) ^ mixed(z)
+        if (half == 1) != flip:
             x = x ^ k
         else:
             z = z ^ k
-        pairs.append((i, (x * RING + z) * 2 + c))
+        pairs.append((i, (x * RING + z) * 2 + (half ^ mixed(x) ^ mixed(z))))
     return pairs
 
 
@@ -566,8 +572,9 @@
 ):
     count, places, _ = features.shape
     peers = lax.axis_size("dp")
-    me = lax.axis_index("dp").astype(jnp.int32).reshape(1)
-    core = jnp.bitwise_and(me, 1)
+    me = lax.axis_index("dp").astype(jnp.int32)
+    core = me ^ mixed(me >> 3) ^ mixed((me >> 1) & 3)
+    core = jnp.bitwise_and(core, 1).reshape(1)
     rows = count * places
     x = jnp.transpose(features, (1, 0, 2))
     gain_two, shift_two = gain_two[None], shift_two[None]
@@ -586,7 +593,7 @@
         return None, None
 
     first = queue_swap(queries, 1)
-    y, keep, send, by_set, by_image, x = reduce_stage(me, x, reduce_weight, shuffle)
+    y, keep, send, by_set, by_image, x = reduce_stage(me.reshape(1), core, x, reduce_weight, shuffle)
     pair = jnp.concatenate([queries, first], 0)
     mine, other, _ = reduce_sets(keep, send, (nothing, nothing), None, F32)
     asked = jnp.concatenate([pair, queue_swap(pair, 3)], 0)

time: 98.8 us -> 95.1 us (0.963)
  starting transfers between devices: 38.1 us -> 35.8 us
  waiting for transfers between devices: 30.5 us -> 29.2 us
    ppermute x18, starting transfers between devices: 26 us -> 24.4 us  [reduce_sets(): parts.append(lax.ppermute(sent, 'dp', ring_swap(k, turn == 1)).astype(F32))]
    ppermute x18, waiting for transfers between devices: 16.8 us -> 15.3 us  [reduce_sets(): parts.append(lax.ppermute(sent, 'dp', ring_swap(k, turn == 1)).astype(F32))]
  transfers between devices with their start and end apart: 29 -> 29, of which waited for: 16 -> 18; matrix products, arithmetic and copies ran while one was open for 0% -> 0% of each run, Pallas kernels for 17% -> 17%
where the time goes in v2:
time: 95.1 us; the launch traced here: 93.7 us
  starting transfers between devices  35.8 us (38%)
  waiting for transfers between devices  29.2 us (31%)
  Pallas kernels  27.1 us (28%)
  between operations  0.99 us (1%)
    ppermute x18, starting transfers between devices, reduce_sets(): parts.append(lax.ppermute(sent, 'dp', ring_swap(k, turn == 1)).astype(F32))  24.4 us
    ppermute x18, waiting for transfers between devices, reduce_sets(): parts.append(lax.ppermute(sent, 'dp', ring_swap(k, turn == 1)).astype(F32))  15.3 us
    pallas_call x1, Pallas kernels, conv_stage(): pl.pallas_call(functools.partial(conv_kernel, rows), name='conv', grid=(S...  8.12 us
    pallas_call x1, Pallas kernels, reduce_stage(): pl.pallas_call(reduce_kernel, name='reduce', in_specs=[SMEM, SMEM, hbm, h...  6 us
    ppermute x4, starting transfers between devices, queue_swap(): return lax.ppermute(values, 'queue', [(i, i ^ k) for i in range(RING)])  5.76 us
    all_to_all x1, waiting for transfers between devices, on_device(): lax.all_to_all(copies, 'dp', split_axis=0, concat_axis=0, tiled=True)  5.22 us
    all_to_all x1, starting transfers between devices, on_device(): lax.all_to_all(copies, 'dp', split_axis=0, concat_axis=0, tiled=True)  4.62 us
    pallas_call x1, Pallas kernels, merge_stage(): pl.pallas_call(functools.partial(merge_kernel, rows), name='merge', in_sp...  4.22 us
  transfers between devices with their start and end apart: 29, of which 18 were waited for; matrix products, arithmetic and copies ran while one was open for 0% of the time, Pallas kernels for 17%

profile of v2, /device:TPU:0, one launch (start us, length us, event | category | flops | bytes accessed | tf_op | source)
XLA Modules:
  0.0 93.7 jit_solution(14493583975836052619)
XLA Ops:
  0.7 6.0 %reduce.1 = (f32[49,32,512]{2,1,0:T(8,128)S(1)}, f32[32,512]{1,0:T(8,128)S(1)}, f32[32,512]{1,0:T(8,128)S(1)}, bf16[32,96]{1,0:T(8,128)(2,1)S(1)}, bf16[32,96]{1...) custom-call(s32[1]{0:T(128)} %bitcast.1.me_ref, s32[1]{0:T(128)} %bitcast.core_ref, bf16[49,32,2048]{2,1,0:T(8,128)(2,1)} %bitcast.23, ...), custom_call_target="tpu_custom_call" | custom-call | flops 3288334336 | bytes 9633792 | tf_op jit(solution)/shard_map/reduce/pallas_call | solution.py:124
  6.7 0.1 collective-permute-start
  6.8 1.2 %collective-permute-done = f32[32,512]{1,0:T(8,128)S(1)} collective-permute-done((f32[32,512]{1,0:T(8,128)S(1)}, f32[32,512]{1,0:T(8,128)S(1)}, u32[]{:S(2)}, u32[]{:S(2)}) %collective-permute-start) | collective-permute-done | bytes 65568 | tf_op jit(solution)/shard_map/ppermute | solution.py:543
  8.0 4.2 %collective-permute-start.3 = (f32[32,512]{1,0:T(8,128)S(1)}, f32[32,512]{1,0:T(8,128)S(1)}, u32[]{:S(2)}, u32[]{:S(2)}) collective-permute-start(f32[32,512]{1,0:T(8,128)S(1)} %add.83), channel_id=1, source_target_pairs={{0,6},{1,25},{2,26},{3,5},{4,28},{5,3},{6,0},{7,31},{8,16},{9,15},... | collective-permute-start | bytes 196616 | tf_op jit(solution)/shard_map/ppermute | solution.py:548
  12.3 0.7 collective-permute-start.1
  12.9 1.7 %collective-permute-done.3 = f32[32,512]{1,0:T(8,128)S(1)} collective-permute-done((f32[32,512]{1,0:T(8,128)S(1)}, f32[32,512]{1,0:T(8,128)S(1)}, u32[]{:S(2)}, u32[]{:S(2)}) %collective-permute-start.3) | collective-permute-done | bytes 65568 | tf_op jit(solution)/shard_map/ppermute | solution.py:548
  14.6 2.9 %collective-permute-done.2 = f32[32,512]{1,0:T(8,128)S(1)} collective-permute-done((f32[32,512]{1,0:T(8,128)S(1)}, f32[32,512]{1,0:T(8,128)S(1)}, u32[]{:S(2)}, u32[]{:S(2)}) %collective-permute-start.2) | collective-permute-done | bytes 65568 | tf_op jit(solution)/shard_map/ppermute | solution.py:548
  17.5 2.8 %collective-permute-start.6 = (f32[32,512]{1,0:T(8,128)S(1)}, f32[32,512]{1,0:T(8,128)S(1)}, u32[]{:S(2)}, u32[]{:S(2)}) collective-permute-start(f32[32,512]{1,0:T(8,128)S(1)} %add_add_fusion.5), channel_id=1, source_target_pairs={{0,24},{1,7},{2,4},{3,27},{4,2},{5,29},{6,30},{7,1},{8,14},{9,17},... | collective-permute-start | bytes 196616 | tf_op jit(solution)/shard_map/ppermute | solution.py:548
  20.3 1.1 %collective-permute-start.4 = (f32[32,512]{1,0:T(8,128)S(1)}, f32[32,512]{1,0:T(8,128)S(1)}, u32[]{:S(2)}, u32[]{:S(2)}) collective-permute-start(f32[32,512]{1,0:T(8,128)S(1)} %add_add_fusion.5), channel_id=1, source_target_pairs={{0,9},{1,2},{2,1},{3,10},{4,7},{5,12},{6,15},{7,4},{8,11},{9,0},{1... | collective-permute-start | bytes 196616 | tf_op jit(solution)/shard_map/ppermute | solution.py:548
  21.4 1.6 %collective-permute-start.12 = (bf16[32,128]{1,0:T(8,128)(2,1)S(1)}, bf16[32,128]{1,0:T(8,128)(2,1)S(1)}, u32[]{:S(2)}, u32[]{:S(2)}) collective-permute-start(bf16[32,128]{1,0:T(8,128)(2,1)S(1)} %copy-done.11), channel_id=1, source_target_pairs={{0,32},{32,0},{64,96},{96,64},{1,33},{33,1},{65,97},{97,65},{2,34}... | collective-permute-start | bytes 24584 | tf_op jit(solution)/shard_map/ppermute | solution.py:539
  23.0 0.1 collective-permute-done.6
  23.1 2.5 %collective-permute-done.5 = f32[32,512]{1,0:T(8,128)S(1)} collective-permute-done((f32[32,512]{1,0:T(8,128)S(1)}, f32[32,512]{1,0:T(8,128)S(1)}, u32[]{:S(2)}, u32[]{:S(2)}) %collective-permute-start.5) | collective-permute-done | bytes 65568 | tf_op jit(solution)/shard_map/ppermute | solution.py:548
  25.6 0.1 collective-permute-start.7
  25.7 3.1 %collective-permute-start.13 = (bf16[64,128]{1,0:T(8,128)(2,1)S(1)}, bf16[64,128]{1,0:T(8,128)(2,1)S(1)}, u32[]{:S(2)}, u32[]{:S(2)}) collective-permute-start(bf16[64,128]{1,0:T(8,128)(2,1)S(1)} %pad_maximum_fusion.1), channel_id=1, source_target_pairs={{0,96},{32,64},{64,32},{96,0},{1,97},{33,65},{65,33},{97,1},{2,98}... | collective-permute-start | bytes 49160 | tf_op jit(solution)/shard_map/ppermute | solution.py:539
  28.8 0.0 copy-start.1
  28.8 0.0 copy-start.5
  28.8 0.0 copy-start.6
  28.8 8.1 %conv.1 = (f32[49,32,512]{2,1,0:T(8,128)S(1)}, f32[32,512]{1,0:T(8,128)S(1)}, f32[32,512]{1,0:T(8,128)S(1)}) custom-call(s32[1]{0:T(128)} %bitcast.core_ref, f32[49,32,512]{2,1,0:T(8,128)S(1)} %get-tuple-element.51.y_ref, f32[32,512]{1,0:T(8,128)S(1)} %add_add_fusion.4.mine_ref, f32[32,512]{1,0:T(8,128)S(1)} %collective-permute-done.7.other_ref, ...), custom_call_target="tpu_custom_call" | custom-call | flops 6056574976 | bytes 11141120 | tf_op jit(solution)/shard_map/conv/pallas_call | solution.py:240
  37.0 0.2 collective-permute-start.8
  37.2 1.1 %collective-permute-done.8 = f32[32,512]{1,0:T(8,128)S(1)} collective-permute-done((f32[32,512]{1,0:T(8,128)S(1)}, f32[32,512]{1,0:T(8,128)S(1)}, u32[]{:S(2)}, u32[]{:S(2)}) %collective-permute-start.8) | collective-permute-done | bytes 65568 | tf_op jit(solution)/shard_map/ppermute | solution.py:543
  38.3 1.3 %collective-permute-start.11 = (f32[32,512]{1,0:T(8,128)S(1)}, f32[32,512]{1,0:T(8,128)S(1)}, u32[]{:S(2)}, u32[]{:S(2)}) collective-permute-start(f32[32,512]{1,0:T(8,128)S(1)} %add.90), channel_id=1, source_target_pairs={{0,6},{1,25},{2,26},{3,5},{4,28},{5,3},{6,0},{7,31},{8,16},{9,15},... | collective-permute-start | bytes 196616 | tf_op jit(solution)/shard_map/ppermute | solution.py:548
  39.7 0.5 collective-permute-start.10
  40.1 2.1 %collective-permute-start.9 = (f32[32,512]{1,0:T(8,128)S(1)}, f32[32,512]{1,0:T(8,128)S(1)}, u32[]{:S(2)}, u32[]{:S(2)}) collective-permute-start(f32[32,512]{1,0:T(8,128)S(1)} %add.90), channel_id=1, source_target_pairs={{0,3},{1,8},{2,11},{3,0},{4,13},{5,6},{6,5},{7,14},{8,1},{9,10},{1... | collective-permute-start | bytes 196616 | tf_op jit(solution)/shard_map/ppermute | solution.py:548
  42.2 0.1 fusion
  42.3 0.1 fusion.1.q_ref
  42.5 0.4 center.1
  42.8 1.8 %negative.2 = f32[1,128]{1,0:T(1,128)S(1)} custom-call(bf16[128,128]{1,0:T(8,128)(2,1)S(1)} %fusion.1.q_ref, bf16[16384,128]{1,0:T(8,128)(2,1)S(1)} %copy-done), custom_call_target="tpu_custom_call" | custom-call | flops 268435456 | bytes 2097152 | tf_op jit(solution)/shard_map/negative/pallas_call | solution.py:471
  44.7 0.2 collective-permute-done.10
  44.8 0.0 collective-permute-done.9
  44.9 2.1 %collective-permute-start.16 = (f32[32,512]{1,0:T(8,128)S(1)}, f32[32,512]{1,0:T(8,128)S(1)}, u32[]{:S(2)}, u32[]{:S(2)}) collective-permute-start(f32[32,512]{1,0:T(8,128)S(1)} %add_add_fusion.3), channel_id=1, source_target_pairs={{0,24},{1,7},{2,4},{3,27},{4,2},{5,29},{6,30},{7,1},{8,14},{9,17},... | collective-permute-start | bytes 196616 | tf_op jit(solution)/shard_map/ppermute | solution.py:548
  47.0 0.2 collective-permute-start.15
  47.2 1.5 %collective-permute-start.14 = (f32[32,512]{1,0:T(8,128)S(1)}, f32[32,512]{1,0:T(8,128)S(1)}, u32[]{:S(2)}, u32[]{:S(2)}) collective-permute-start(f32[32,512]{1,0:T(8,128)S(1)} %add_add_fusion.3), channel_id=1, source_target_pairs={{0,9},{1,2},{2,1},{3,10},{4,7},{5,12},{6,15},{7,4},{8,11},{9,0},{1... | collective-permute-start | bytes 196616 | tf_op jit(solution)/shard_map/ppermute | solution.py:548
  48.8 1.8 %negative.3 = f32[1,128]{1,0:T(1,128)S(1)} custom-call(bf16[128,128]{1,0:T(8,128)(2,1)S(1)} %fusion.1.q_ref, bf16[16384,128]{1,0:T(8,128)(2,1)S(1)} %copy-done), custom_call_target="tpu_custom_call" | custom-call | flops 268435456 | bytes 2097152 | tf_op jit(solution)/shard_map/negative/pallas_call | solution.py:471
  50.6 1.6 %collective-permute-done.15 = f32[32,512]{1,0:T(8,128)S(1)} collective-permute-done((f32[32,512]{1,0:T(8,128)S(1)}, f32[32,512]{1,0:T(8,128)S(1)}, u32[]{:S(2)}, u32[]{:S(2)}) %collective-permute-start.15) | collective-permute-done | bytes 65568 | tf_op jit(solution)/shard_map/ppermute | solution.py:548
  52.2 0.3 collective-permute-start.17
  52.6 1.2 %collective-permute-done.17.other_ref = f32[32,512]{1,0:T(8,128)S(1)} collective-permute-done((f32[32,512]{1,0:T(8,128)S(1)}, f32[32,512]{1,0:T(8,128)S(1)}, u32[]{:S(2)}, u32[]{:S(2)}) %collective-permute-start.17) | collective-permute-done | bytes 65568 | tf_op jit(solution)/shard_map/ppermute | solution.py:553
  53.8 3.9 %expand.1 = (f32[49,32,2048]{2,1,0:T(8,128)S(1)}, f32[32,1280]{1,0:T(8,128)S(1)}, f32[32,1280]{1,0:T(8,128)S(1)}) custom-call(s32[1]{0:T(128)} %bitcast.core_ref, f32[49,32,512]{2,1,0:T(8,128)S(1)} %get-tuple-element.62.z_ref, f32[32,512]{1,0:T(8,128)S(1)} %add_add_fusion.2.mine_ref, f32[32,512]{1,0:T(8,128)S(1)} %collective-permute-done.17.other_ref, ...), custom_call_target="tpu_custom_call" | custom-call | flops 3288334336 | bytes 16056320 | tf_op jit(solution)/shard_map/expand/pallas_call | solution.py:352
  57.7 0.2 collective-permute-start.18
  57.9 1.2 %collective-permute-done.18 = f32[32,1280]{1,0:T(8,128)S(1)} collective-permute-done((f32[32,1280]{1,0:T(8,128)S(1)}, f32[32,1280]{1,0:T(8,128)S(1)}, u32[]{:S(2)}, u32[]{:S(2)}) %collective-permute-start.18) | collective-permute-done | bytes 163872 | tf_op jit(solution)/shard_map/ppermute | solution.py:543
  59.2 2.1 %collective-permute-start.21 = (bf16[32,1280]{1,0:T(8,128)(2,1)S(1)}, bf16[32,1280]{1,0:T(8,128)(2,1)S(1)}, u32[]{:S(2)}, u32[]{:S(2)}) collective-permute-start(bf16[32,1280]{1,0:T(8,128)(2,1)S(1)} %get-tuple-element.102), channel_id=1, source_target_pairs={{0,6},{1,25},{2,26},{3,5},{4,28},{5,3},{6,0},{7,31},{8,16},{9,15},... | collective-permute-start | bytes 245768 | tf_op jit(solution)/shard_map/ppermute | solution.py:548
  61.2 0.6 collective-permute-start.20
  61.8 1.3 %collective-permute-start.19 = (bf16[32,1280]{1,0:T(8,128)(2,1)S(1)}, bf16[32,1280]{1,0:T(8,128)(2,1)S(1)}, u32[]{:S(2)}, u32[]{:S(2)}) collective-permute-start(bf16[32,1280]{1,0:T(8,128)(2,1)S(1)} %get-tuple-element.102), channel_id=1, source_target_pairs={{0,3},{1,8},{2,11},{3,0},{4,13},{5,6},{6,5},{7,14},{8,1},{9,10},{1... | collective-permute-start | bytes 245768 | tf_op jit(solution)/shard_map/ppermute | solution.py:548
  63.1 1.8 %collective-permute-done.21 = bf16[32,1280]{1,0:T(8,128)(2,1)S(1)} collective-permute-done((bf16[32,1280]{1,0:T(8,128)(2,1)S(1)}, bf16[32,1280]{1,0:T(8,128)(2,1)S(1)}, u32[]{:S(2)}, u32[]{:S(2)}) %collective-permute-start.21) | collective-permute-done | bytes 81952 | tf_op jit(solution)/shard_map/ppermute | solution.py:548
  64.9 1.7 %collective-permute-done.20 = bf16[32,1280]{1,0:T(8,128)(2,1)S(1)} collective-permute-done((bf16[32,1280]{1,0:T(8,128)(2,1)S(1)}, bf16[32,1280]{1,0:T(8,128)(2,1)S(1)}, u32[]{:S(2)}, u32[]{:S(2)}) %collective-permute-start.20) | collective-permute-done | bytes 81952 | tf_op jit(solution)/shard_map/ppermute | solution.py:548
  66.6 0.1 fusion.2
  66.7 1.3 %collective-permute-start.24 = (bf16[32,1280]{1,0:T(8,128)(2,1)S(1)}, bf16[32,1280]{1,0:T(8,128)(2,1)S(1)}, u32[]{:S(2)}, u32[]{:S(2)}) collective-permute-start(bf16[32,1280]{1,0:T(8,128)(2,1)S(1)} %get-tuple-element.100), channel_id=1, source_target_pairs={{0,24},{1,7},{2,4},{3,27},{4,2},{5,29},{6,30},{7,1},{8,14},{9,17},... | collective-permute-start | bytes 245768 | tf_op jit(solution)/shard_map/ppermute | solution.py:548
  68.0 0.5 collective-permute-start.23
  68.5 2.0 %collective-permute-start.22 = (bf16[32,1280]{1,0:T(8,128)(2,1)S(1)}, bf16[32,1280]{1,0:T(8,128)(2,1)S(1)}, u32[]{:S(2)}, u32[]{:S(2)}) collective-permute-start(bf16[32,1280]{1,0:T(8,128)(2,1)S(1)} %get-tuple-element.100), channel_id=1, source_target_pairs={{0,9},{1,2},{2,1},{3,10},{4,7},{5,12},{6,15},{7,4},{8,11},{9,0},{1... | collective-permute-start | bytes 245768 | tf_op jit(solution)/shard_map/ppermute | solution.py:548
  70.6 1.8 %collective-permute-done.24 = bf16[32,1280]{1,0:T(8,128)(2,1)S(1)} collective-permute-done((bf16[32,1280]{1,0:T(8,128)(2,1)S(1)}, bf16[32,1280]{1,0:T(8,128)(2,1)S(1)}, u32[]{:S(2)}, u32[]{:S(2)}) %collective-permute-start.24) | collective-permute-done | bytes 81952 | tf_op jit(solution)/shard_map/ppermute | solution.py:548
  72.4 1.0 %collective-permute-done.23 = bf16[32,1280]{1,0:T(8,128)(2,1)S(1)} collective-permute-done((bf16[32,1280]{1,0:T(8,128)(2,1)S(1)}, bf16[32,1280]{1,0:T(8,128)(2,1)S(1)}, u32[]{:S(2)}, u32[]{:S(2)}) %collective-permute-start.23) | collective-permute-done | bytes 81952 | tf_op jit(solution)/shard_map/ppermute | solution.py:548
  73.4 0.2 collective-permute-done.22
  73.6 0.1 add_add_fusion.mine_ref
  73.7 0.1 collective-permute-start.25
  73.7 0.1 slice.17
  73.8 0.9 collective-permute-start.26
  74.7 0.4 collective-permute-done.25.other_ref
  75.1 0.0 copy-start.7
  75.2 4.2 %merge.1 = (bf16[32,128]{1,0:T(8,128)(2,1)}, bf16[32,32,128]{2,1,0:T(8,128)(2,1)}) custom-call(s32[1]{0:T(128)} %bitcast.core_ref, f32[49,32,2048]{2,1,0:T(8,128)S(1)} %get-tuple-element.86.e_ref, bf16[49,32,2048]{2,1,0:T(8,128)(2,1)S(1)} %get-tuple-element.87.x_ref, f32[32,1280]{1,0:T(8,128)S(1)} %add_add_fusion.mine_ref, ...), custom_call_target="tpu_custom_call" | custom-call | flops 25690112 | bytes 19267584 | tf_op jit(solution)/shard_map/merge/pallas_call | solution.py:429
  79.4 4.6 %all-to-all-start = ((bf16[32,32,128]{2,1,0:T(8,128)(2,1)}), bf16[32,32,128]{2,1,0:T(8,128)(2,1)S(1)}, u32[]{:S(2)}, u32[]{:S(2)}) async-start(bf16[32,32,128]{2,1,0:T(8,128)(2,1)} %get-tuple-element.96), calls=%async_computation | async-start | bytes 524288 | tf_op jit(solution)/shard_map/all_to_all | solution.py:628
  84.0 0.1 slice.19
  84.1 0.2 collective-permute-start.27
  84.3 3.4 %collective-permute-done.27 = f32[1,32]{1,0:T(1,128)S(1)} collective-permute-done((f32[1,32]{1,0:T(1,128)S(1)}, f32[1,32]{1,0:T(1,128)S(1)}, u32[]{:S(2)}, u32[]{:S(2)}) %collective-permute-start.27) | collective-permute-done | bytes 160 | tf_op jit(solution)/shard_map/ppermute | solution.py:539
  87.7 5.2 %all-to-all-done = bf16[32,32,128]{2,1,0:T(8,128)(2,1)S(1)} async-done(((bf16[32,32,128]{2,1,0:T(8,128)(2,1)}), bf16[32,32,128]{2,1,0:T(8,128)(2,1)S(1)}, u32[]{:S(2)}, u32[]{:S(2)}) %all-to-all-start) | async-done | bytes 262176 | tf_op jit(solution)/shard_map/all_to_all | solution.py:628
  92.9 0.8 loss.1
  (52 shorter events, 0.3 us)
Async XLA Ops:
  0.6 20.7 %copy-start.11 = (bf16[32,128]{1,0:T(8,128)(2,1)S(1)}, bf16[32,128]{1,0:T(8,128)(2,1)}, u32[]{:S(2)}) copy-start(bf16[32,128]{1,0:T(8,128)(2,1)} %param.18) | copy-start | bytes 24580
  0.7 28.1 %copy-start.8 = (bf16[9,512,512]{2,1,0:T(8,128)(2,1)S(1)}, bf16[9,512,512]{2,1,0:T(8,128)(2,1)}, u32[]{:S(2)}) copy-start(bf16[9,512,512]{2,1,0:T(8,128)(2,1)} %w_ref.4) | copy-start | bytes 14155780
  0.7 28.1 %copy-start.9 = (f32[512]{0:T(512)S(1)}, f32[512]{0:T(512)}, u32[]{:S(2)}) copy-start(f32[512]{0:T(512)} %param.21) | copy-start | bytes 6148
  0.7 28.1 %copy-start.10 = (f32[512]{0:T(512)S(1)}, f32[512]{0:T(512)}, u32[]{:S(2)}) copy-start(f32[512]{0:T(512)} %param.22) | copy-start | bytes 6148
  6.7 1.3 %collective-permute-start = (f32[32,512]{1,0:T(8,128)S(1)}, f32[32,512]{1,0:T(8,128)S(1)}, u32[]{:S(2)}, u32[]{:S(2)}) collective-permute-start(f32[32,512]{1,0:T(8,128)S(1)} %get-tuple-element.53), channel_id=1, source_target_pairs={{0,1},{1,0},{2,3},{3,2},{4,5},{5,4},{6,7},{7,6},{8,9},{9,8},{10,11... | collective-permute-start | bytes 196616 | tf_op jit(solution)/shard_map/ppermute | solution.py:543
  8.0 6.6 %collective-permute-start.3 = (f32[32,512]{1,0:T(8,128)S(1)}, f32[32,512]{1,0:T(8,128)S(1)}, u32[]{:S(2)}, u32[]{:S(2)}) collective-permute-start(f32[32,512]{1,0:T(8,128)S(1)} %add.83), channel_id=1, source_target_pairs={{0,6},{1,25},{2,26},{3,5},{4,28},{5,3},{6,0},{7,31},{8,16},{9,15},... | collective-permute-start | bytes 196616 | tf_op jit(solution)/shard_map/ppermute | solution.py:548
  12.3 5.2 %collective-permute-start.2 = (f32[32,512]{1,0:T(8,128)S(1)}, f32[32,512]{1,0:T(8,128)S(1)}, u32[]{:S(2)}, u32[]{:S(2)}) collective-permute-start(f32[32,512]{1,0:T(8,128)S(1)} %add.83), channel_id=1, source_target_pairs={{0,5},{1,16},{2,19},{3,6},{4,21},{5,0},{6,3},{7,22},{8,25},{9,12},... | collective-permute-start | bytes 196616 | tf_op jit(solution)/shard_map/ppermute | solution.py:548
  12.3 5.2 %collective-permute-start.1 = (f32[32,512]{1,0:T(8,128)S(1)}, f32[32,512]{1,0:T(8,128)S(1)}, u32[]{:S(2)}, u32[]{:S(2)}) collective-permute-start(f32[32,512]{1,0:T(8,128)S(1)} %add.83), channel_id=1, source_target_pairs={{0,3},{1,8},{2,11},{3,0},{4,13},{5,6},{6,5},{7,14},{8,1},{9,10},{1... | collective-permute-start | bytes 196616 | tf_op jit(solution)/shard_map/ppermute | solution.py:548
  17.5 5.6 %collective-permute-start.6 = (f32[32,512]{1,0:T(8,128)S(1)}, f32[32,512]{1,0:T(8,128)S(1)}, u32[]{:S(2)}, u32[]{:S(2)}) collective-permute-start(f32[32,512]{1,0:T(8,128)S(1)} %add_add_fusion.5), channel_id=1, source_target_pairs={{0,24},{1,7},{2,4},{3,27},{4,2},{5,29},{6,30},{7,1},{8,14},{9,17},... | collective-permute-start | bytes 196616 | tf_op jit(solution)/shard_map/ppermute | solution.py:548
  20.3 5.2 %collective-permute-start.5 = (f32[32,512]{1,0:T(8,128)S(1)}, f32[32,512]{1,0:T(8,128)S(1)}, u32[]{:S(2)}, u32[]{:S(2)}) collective-permute-start(f32[32,512]{1,0:T(8,128)S(1)} %add_add_fusion.5), channel_id=1, source_target_pairs={{0,17},{1,4},{2,7},{3,18},{4,1},{5,20},{6,23},{7,2},{8,13},{9,24},... | collective-permute-start | bytes 196616 | tf_op jit(solution)/shard_map/ppermute | solution.py:548
  20.3 5.2 %collective-permute-start.4 = (f32[32,512]{1,0:T(8,128)S(1)}, f32[32,512]{1,0:T(8,128)S(1)}, u32[]{:S(2)}, u32[]{:S(2)}) collective-permute-start(f32[32,512]{1,0:T(8,128)S(1)} %add_add_fusion.5), channel_id=1, source_target_pairs={{0,9},{1,2},{2,1},{3,10},{4,7},{5,12},{6,15},{7,4},{8,11},{9,0},{1... | collective-permute-start | bytes 196616 | tf_op jit(solution)/shard_map/ppermute | solution.py:548
  21.4 4.3 %collective-permute-start.12 = (bf16[32,128]{1,0:T(8,128)(2,1)S(1)}, bf16[32,128]{1,0:T(8,128)(2,1)S(1)}, u32[]{:S(2)}, u32[]{:S(2)}) collective-permute-start(bf16[32,128]{1,0:T(8,128)(2,1)S(1)} %copy-done.11), channel_id=1, source_target_pairs={{0,32},{32,0},{64,96},{96,64},{1,33},{33,1},{65,97},{97,65},{2,34}... | collective-permute-start | bytes 24584 | tf_op jit(solution)/shard_map/ppermute | solution.py:539
  25.6 3.2 %collective-permute-start.7 = (f32[32,512]{1,0:T(8,128)S(1)}, f32[32,512]{1,0:T(8,128)S(1)}, u32[]{:S(2)}, u32[]{:S(2)}) collective-permute-start(f32[32,512]{1,0:T(8,128)S(1)} %add_add_fusion.4.mine_ref), channel_id=1, source_target_pairs={{0,1},{1,0},{2,3},{3,2},{4,5},{5,4},{6,7},{7,6},{8,9},{9,8},{10,11... | collective-permute-start | bytes 196616 | tf_op jit(solution)/shard_map/ppermute | solution.py:553
  25.7 11.5 %collective-permute-start.13 = (bf16[64,128]{1,0:T(8,128)(2,1)S(1)}, bf16[64,128]{1,0:T(8,128)(2,1)S(1)}, u32[]{:S(2)}, u32[]{:S(2)}) collective-permute-start(bf16[64,128]{1,0:T(8,128)(2,1)S(1)} %pad_maximum_fusion.1), channel_id=1, source_target_pairs={{0,96},{32,64},{64,32},{96,0},{1,97},{33,65},{65,33},{97,1},{2,98}... | collective-permute-start | bytes 49160 | tf_op jit(solution)/shard_map/ppermute | solution.py:539
  28.8 13.6 %copy-start.1 = (bf16[512,2048]{1,0:T(8,128)(2,1)S(1)}, bf16[512,2048]{1,0:T(8,128)(2,1)}, u32[]{:S(2)}) copy-start(bf16[512,2048]{1,0:T(8,128)(2,1)} %w_ref.7) | copy-start | bytes 6291460
  28.8 13.6 %copy-start.5 = (f32[512]{0:T(512)S(1)}, f32[512]{0:T(512)}, u32[]{:S(2)}) copy-start(f32[512]{0:T(512)} %param.24) | copy-start | bytes 6148
  28.8 13.6 %copy-start.6 = (f32[512]{0:T(512)S(1)}, f32[512]{0:T(512)}, u32[]{:S(2)}) copy-start(f32[512]{0:T(512)} %param.25) | copy-start | bytes 6148
  28.8 14.0 %copy-start = (bf16[16384,128]{1,0:T(8,128)(2,1)S(1)}, bf16[16384,128]{1,0:T(8,128)(2,1)}, u32[]{:S(2)}) copy-start(bf16[16384,128]{1,0:T(8,128)(2,1)} %k_ref.3) | copy-start | bytes 12582916
  37.0 1.3 %collective-permute-start.8 = (f32[32,512]{1,0:T(8,128)S(1)}, f32[32,512]{1,0:T(8,128)S(1)}, u32[]{:S(2)}, u32[]{:S(2)}) collective-permute-start(f32[32,512]{1,0:T(8,128)S(1)} %get-tuple-element.64), channel_id=1, source_target_pairs={{0,1},{1,0},{2,3},{3,2},{4,5},{5,4},{6,7},{7,6},{8,9},{9,8},{10,11... | collective-permute-start | bytes 196616 | tf_op jit(solution)/shard_map/ppermute | solution.py:543
  38.3 6.4 %collective-permute-start.11 = (f32[32,512]{1,0:T(8,128)S(1)}, f32[32,512]{1,0:T(8,128)S(1)}, u32[]{:S(2)}, u32[]{:S(2)}) collective-permute-start(f32[32,512]{1,0:T(8,128)S(1)} %add.90), channel_id=1, source_target_pairs={{0,6},{1,25},{2,26},{3,5},{4,28},{5,3},{6,0},{7,31},{8,16},{9,15},... | collective-permute-start | bytes 196616 | tf_op jit(solution)/shard_map/ppermute | solution.py:548
  39.7 5.2 %collective-permute-start.10 = (f32[32,512]{1,0:T(8,128)S(1)}, f32[32,512]{1,0:T(8,128)S(1)}, u32[]{:S(2)}, u32[]{:S(2)}) collective-permute-start(f32[32,512]{1,0:T(8,128)S(1)} %add.90), channel_id=1, source_target_pairs={{0,5},{1,16},{2,19},{3,6},{4,21},{5,0},{6,3},{7,22},{8,25},{9,12},... | collective-permute-start | bytes 196616 | tf_op jit(solution)/shard_map/ppermute | solution.py:548
  40.1 4.7 %collective-permute-start.9 = (f32[32,512]{1,0:T(8,128)S(1)}, f32[32,512]{1,0:T(8,128)S(1)}, u32[]{:S(2)}, u32[]{:S(2)}) collective-permute-start(f32[32,512]{1,0:T(8,128)S(1)} %add.90), channel_id=1, source_target_pairs={{0,3},{1,8},{2,11},{3,0},{4,13},{5,6},{6,5},{7,14},{8,1},{9,10},{1... | collective-permute-start | bytes 196616 | tf_op jit(solution)/shard_map/ppermute | solution.py:548
  44.9 5.7 %collective-permute-start.16 = (f32[32,512]{1,0:T(8,128)S(1)}, f32[32,512]{1,0:T(8,128)S(1)}, u32[]{:S(2)}, u32[]{:S(2)}) collective-permute-start(f32[32,512]{1,0:T(8,128)S(1)} %add_add_fusion.3), channel_id=1, source_target_pairs={{0,24},{1,7},{2,4},{3,27},{4,2},{5,29},{6,30},{7,1},{8,14},{9,17},... | collective-permute-start | bytes 196616 | tf_op jit(solution)/shard_map/ppermute | solution.py:548
  47.0 5.2 %collective-permute-start.15 = (f32[32,512]{1,0:T(8,128)S(1)}, f32[32,512]{1,0:T(8,128)S(1)}, u32[]{:S(2)}, u32[]{:S(2)}) collective-permute-start(f32[32,512]{1,0:T(8,128)S(1)} %add_add_fusion.3), channel_id=1, source_target_pairs={{0,17},{1,4},{2,7},{3,18},{4,1},{5,20},{6,23},{7,2},{8,13},{9,24},... | collective-permute-start | bytes 196616 | tf_op jit(solution)/shard_map/ppermute | solution.py:548
  47.2 5.0 %collective-permute-start.14 = (f32[32,512]{1,0:T(8,128)S(1)}, f32[32,512]{1,0:T(8,128)S(1)}, u32[]{:S(2)}, u32[]{:S(2)}) collective-permute-start(f32[32,512]{1,0:T(8,128)S(1)} %add_add_fusion.3), channel_id=1, source_target_pairs={{0,9},{1,2},{2,1},{3,10},{4,7},{5,12},{6,15},{7,4},{8,11},{9,0},{1... | collective-permute-start | bytes 196616 | tf_op jit(solution)/shard_map/ppermute | solution.py:548
  52.2 1.5 %collective-permute-start.17 = (f32[32,512]{1,0:T(8,128)S(1)}, f32[32,512]{1,0:T(8,128)S(1)}, u32[]{:S(2)}, u32[]{:S(2)}) collective-permute-start(f32[32,512]{1,0:T(8,128)S(1)} %add_add_fusion.2.mine_ref), channel_id=1, source_target_pairs={{0,1},{1,0},{2,3},{3,2},{4,5},{5,4},{6,7},{7,6},{8,9},{9,8},{10,11... | collective-permute-start | bytes 196616 | tf_op jit(solution)/shard_map/ppermute | solution.py:553
  53.8 21.4 %copy-start.2 = (bf16[2048,128]{1,0:T(8,128)(2,1)S(1)}, bf16[2048,128]{1,0:T(8,128)(2,1)}, u32[]{:S(2)}) copy-start(bf16[2048,128]{1,0:T(8,128)(2,1)} %proj_ref.1) | copy-start | bytes 1572868
  53.8 21.4 %copy-start.3 = (f32[2048]{0:T(1024)S(1)}, f32[2048]{0:T(1024)}, u32[]{:S(2)}) copy-start(f32[2048]{0:T(1024)} %param.27) | copy-start | bytes 24580
  53.8 21.4 %copy-start.4 = (f32[2048]{0:T(1024)S(1)}, f32[2048]{0:T(1024)}, u32[]{:S(2)}) copy-start(f32[2048]{0:T(1024)} %param.28) | copy-start | bytes 24580
  57.7 1.5 %collective-permute-start.18 = (f32[32,1280]{1,0:T(8,128)S(1)}, f32[32,1280]{1,0:T(8,128)S(1)}, u32[]{:S(2)}, u32[]{:S(2)}) collective-permute-start(f32[32,1280]{1,0:T(8,128)S(1)} %get-tuple-element.89), channel_id=1, source_target_pairs={{0,1},{1,0},{2,3},{3,2},{4,5},{5,4},{6,7},{7,6},{8,9},{9,8},{10,11... | collective-permute-start | bytes 491528 | tf_op jit(solution)/shard_map/ppermute | solution.py:543
  59.2 5.7 %collective-permute-start.21 = (bf16[32,1280]{1,0:T(8,128)(2,1)S(1)}, bf16[32,1280]{1,0:T(8,128)(2,1)S(1)}, u32[]{:S(2)}, u32[]{:S(2)}) collective-permute-start(bf16[32,1280]{1,0:T(8,128)(2,1)S(1)} %get-tuple-element.102), channel_id=1, source_target_pairs={{0,6},{1,25},{2,26},{3,5},{4,28},{5,3},{6,0},{7,31},{8,16},{9,15},... | collective-permute-start | bytes 245768 | tf_op jit(solution)/shard_map/ppermute | solution.py:548
  61.2 5.4 %collective-permute-start.20 = (bf16[32,1280]{1,0:T(8,128)(2,1)S(1)}, bf16[32,1280]{1,0:T(8,128)(2,1)S(1)}, u32[]{:S(2)}, u32[]{:S(2)}) collective-permute-start(bf16[32,1280]{1,0:T(8,128)(2,1)S(1)} %get-tuple-element.102), channel_id=1, source_target_pairs={{0,5},{1,16},{2,19},{3,6},{4,21},{5,0},{6,3},{7,22},{8,25},{9,12},... | collective-permute-start | bytes 245768 | tf_op jit(solution)/shard_map/ppermute | solution.py:548
  61.8 4.8 %collective-permute-start.19 = (bf16[32,1280]{1,0:T(8,128)(2,1)S(1)}, bf16[32,1280]{1,0:T(8,128)(2,1)S(1)}, u32[]{:S(2)}, u32[]{:S(2)}) collective-permute-start(bf16[32,1280]{1,0:T(8,128)(2,1)S(1)} %get-tuple-element.102), channel_id=1, source_target_pairs={{0,3},{1,8},{2,11},{3,0},{4,13},{5,6},{6,5},{7,14},{8,1},{9,10},{1... | collective-permute-start | bytes 245768 | tf_op jit(solution)/shard_map/ppermute | solution.py:548
  66.7 5.7 %collective-permute-start.24 = (bf16[32,1280]{1,0:T(8,128)(2,1)S(1)}, bf16[32,1280]{1,0:T(8,128)(2,1)S(1)}, u32[]{:S(2)}, u32[]{:S(2)}) collective-permute-start(bf16[32,1280]{1,0:T(8,128)(2,1)S(1)} %get-tuple-element.100), channel_id=1, source_target_pairs={{0,24},{1,7},{2,4},{3,27},{4,2},{5,29},{6,30},{7,1},{8,14},{9,17},... | collective-permute-start | bytes 245768 | tf_op jit(solution)/shard_map/ppermute | solution.py:548
  68.0 5.4 %collective-permute-start.23 = (bf16[32,1280]{1,0:T(8,128)(2,1)S(1)}, bf16[32,1280]{1,0:T(8,128)(2,1)S(1)}, u32[]{:S(2)}, u32[]{:S(2)}) collective-permute-start(bf16[32,1280]{1,0:T(8,128)(2,1)S(1)} %get-tuple-element.100), channel_id=1, source_target_pairs={{0,17},{1,4},{2,7},{3,18},{4,1},{5,20},{6,23},{7,2},{8,13},{9,24},... | collective-permute-start | bytes 245768 | tf_op jit(solution)/shard_map/ppermute | solution.py:548
  68.5 5.0 %collective-permute-start.22 = (bf16[32,1280]{1,0:T(8,128)(2,1)S(1)}, bf16[32,1280]{1,0:T(8,128)(2,1)S(1)}, u32[]{:S(2)}, u32[]{:S(2)}) collective-permute-start(bf16[32,1280]{1,0:T(8,128)(2,1)S(1)} %get-tuple-element.100), channel_id=1, source_target_pairs={{0,9},{1,2},{2,1},{3,10},{4,7},{5,12},{6,15},{7,4},{8,11},{9,0},{1... | collective-permute-start | bytes 245768 | tf_op jit(solution)/shard_map/ppermute | solution.py:548
  73.7 1.5 %collective-permute-start.25 = (f32[32,1280]{1,0:T(8,128)S(1)}, f32[32,1280]{1,0:T(8,128)S(1)}, u32[]{:S(2)}, u32[]{:S(2)}) collective-permute-start(f32[32,1280]{1,0:T(8,128)S(1)} %add_add_fusion.mine_ref), channel_id=1, source_target_pairs={{0,1},{1,0},{2,3},{3,2},{4,5},{5,4},{6,7},{7,6},{8,9},{9,8},{10,11... | collective-permute-start | bytes 491528 | tf_op jit(solution)/shard_map/ppermute | solution.py:553
  73.8 10.2 %collective-permute-start.26 = (f32[1,64]{1,0:T(1,128)S(1)}, f32[1,64]{1,0:T(1,128)S(1)}, u32[]{:S(2)}, u32[]{:S(2)}) collective-permute-start(f32[1,64]{1,0:T(1,128)S(1)} %slice.17), channel_id=1, source_target_pairs={{0,96},{32,64},{64,32},{96,0},{1,97},{33,65},{65,33},{97,1},{2,98}... | collective-permute-start | bytes 776 | tf_op jit(solution)/shard_map/ppermute | solution.py:539
  75.1 17.8 %copy-start.7 = (s32[32]{0:T(128)S(1)}, s32[32]{0:T(128)}, u32[]{:S(2)}) copy-start(s32[32]{0:T(128)} %param.17) | copy-start | bytes 388
  79.4 13.5 %all-to-all-start = ((bf16[32,32,128]{2,1,0:T(8,128)(2,1)}), bf16[32,32,128]{2,1,0:T(8,128)(2,1)S(1)}, u32[]{:S(2)}, u32[]{:S(2)}) async-start(bf16[32,32,128]{2,1,0:T(8,128)(2,1)} %get-tuple-element.96), calls=%async_computation | async-start | bytes 524288 | tf_op jit(solution)/shard_map/all_to_all | solution.py:628
  84.1 3.6 %collective-permute-start.27 = (f32[1,32]{1,0:T(1,128)S(1)}, f32[1,32]{1,0:T(1,128)S(1)}, u32[]{:S(2)}, u32[]{:S(2)}) collective-permute-start(f32[1,32]{1,0:T(1,128)S(1)} %slice.19), channel_id=1, source_target_pairs={{0,32},{32,0},{64,96},{96,64},{1,33},{33,1},{65,97},{97,65},{2,34}... | collective-permute-start | bytes 392 | tf_op jit(solution)/shard_map/ppermute | solution.py:539

commit v3 on v2

--- a/solution.py
+++ b/solution.py
@@ -75,12 +75,14 @@
     x_hbm,
     w_hbm,
     shuffle_hbm,
+    next_hbm,
     y_ref,
     keep_ref,
     send_ref,
     by_set_ref,
     by_image_ref,
     x_ref,
+    next_ref,
     w_ref,
     shuffle_ref,
     sems,
@@ -96,6 +98,8 @@
         part = pl.ds(first, size)
         copies.append(pltpu.make_async_copy(x_hbm.at[part], x_ref.at[part], sems.at[n + 1]))
         copies[-1].start()
+    next_copy = pltpu.make_async_copy(next_hbm, next_ref, sems.at[len(CHUNKS) + 2])
+    next_copy.start()
     shuffle_copy.wait()
     by_set, by_image = set_onehots(me_ref[0], shuffle_ref[...], count)
     by_set_ref[...] = by_set
@@ -114,9 +118,10 @@
     core = core_ref[0]
     split_halves(core, reorder(by_set, s1), keep_ref, send_ref, 0)
     split_halves(core, reorder(by_set, s2), keep_ref, send_ref, mid // 2)
-
-
-def reduce_stage(me, core, x, weight, shuffle):
+    next_copy.wait()
+
+
+def reduce_stage(me, core, x, weight, shuffle, later):
     places, count, channels = x.shape
     mid = weight.shape[1]
     sets = shuffle.shape[1] // count
@@ -124,8 +129,8 @@
     return pl.pallas_call(
         reduce_kernel,
         name="reduce",
-        in_specs=[SMEM, SMEM, hbm, hbm, hbm],
-        out_specs=[VMEM] * 6,
+        in_specs=[SMEM, SMEM, hbm, hbm, hbm, hbm],
+        out_specs=[VMEM] * 7,
         out_shape=[
             jax.ShapeDtypeStruct((places, count, mid), F32),
             jax.ShapeDtypeStruct((count, mid), F32),
@@ -133,11 +138,12 @@
             jax.ShapeDtypeStruct((sets, 3 * count), BF16),
             jax.ShapeDtypeStruct((count, 3 * sets), BF16),
             jax.ShapeDtypeStruct(x.shape, x.dtype),
+            jax.ShapeDtypeStruct(later.shape, later.dtype),
         ],
         scratch_shapes=[
             pltpu.VMEM(weight.shape, weight.dtype),
             pltpu.VMEM(shuffle.shape, shuffle.dtype),
-            pltpu.SemaphoreType.DMA((len(CHUNKS) + 2,)),
+            pltpu.SemaphoreType.DMA((len(CHUNKS) + 3,)),
         ],
         compiler_params=pltpu.CompilerParams(vmem_limit_bytes=24 * 1024 * 1024),
         cost_estimate=pl.CostEstimate(
@@ -145,7 +151,11 @@
             bytes_accessed=2 * x.size + 4 * places * count * mid,
             transcendentals=0,
         ),
-    )(me, core, *[pltpu.with_memory_space_constraint(v, pltpu.HBM) for v in (x, weight, shuffle)])
+    )(
+        me,
+        core,
+        *[pltpu.with_memory_space_constraint(v, pltpu.HBM) for v in (x, weight, shuffle, later)],
+    )
 
 
 def scale_shift(core, mine, other, onehot, gain, shift, rows):
@@ -593,7 +603,9 @@
         return None, None
 
     first = queue_swap(queries, 1)
-    y, keep, send, by_set, by_image, x = reduce_stage(me.reshape(1), core, x, reduce_weight, shuffle)
+    y, keep, send, by_set, by_image, x, w_spatial = reduce_stage(
+        me.reshape(1), core, x, reduce_weight, shuffle, w_spatial
+    )
     pair = jnp.concatenate([queries, first], 0)
     mine, other, _ = reduce_sets(keep, send, (nothing, nothing), None, F32)
     asked = jnp.concatenate([pair, queue_swap(pair, 3)], 0)

time: 95.1 us -> 95 us (level)
  no operation moved by 1% of the time
where the time goes in v3:
time: 95 us; the launch traced here: 93.6 us
  starting transfers between devices  35.7 us (38%)
  waiting for transfers between devices  29.2 us (31%)
  Pallas kernels  26.9 us (28%)
  between operations  0.97 us (1%)
    ppermute x18, starting transfers between devices, reduce_sets(): parts.append(lax.ppermute(sent, 'dp', ring_swap(k, turn == 1)).astype(F32))  24.4 us
    ppermute x18, waiting for transfers between devices, reduce_sets(): parts.append(lax.ppermute(sent, 'dp', ring_swap(k, turn == 1)).astype(F32))  15.3 us
    pallas_call x1, Pallas kernels, conv_stage(): pl.pallas_call(functools.partial(conv_kernel, rows), name='conv', grid=(S...  8.12 us
    pallas_call x1, Pallas kernels, reduce_stage(): pl.pallas_call(reduce_kernel, name='reduce', in_specs=[SMEM, SMEM, hbm, h...  5.87 us
    ppermute x4, starting transfers between devices, queue_swap(): return lax.ppermute(values, 'queue', [(i, i ^ k) for i in range(RING)])  5.72 us
    all_to_all x1, waiting for transfers between devices, on_device(): lax.all_to_all(copies, 'dp', split_axis=0, concat_axis=0, tiled=True)  5.22 us
    all_to_all x1, starting transfers between devices, on_device(): lax.all_to_all(copies, 'dp', split_axis=0, concat_axis=0, tiled=True)  4.63 us
    pallas_call x1, Pallas kernels, merge_stage(): pl.pallas_call(functools.partial(merge_kernel, rows), name='merge', in_sp...  4.21 us
  transfers between devices with their start and end apart: 29, of which 18 were waited for; matrix products, arithmetic and copies ran while one was open for 0% of the time, Pallas kernels for 17%

profile of v3, /device:TPU:0, one launch (start us, length us, event | category | flops | bytes accessed | tf_op | source)
XLA Modules:
  0.0 93.6 jit_solution(265399689018327687)
XLA Ops:
  0.7 5.9 %reduce.1 = (f32[49,32,512]{2,1,0:T(8,128)S(1)}, f32[32,512]{1,0:T(8,128)S(1)}, f32[32,512]{1,0:T(8,128)S(1)}, bf16[32,96]{1,0:T(8,128)(2,1)S(1)}, bf16[32,96]{1...) custom-call(s32[1]{0:T(128)} %bitcast.1.me_ref, s32[1]{0:T(128)} %bitcast.core_ref, ...), custom_call_target="tpu_custom_call" | custom-call | flops 3288334336 | bytes 9633792 | tf_op jit(solution)/shard_map/reduce/pallas_call | solution.py:129
  6.6 0.1 collective-permute-start
  6.6 1.2 %collective-permute-done = f32[32,512]{1,0:T(8,128)S(1)} collective-permute-done((f32[32,512]{1,0:T(8,128)S(1)}, f32[32,512]{1,0:T(8,128)S(1)}, u32[]{:S(2)}, u32[]{:S(2)}) %collective-permute-start) | collective-permute-done | bytes 65568 | tf_op jit(solution)/shard_map/ppermute | solution.py:553
  7.9 4.2 %collective-permute-start.3 = (f32[32,512]{1,0:T(8,128)S(1)}, f32[32,512]{1,0:T(8,128)S(1)}, u32[]{:S(2)}, u32[]{:S(2)}) collective-permute-start(f32[32,512]{1,0:T(8,128)S(1)} %add.83), channel_id=1, source_target_pairs={{0,6},{1,25},{2,26},{3,5},{4,28},{5,3},{6,0},{7,31},{8,16},{9,15},... | collective-permute-start | bytes 196616 | tf_op jit(solution)/shard_map/ppermute | solution.py:558
  12.1 0.7 collective-permute-start.1
  12.8 1.7 %collective-permute-done.3 = f32[32,512]{1,0:T(8,128)S(1)} collective-permute-done((f32[32,512]{1,0:T(8,128)S(1)}, f32[32,512]{1,0:T(8,128)S(1)}, u32[]{:S(2)}, u32[]{:S(2)}) %collective-permute-start.3) | collective-permute-done | bytes 65568 | tf_op jit(solution)/shard_map/ppermute | solution.py:558
  14.5 2.9 %collective-permute-done.2 = f32[32,512]{1,0:T(8,128)S(1)} collective-permute-done((f32[32,512]{1,0:T(8,128)S(1)}, f32[32,512]{1,0:T(8,128)S(1)}, u32[]{:S(2)}, u32[]{:S(2)}) %collective-permute-start.2) | collective-permute-done | bytes 65568 | tf_op jit(solution)/shard_map/ppermute | solution.py:558
  17.4 2.8 %collective-permute-start.6 = (f32[32,512]{1,0:T(8,128)S(1)}, f32[32,512]{1,0:T(8,128)S(1)}, u32[]{:S(2)}, u32[]{:S(2)}) collective-permute-start(f32[32,512]{1,0:T(8,128)S(1)} %add_add_fusion.5), channel_id=1, source_target_pairs={{0,24},{1,7},{2,4},{3,27},{4,2},{5,29},{6,30},{7,1},{8,14},{9,17},... | collective-permute-start | bytes 196616 | tf_op jit(solution)/shard_map/ppermute | solution.py:558
  20.2 0.0 collective-permute-start.5
  20.2 1.1 %collective-permute-start.4 = (f32[32,512]{1,0:T(8,128)S(1)}, f32[32,512]{1,0:T(8,128)S(1)}, u32[]{:S(2)}, u32[]{:S(2)}) collective-permute-start(f32[32,512]{1,0:T(8,128)S(1)} %add_add_fusion.5), channel_id=1, source_target_pairs={{0,9},{1,2},{2,1},{3,10},{4,7},{5,12},{6,15},{7,4},{8,11},{9,0},{1... | collective-permute-start | bytes 196616 | tf_op jit(solution)/shard_map/ppermute | solution.py:558
  21.3 1.6 %collective-permute-start.12 = (bf16[32,128]{1,0:T(8,128)(2,1)S(1)}, bf16[32,128]{1,0:T(8,128)(2,1)S(1)}, u32[]{:S(2)}, u32[]{:S(2)}) collective-permute-start(bf16[32,128]{1,0:T(8,128)(2,1)S(1)} %copy-done.10), channel_id=1, source_target_pairs={{0,32},{32,0},{64,96},{96,64},{1,33},{33,1},{65,97},{97,65},{2,34}... | collective-permute-start | bytes 24584 | tf_op jit(solution)/shard_map/ppermute | solution.py:549
  22.8 0.1 collective-permute-done.6
  22.9 2.5 %collective-permute-done.5 = f32[32,512]{1,0:T(8,128)S(1)} collective-permute-done((f32[32,512]{1,0:T(8,128)S(1)}, f32[32,512]{1,0:T(8,128)S(1)}, u32[]{:S(2)}, u32[]{:S(2)}) %collective-permute-start.5) | collective-permute-done | bytes 65568 | tf_op jit(solution)/shard_map/ppermute | solution.py:558
  25.4 0.1 collective-permute-start.7
  25.5 3.1 %collective-permute-start.13 = (bf16[64,128]{1,0:T(8,128)(2,1)S(1)}, bf16[64,128]{1,0:T(8,128)(2,1)S(1)}, u32[]{:S(2)}, u32[]{:S(2)}) collective-permute-start(bf16[64,128]{1,0:T(8,128)(2,1)S(1)} %pad_maximum_fusion.1), channel_id=1, source_target_pairs={{0,96},{32,64},{64,32},{96,0},{1,97},{33,65},{65,33},{97,1},{2,98}... | collective-permute-start | bytes 49160 | tf_op jit(solution)/shard_map/ppermute | solution.py:549
  28.6 0.0 copy-start.1
  28.6 0.0 copy-start.5
  28.7 0.0 copy-start
  28.7 8.1 %conv.1 = (f32[49,32,512]{2,1,0:T(8,128)S(1)}, f32[32,512]{1,0:T(8,128)S(1)}, f32[32,512]{1,0:T(8,128)S(1)}) custom-call(s32[1]{0:T(128)} %bitcast.core_ref, f32[49,32,512]{2,1,0:T(8,128)S(1)} %get-tuple-element.52.y_ref, f32[32,512]{1,0:T(8,128)S(1)} %add_add_fusion.4.mine_ref, f32[32,512]{1,0:T(8,128)S(1)} %collective-permute-done.7.other_ref, ...), custom_call_target="tpu_custom_call" | custom-call | flops 6056574976 | bytes 11141120 | tf_op jit(solution)/shard_map/conv/pallas_call | solution.py:250
  36.8 0.2 collective-permute-start.8
  37.0 1.1 %collective-permute-done.8 = f32[32,512]{1,0:T(8,128)S(1)} collective-permute-done((f32[32,512]{1,0:T(8,128)S(1)}, f32[32,512]{1,0:T(8,128)S(1)}, u32[]{:S(2)}, u32[]{:S(2)}) %collective-permute-start.8) | collective-permute-done | bytes 65568 | tf_op jit(solution)/shard_map/ppermute | solution.py:553
  38.2 1.3 %collective-permute-start.11 = (f32[32,512]{1,0:T(8,128)S(1)}, f32[32,512]{1,0:T(8,128)S(1)}, u32[]{:S(2)}, u32[]{:S(2)}) collective-permute-start(f32[32,512]{1,0:T(8,128)S(1)} %add.90), channel_id=1, source_target_pairs={{0,6},{1,25},{2,26},{3,5},{4,28},{5,3},{6,0},{7,31},{8,16},{9,15},... | collective-permute-start | bytes 196616 | tf_op jit(solution)/shard_map/ppermute | solution.py:558
  39.5 0.5 collective-permute-start.10
  40.0 2.1 %collective-permute-start.9 = (f32[32,512]{1,0:T(8,128)S(1)}, f32[32,512]{1,0:T(8,128)S(1)}, u32[]{:S(2)}, u32[]{:S(2)}) collective-permute-start(f32[32,512]{1,0:T(8,128)S(1)} %add.90), channel_id=1, source_target_pairs={{0,3},{1,8},{2,11},{3,0},{4,13},{5,6},{6,5},{7,14},{8,1},{9,10},{1... | collective-permute-start | bytes 196616 | tf_op jit(solution)/shard_map/ppermute | solution.py:558
  42.1 0.1 fusion
  42.2 0.1 fusion.1.q_ref
  42.3 0.4 center.1
  42.7 1.8 %negative.2 = f32[1,128]{1,0:T(1,128)S(1)} custom-call(bf16[128,128]{1,0:T(8,128)(2,1)S(1)} %fusion.1.q_ref, bf16[16384,128]{1,0:T(8,128)(2,1)S(1)} %copy-done), custom_call_target="tpu_custom_call" | custom-call | flops 268435456 | bytes 2097152 | tf_op jit(solution)/shard_map/negative/pallas_call | solution.py:481
  44.5 0.2 collective-permute-done.10
  44.7 0.0 collective-permute-done.9
  44.7 2.1 %collective-permute-start.16 = (f32[32,512]{1,0:T(8,128)S(1)}, f32[32,512]{1,0:T(8,128)S(1)}, u32[]{:S(2)}, u32[]{:S(2)}) collective-permute-start(f32[32,512]{1,0:T(8,128)S(1)} %add_add_fusion.3), channel_id=1, source_target_pairs={{0,24},{1,7},{2,4},{3,27},{4,2},{5,29},{6,30},{7,1},{8,14},{9,17},... | collective-permute-start | bytes 196616 | tf_op jit(solution)/shard_map/ppermute | solution.py:558
  46.9 0.2 collective-permute-start.15
  47.1 1.5 %collective-permute-start.14 = (f32[32,512]{1,0:T(8,128)S(1)}, f32[32,512]{1,0:T(8,128)S(1)}, u32[]{:S(2)}, u32[]{:S(2)}) collective-permute-start(f32[32,512]{1,0:T(8,128)S(1)} %add_add_fusion.3), channel_id=1, source_target_pairs={{0,9},{1,2},{2,1},{3,10},{4,7},{5,12},{6,15},{7,4},{8,11},{9,0},{1... | collective-permute-start | bytes 196616 | tf_op jit(solution)/shard_map/ppermute | solution.py:558
  48.6 1.8 %negative.3 = f32[1,128]{1,0:T(1,128)S(1)} custom-call(bf16[128,128]{1,0:T(8,128)(2,1)S(1)} %fusion.1.q_ref, bf16[16384,128]{1,0:T(8,128)(2,1)S(1)} %copy-done), custom_call_target="tpu_custom_call" | custom-call | flops 268435456 | bytes 2097152 | tf_op jit(solution)/shard_map/negative/pallas_call | solution.py:481
  50.5 1.6 %collective-permute-done.15 = f32[32,512]{1,0:T(8,128)S(1)} collective-permute-done((f32[32,512]{1,0:T(8,128)S(1)}, f32[32,512]{1,0:T(8,128)S(1)}, u32[]{:S(2)}, u32[]{:S(2)}) %collective-permute-start.15) | collective-permute-done | bytes 65568 | tf_op jit(solution)/shard_map/ppermute | solution.py:558
  52.1 0.3 collective-permute-start.17
  52.4 1.2 %collective-permute-done.17.other_ref = f32[32,512]{1,0:T(8,128)S(1)} collective-permute-done((f32[32,512]{1,0:T(8,128)S(1)}, f32[32,512]{1,0:T(8,128)S(1)}, u32[]{:S(2)}, u32[]{:S(2)}) %collective-permute-start.17) | collective-permute-done | bytes 65568 | tf_op jit(solution)/shard_map/ppermute | solution.py:563
  53.6 3.9 %expand.1 = (f32[49,32,2048]{2,1,0:T(8,128)S(1)}, f32[32,1280]{1,0:T(8,128)S(1)}, f32[32,1280]{1,0:T(8,128)S(1)}) custom-call(s32[1]{0:T(128)} %bitcast.core_ref, f32[49,32,512]{2,1,0:T(8,128)S(1)} %get-tuple-element.64.z_ref, f32[32,512]{1,0:T(8,128)S(1)} %add_add_fusion.2.mine_ref, f32[32,512]{1,0:T(8,128)S(1)} %collective-permute-done.17.other_ref, ...), custom_call_target="tpu_custom_call" | custom-call | flops 3288334336 | bytes 16056320 | tf_op jit(solution)/shard_map/expand/pallas_call | solution.py:362
  57.5 0.2 collective-permute-start.18
  57.7 1.2 %collective-permute-done.18 = f32[32,1280]{1,0:T(8,128)S(1)} collective-permute-done((f32[32,1280]{1,0:T(8,128)S(1)}, f32[32,1280]{1,0:T(8,128)S(1)}, u32[]{:S(2)}, u32[]{:S(2)}) %collective-permute-start.18) | collective-permute-done | bytes 163872 | tf_op jit(solution)/shard_map/ppermute | solution.py:553
  59.0 2.1 %collective-permute-start.21 = (bf16[32,1280]{1,0:T(8,128)(2,1)S(1)}, bf16[32,1280]{1,0:T(8,128)(2,1)S(1)}, u32[]{:S(2)}, u32[]{:S(2)}) collective-permute-start(bf16[32,1280]{1,0:T(8,128)(2,1)S(1)} %get-tuple-element.104), channel_id=1, source_target_pairs={{0,6},{1,25},{2,26},{3,5},{4,28},{5,3},{6,0},{7,31},{8,16},{9,15},... | collective-permute-start | bytes 245768 | tf_op jit(solution)/shard_map/ppermute | solution.py:558
  61.1 0.6 collective-permute-start.20
  61.6 1.3 %collective-permute-start.19 = (bf16[32,1280]{1,0:T(8,128)(2,1)S(1)}, bf16[32,1280]{1,0:T(8,128)(2,1)S(1)}, u32[]{:S(2)}, u32[]{:S(2)}) collective-permute-start(bf16[32,1280]{1,0:T(8,128)(2,1)S(1)} %get-tuple-element.104), channel_id=1, source_target_pairs={{0,3},{1,8},{2,11},{3,0},{4,13},{5,6},{6,5},{7,14},{8,1},{9,10},{1... | collective-permute-start | bytes 245768 | tf_op jit(solution)/shard_map/ppermute | solution.py:558
  62.9 1.8 %collective-permute-done.21 = bf16[32,1280]{1,0:T(8,128)(2,1)S(1)} collective-permute-done((bf16[32,1280]{1,0:T(8,128)(2,1)S(1)}, bf16[32,1280]{1,0:T(8,128)(2,1)S(1)}, u32[]{:S(2)}, u32[]{:S(2)}) %collective-permute-start.21) | collective-permute-done | bytes 81952 | tf_op jit(solution)/shard_map/ppermute | solution.py:558
  64.8 1.7 %collective-permute-done.20 = bf16[32,1280]{1,0:T(8,128)(2,1)S(1)} collective-permute-done((bf16[32,1280]{1,0:T(8,128)(2,1)S(1)}, bf16[32,1280]{1,0:T(8,128)(2,1)S(1)}, u32[]{:S(2)}, u32[]{:S(2)}) %collective-permute-start.20) | collective-permute-done | bytes 81952 | tf_op jit(solution)/shard_map/ppermute | solution.py:558
  66.5 0.1 fusion.2
  66.5 1.3 %collective-permute-start.24 = (bf16[32,1280]{1,0:T(8,128)(2,1)S(1)}, bf16[32,1280]{1,0:T(8,128)(2,1)S(1)}, u32[]{:S(2)}, u32[]{:S(2)}) collective-permute-start(bf16[32,1280]{1,0:T(8,128)(2,1)S(1)} %get-tuple-element.102), channel_id=1, source_target_pairs={{0,24},{1,7},{2,4},{3,27},{4,2},{5,29},{6,30},{7,1},{8,14},{9,17},... | collective-permute-start | bytes 245768 | tf_op jit(solution)/shard_map/ppermute | solution.py:558
  67.9 0.5 collective-permute-start.23
  68.4 2.1 %collective-permute-start.22 = (bf16[32,1280]{1,0:T(8,128)(2,1)S(1)}, bf16[32,1280]{1,0:T(8,128)(2,1)S(1)}, u32[]{:S(2)}, u32[]{:S(2)}) collective-permute-start(bf16[32,1280]{1,0:T(8,128)(2,1)S(1)} %get-tuple-element.102), channel_id=1, source_target_pairs={{0,9},{1,2},{2,1},{3,10},{4,7},{5,12},{6,15},{7,4},{8,11},{9,0},{1... | collective-permute-start | bytes 245768 | tf_op jit(solution)/shard_map/ppermute | solution.py:558
  70.4 1.8 %collective-permute-done.24 = bf16[32,1280]{1,0:T(8,128)(2,1)S(1)} collective-permute-done((bf16[32,1280]{1,0:T(8,128)(2,1)S(1)}, bf16[32,1280]{1,0:T(8,128)(2,1)S(1)}, u32[]{:S(2)}, u32[]{:S(2)}) %collective-permute-start.24) | collective-permute-done | bytes 81952 | tf_op jit(solution)/shard_map/ppermute | solution.py:558
  72.3 1.0 %collective-permute-done.23 = bf16[32,1280]{1,0:T(8,128)(2,1)S(1)} collective-permute-done((bf16[32,1280]{1,0:T(8,128)(2,1)S(1)}, bf16[32,1280]{1,0:T(8,128)(2,1)S(1)}, u32[]{:S(2)}, u32[]{:S(2)}) %collective-permute-start.23) | collective-permute-done | bytes 81952 | tf_op jit(solution)/shard_map/ppermute | solution.py:558
  73.3 0.2 collective-permute-done.22
  73.4 0.1 add_add_fusion.mine_ref
  73.5 0.1 collective-permute-start.25
  73.6 0.1 slice.17
  73.7 0.9 collective-permute-start.26
  74.6 0.4 collective-permute-done.25.other_ref
  75.0 4.2 %merge.1 = (bf16[32,128]{1,0:T(8,128)(2,1)}, bf16[32,32,128]{2,1,0:T(8,128)(2,1)}) custom-call(s32[1]{0:T(128)} %bitcast.core_ref, f32[49,32,2048]{2,1,0:T(8,128)S(1)} %get-tuple-element.88.e_ref, bf16[49,32,2048]{2,1,0:T(8,128)(2,1)S(1)} %get-tuple-element.89.x_ref, f32[32,1280]{1,0:T(8,128)S(1)} %add_add_fusion.mine_ref, ...), custom_call_target="tpu_custom_call" | custom-call | flops 25690112 | bytes 19267584 | tf_op jit(solution)/shard_map/merge/pallas_call | solution.py:439
  79.2 4.6 %all-to-all-start = ((bf16[32,32,128]{2,1,0:T(8,128)(2,1)}), bf16[32,32,128]{2,1,0:T(8,128)(2,1)S(1)}, u32[]{:S(2)}, u32[]{:S(2)}) async-start(bf16[32,32,128]{2,1,0:T(8,128)(2,1)} %get-tuple-element.98), calls=%async_computation | async-start | bytes 524288 | tf_op jit(solution)/shard_map/all_to_all | solution.py:640
  83.9 0.1 slice.19
  83.9 0.1 collective-permute-start.27
  84.1 3.4 %collective-permute-done.27 = f32[1,32]{1,0:T(1,128)S(1)} collective-permute-done((f32[1,32]{1,0:T(1,128)S(1)}, f32[1,32]{1,0:T(1,128)S(1)}, u32[]{:S(2)}, u32[]{:S(2)}) %collective-permute-start.27) | collective-permute-done | bytes 160 | tf_op jit(solution)/shard_map/ppermute | solution.py:549
  87.5 5.2 %all-to-all-done = bf16[32,32,128]{2,1,0:T(8,128)(2,1)S(1)} async-done(((bf16[32,32,128]{2,1,0:T(8,128)(2,1)}), bf16[32,32,128]{2,1,0:T(8,128)(2,1)S(1)}, u32[]{:S(2)}, u32[]{:S(2)}) %all-to-all-start) | async-done | bytes 262176 | tf_op jit(solution)/shard_map/all_to_all | solution.py:640
  92.8 0.8 loss.1
  (50 shorter events, 0.3 us)
Async XLA Ops:
  0.6 20.6 %copy-start.10 = (bf16[32,128]{1,0:T(8,128)(2,1)S(1)}, bf16[32,128]{1,0:T(8,128)(2,1)}, u32[]{:S(2)}) copy-start(bf16[32,128]{1,0:T(8,128)(2,1)} %param.18) | copy-start | bytes 24580
  0.7 28.0 %copy-start.8 = (f32[512]{0:T(512)S(1)}, f32[512]{0:T(512)}, u32[]{:S(2)}) copy-start(f32[512]{0:T(512)} %param.21) | copy-start | bytes 6148
  0.7 28.0 %copy-start.9 = (f32[512]{0:T(512)S(1)}, f32[512]{0:T(512)}, u32[]{:S(2)}) copy-start(f32[512]{0:T(512)} %param.22) | copy-start | bytes 6148
  6.6 1.3 %collective-permute-start = (f32[32,512]{1,0:T(8,128)S(1)}, f32[32,512]{1,0:T(8,128)S(1)}, u32[]{:S(2)}, u32[]{:S(2)}) collective-permute-start(f32[32,512]{1,0:T(8,128)S(1)} %get-tuple-element.54), channel_id=1, source_target_pairs={{0,1},{1,0},{2,3},{3,2},{4,5},{5,4},{6,7},{7,6},{8,9},{9,8},{10,11... | collective-permute-start | bytes 196616 | tf_op jit(solution)/shard_map/ppermute | solution.py:553
  7.9 6.6 %collective-permute-start.3 = (f32[32,512]{1,0:T(8,128)S(1)}, f32[32,512]{1,0:T(8,128)S(1)}, u32[]{:S(2)}, u32[]{:S(2)}) collective-permute-start(f32[32,512]{1,0:T(8,128)S(1)} %add.83), channel_id=1, source_target_pairs={{0,6},{1,25},{2,26},{3,5},{4,28},{5,3},{6,0},{7,31},{8,16},{9,15},... | collective-permute-start | bytes 196616 | tf_op jit(solution)/shard_map/ppermute | solution.py:558
  12.1 5.2 %collective-permute-start.2 = (f32[32,512]{1,0:T(8,128)S(1)}, f32[32,512]{1,0:T(8,128)S(1)}, u32[]{:S(2)}, u32[]{:S(2)}) collective-permute-start(f32[32,512]{1,0:T(8,128)S(1)} %add.83), channel_id=1, source_target_pairs={{0,5},{1,16},{2,19},{3,6},{4,21},{5,0},{6,3},{7,22},{8,25},{9,12},... | collective-permute-start | bytes 196616 | tf_op jit(solution)/shard_map/ppermute | solution.py:558
  12.1 5.2 %collective-permute-start.1 = (f32[32,512]{1,0:T(8,128)S(1)}, f32[32,512]{1,0:T(8,128)S(1)}, u32[]{:S(2)}, u32[]{:S(2)}) collective-permute-start(f32[32,512]{1,0:T(8,128)S(1)} %add.83), channel_id=1, source_target_pairs={{0,3},{1,8},{2,11},{3,0},{4,13},{5,6},{6,5},{7,14},{8,1},{9,10},{1... | collective-permute-start | bytes 196616 | tf_op jit(solution)/shard_map/ppermute | solution.py:558
  17.4 5.6 %collective-permute-start.6 = (f32[32,512]{1,0:T(8,128)S(1)}, f32[32,512]{1,0:T(8,128)S(1)}, u32[]{:S(2)}, u32[]{:S(2)}) collective-permute-start(f32[32,512]{1,0:T(8,128)S(1)} %add_add_fusion.5), channel_id=1, source_target_pairs={{0,24},{1,7},{2,4},{3,27},{4,2},{5,29},{6,30},{7,1},{8,14},{9,17},... | collective-permute-start | bytes 196616 | tf_op jit(solution)/shard_map/ppermute | solution.py:558
  20.2 5.2 %collective-permute-start.5 = (f32[32,512]{1,0:T(8,128)S(1)}, f32[32,512]{1,0:T(8,128)S(1)}, u32[]{:S(2)}, u32[]{:S(2)}) collective-permute-start(f32[32,512]{1,0:T(8,128)S(1)} %add_add_fusion.5), channel_id=1, source_target_pairs={{0,17},{1,4},{2,7},{3,18},{4,1},{5,20},{6,23},{7,2},{8,13},{9,24},... | collective-permute-start | bytes 196616 | tf_op jit(solution)/shard_map/ppermute | solution.py:558
  20.2 5.2 %collective-permute-start.4 = (f32[32,512]{1,0:T(8,128)S(1)}, f32[32,512]{1,0:T(8,128)S(1)}, u32[]{:S(2)}, u32[]{:S(2)}) collective-permute-start(f32[32,512]{1,0:T(8,128)S(1)} %add_add_fusion.5), channel_id=1, source_target_pairs={{0,9},{1,2},{2,1},{3,10},{4,7},{5,12},{6,15},{7,4},{8,11},{9,0},{1... | collective-permute-start | bytes 196616 | tf_op jit(solution)/shard_map/ppermute | solution.py:558
  21.3 4.3 %collective-permute-start.12 = (bf16[32,128]{1,0:T(8,128)(2,1)S(1)}, bf16[32,128]{1,0:T(8,128)(2,1)S(1)}, u32[]{:S(2)}, u32[]{:S(2)}) collective-permute-start(bf16[32,128]{1,0:T(8,128)(2,1)S(1)} %copy-done.10), channel_id=1, source_target_pairs={{0,32},{32,0},{64,96},{96,64},{1,33},{33,1},{65,97},{97,65},{2,34}... | collective-permute-start | bytes 24584 | tf_op jit(solution)/shard_map/ppermute | solution.py:549
  25.4 3.2 %collective-permute-start.7 = (f32[32,512]{1,0:T(8,128)S(1)}, f32[32,512]{1,0:T(8,128)S(1)}, u32[]{:S(2)}, u32[]{:S(2)}) collective-permute-start(f32[32,512]{1,0:T(8,128)S(1)} %add_add_fusion.4.mine_ref), channel_id=1, source_target_pairs={{0,1},{1,0},{2,3},{3,2},{4,5},{5,4},{6,7},{7,6},{8,9},{9,8},{10,11... | collective-permute-start | bytes 196616 | tf_op jit(solution)/shard_map/ppermute | solution.py:563
  25.5 11.5 %collective-permute-start.13 = (bf16[64,128]{1,0:T(8,128)(2,1)S(1)}, bf16[64,128]{1,0:T(8,128)(2,1)S(1)}, u32[]{:S(2)}, u32[]{:S(2)}) collective-permute-start(bf16[64,128]{1,0:T(8,128)(2,1)S(1)} %pad_maximum_fusion.1), channel_id=1, source_target_pairs={{0,96},{32,64},{64,32},{96,0},{1,97},{33,65},{65,33},{97,1},{2,98}... | collective-permute-start | bytes 49160 | tf_op jit(solution)/shard_map/ppermute | solution.py:549
  28.6 13.6 %copy-start.1 = (bf16[512,2048]{1,0:T(8,128)(2,1)S(1)}, bf16[512,2048]{1,0:T(8,128)(2,1)}, u32[]{:S(2)}) copy-start(bf16[512,2048]{1,0:T(8,128)(2,1)} %w_ref.5) | copy-start | bytes 6291460
  28.6 13.6 %copy-start.5 = (f32[512]{0:T(512)S(1)}, f32[512]{0:T(512)}, u32[]{:S(2)}) copy-start(f32[512]{0:T(512)} %param.24) | copy-start | bytes 6148
  28.7 13.6 %copy-start.6 = (f32[512]{0:T(512)S(1)}, f32[512]{0:T(512)}, u32[]{:S(2)}) copy-start(f32[512]{0:T(512)} %param.25) | copy-start | bytes 6148
  28.7 14.0 %copy-start = (bf16[16384,128]{1,0:T(8,128)(2,1)S(1)}, bf16[16384,128]{1,0:T(8,128)(2,1)}, u32[]{:S(2)}) copy-start(bf16[16384,128]{1,0:T(8,128)(2,1)} %k_ref.3) | copy-start | bytes 12582916
  36.8 1.3 %collective-permute-start.8 = (f32[32,512]{1,0:T(8,128)S(1)}, f32[32,512]{1,0:T(8,128)S(1)}, u32[]{:S(2)}, u32[]{:S(2)}) collective-permute-start(f32[32,512]{1,0:T(8,128)S(1)} %get-tuple-element.66), channel_id=1, source_target_pairs={{0,1},{1,0},{2,3},{3,2},{4,5},{5,4},{6,7},{7,6},{8,9},{9,8},{10,11... | collective-permute-start | bytes 196616 | tf_op jit(solution)/shard_map/ppermute | solution.py:553
  38.2 6.4 %collective-permute-start.11 = (f32[32,512]{1,0:T(8,128)S(1)}, f32[32,512]{1,0:T(8,128)S(1)}, u32[]{:S(2)}, u32[]{:S(2)}) collective-permute-start(f32[32,512]{1,0:T(8,128)S(1)} %add.90), channel_id=1, source_target_pairs={{0,6},{1,25},{2,26},{3,5},{4,28},{5,3},{6,0},{7,31},{8,16},{9,15},... | collective-permute-start | bytes 196616 | tf_op jit(solution)/shard_map/ppermute | solution.py:558
  39.5 5.2 %collective-permute-start.10 = (f32[32,512]{1,0:T(8,128)S(1)}, f32[32,512]{1,0:T(8,128)S(1)}, u32[]{:S(2)}, u32[]{:S(2)}) collective-permute-start(f32[32,512]{1,0:T(8,128)S(1)} %add.90), channel_id=1, source_target_pairs={{0,5},{1,16},{2,19},{3,6},{4,21},{5,0},{6,3},{7,22},{8,25},{9,12},... | collective-permute-start | bytes 196616 | tf_op jit(solution)/shard_map/ppermute | solution.py:558
  40.0 4.7 %collective-permute-start.9 = (f32[32,512]{1,0:T(8,128)S(1)}, f32[32,512]{1,0:T(8,128)S(1)}, u32[]{:S(2)}, u32[]{:S(2)}) collective-permute-start(f32[32,512]{1,0:T(8,128)S(1)} %add.90), channel_id=1, source_target_pairs={{0,3},{1,8},{2,11},{3,0},{4,13},{5,6},{6,5},{7,14},{8,1},{9,10},{1... | collective-permute-start | bytes 196616 | tf_op jit(solution)/shard_map/ppermute | solution.py:558
  44.7 5.7 %collective-permute-start.16 = (f32[32,512]{1,0:T(8,128)S(1)}, f32[32,512]{1,0:T(8,128)S(1)}, u32[]{:S(2)}, u32[]{:S(2)}) collective-permute-start(f32[32,512]{1,0:T(8,128)S(1)} %add_add_fusion.3), channel_id=1, source_target_pairs={{0,24},{1,7},{2,4},{3,27},{4,2},{5,29},{6,30},{7,1},{8,14},{9,17},... | collective-permute-start | bytes 196616 | tf_op jit(solution)/shard_map/ppermute | solution.py:558
  46.9 5.2 %collective-permute-start.15 = (f32[32,512]{1,0:T(8,128)S(1)}, f32[32,512]{1,0:T(8,128)S(1)}, u32[]{:S(2)}, u32[]{:S(2)}) collective-permute-start(f32[32,512]{1,0:T(8,128)S(1)} %add_add_fusion.3), channel_id=1, source_target_pairs={{0,17},{1,4},{2,7},{3,18},{4,1},{5,20},{6,23},{7,2},{8,13},{9,24},... | collective-permute-start | bytes 196616 | tf_op jit(solution)/shard_map/ppermute | solution.py:558
  47.1 5.0 %collective-permute-start.14 = (f32[32,512]{1,0:T(8,128)S(1)}, f32[32,512]{1,0:T(8,128)S(1)}, u32[]{:S(2)}, u32[]{:S(2)}) collective-permute-start(f32[32,512]{1,0:T(8,128)S(1)} %add_add_fusion.3), channel_id=1, source_target_pairs={{0,9},{1,2},{2,1},{3,10},{4,7},{5,12},{6,15},{7,4},{8,11},{9,0},{1... | collective-permute-start | bytes 196616 | tf_op jit(solution)/shard_map/ppermute | solution.py:558
  52.1 1.5 %collective-permute-start.17 = (f32[32,512]{1,0:T(8,128)S(1)}, f32[32,512]{1,0:T(8,128)S(1)}, u32[]{:S(2)}, u32[]{:S(2)}) collective-permute-start(f32[32,512]{1,0:T(8,128)S(1)} %add_add_fusion.2.mine_ref), channel_id=1, source_target_pairs={{0,1},{1,0},{2,3},{3,2},{4,5},{5,4},{6,7},{7,6},{8,9},{9,8},{10,11... | collective-permute-start | bytes 196616 | tf_op jit(solution)/shard_map/ppermute | solution.py:563
  53.6 21.4 %copy-start.2 = (bf16[2048,128]{1,0:T(8,128)(2,1)S(1)}, bf16[2048,128]{1,0:T(8,128)(2,1)}, u32[]{:S(2)}) copy-start(bf16[2048,128]{1,0:T(8,128)(2,1)} %proj_ref.1) | copy-start | bytes 1572868
  53.6 21.4 %copy-start.3 = (f32[2048]{0:T(1024)S(1)}, f32[2048]{0:T(1024)}, u32[]{:S(2)}) copy-start(f32[2048]{0:T(1024)} %param.27) | copy-start | bytes 24580
  53.6 21.4 %copy-start.4 = (f32[2048]{0:T(1024)S(1)}, f32[2048]{0:T(1024)}, u32[]{:S(2)}) copy-start(f32[2048]{0:T(1024)} %param.28) | copy-start | bytes 24580
  57.5 1.5 %collective-permute-start.18 = (f32[32,1280]{1,0:T(8,128)S(1)}, f32[32,1280]{1,0:T(8,128)S(1)}, u32[]{:S(2)}, u32[]{:S(2)}) collective-permute-start(f32[32,1280]{1,0:T(8,128)S(1)} %get-tuple-element.91), channel_id=1, source_target_pairs={{0,1},{1,0},{2,3},{3,2},{4,5},{5,4},{6,7},{7,6},{8,9},{9,8},{10,11... | collective-permute-start | bytes 491528 | tf_op jit(solution)/shard_map/ppermute | solution.py:553
  59.0 5.7 %collective-permute-start.21 = (bf16[32,1280]{1,0:T(8,128)(2,1)S(1)}, bf16[32,1280]{1,0:T(8,128)(2,1)S(1)}, u32[]{:S(2)}, u32[]{:S(2)}) collective-permute-start(bf16[32,1280]{1,0:T(8,128)(2,1)S(1)} %get-tuple-element.104), channel_id=1, source_target_pairs={{0,6},{1,25},{2,26},{3,5},{4,28},{5,3},{6,0},{7,31},{8,16},{9,15},... | collective-permute-start | bytes 245768 | tf_op jit(solution)/shard_map/ppermute | solution.py:558
  61.1 5.4 %collective-permute-start.20 = (bf16[32,1280]{1,0:T(8,128)(2,1)S(1)}, bf16[32,1280]{1,0:T(8,128)(2,1)S(1)}, u32[]{:S(2)}, u32[]{:S(2)}) collective-permute-start(bf16[32,1280]{1,0:T(8,128)(2,1)S(1)} %get-tuple-element.104), channel_id=1, source_target_pairs={{0,5},{1,16},{2,19},{3,6},{4,21},{5,0},{6,3},{7,22},{8,25},{9,12},... | collective-permute-start | bytes 245768 | tf_op jit(solution)/shard_map/ppermute | solution.py:558
  61.6 4.8 %collective-permute-start.19 = (bf16[32,1280]{1,0:T(8,128)(2,1)S(1)}, bf16[32,1280]{1,0:T(8,128)(2,1)S(1)}, u32[]{:S(2)}, u32[]{:S(2)}) collective-permute-start(bf16[32,1280]{1,0:T(8,128)(2,1)S(1)} %get-tuple-element.104), channel_id=1, source_target_pairs={{0,3},{1,8},{2,11},{3,0},{4,13},{5,6},{6,5},{7,14},{8,1},{9,10},{1... | collective-permute-start | bytes 245768 | tf_op jit(solution)/shard_map/ppermute | solution.py:558
  66.5 5.7 %collective-permute-start.24 = (bf16[32,1280]{1,0:T(8,128)(2,1)S(1)}, bf16[32,1280]{1,0:T(8,128)(2,1)S(1)}, u32[]{:S(2)}, u32[]{:S(2)}) collective-permute-start(bf16[32,1280]{1,0:T(8,128)(2,1)S(1)} %get-tuple-element.102), channel_id=1, source_target_pairs={{0,24},{1,7},{2,4},{3,27},{4,2},{5,29},{6,30},{7,1},{8,14},{9,17},... | collective-permute-start | bytes 245768 | tf_op jit(solution)/shard_map/ppermute | solution.py:558
  67.9 5.4 %collective-permute-start.23 = (bf16[32,1280]{1,0:T(8,128)(2,1)S(1)}, bf16[32,1280]{1,0:T(8,128)(2,1)S(1)}, u32[]{:S(2)}, u32[]{:S(2)}) collective-permute-start(bf16[32,1280]{1,0:T(8,128)(2,1)S(1)} %get-tuple-element.102), channel_id=1, source_target_pairs={{0,17},{1,4},{2,7},{3,18},{4,1},{5,20},{6,23},{7,2},{8,13},{9,24},... | collective-permute-start | bytes 245768 | tf_op jit(solution)/shard_map/ppermute | solution.py:558
  68.4 5.1 %collective-permute-start.22 = (bf16[32,1280]{1,0:T(8,128)(2,1)S(1)}, bf16[32,1280]{1,0:T(8,128)(2,1)S(1)}, u32[]{:S(2)}, u32[]{:S(2)}) collective-permute-start(bf16[32,1280]{1,0:T(8,128)(2,1)S(1)} %get-tuple-element.102), channel_id=1, source_target_pairs={{0,9},{1,2},{2,1},{3,10},{4,7},{5,12},{6,15},{7,4},{8,11},{9,0},{1... | collective-permute-start | bytes 245768 | tf_op jit(solution)/shard_map/ppermute | solution.py:558
  73.5 1.5 %collective-permute-start.25 = (f32[32,1280]{1,0:T(8,128)S(1)}, f32[32,1280]{1,0:T(8,128)S(1)}, u32[]{:S(2)}, u32[]{:S(2)}) collective-permute-start(f32[32,1280]{1,0:T(8,128)S(1)} %add_add_fusion.mine_ref), channel_id=1, source_target_pairs={{0,1},{1,0},{2,3},{3,2},{4,5},{5,4},{6,7},{7,6},{8,9},{9,8},{10,11... | collective-permute-start | bytes 491528 | tf_op jit(solution)/shard_map/ppermute | solution.py:563
  73.7 10.2 %collective-permute-start.26 = (f32[1,64]{1,0:T(1,128)S(1)}, f32[1,64]{1,0:T(1,128)S(1)}, u32[]{:S(2)}, u32[]{:S(2)}) collective-permute-start(f32[1,64]{1,0:T(1,128)S(1)} %slice.17), channel_id=1, source_target_pairs={{0,96},{32,64},{64,32},{96,0},{1,97},{33,65},{65,33},{97,1},{2,98}... | collective-permute-start | bytes 776 | tf_op jit(solution)/shard_map/ppermute | solution.py:549
  75.0 17.8 %copy-start.7 = (s32[32]{0:T(128)S(1)}, s32[32]{0:T(128)}, u32[]{:S(2)}) copy-start(s32[32]{0:T(128)} %param.17) | copy-start | bytes 388
  79.2 13.6 %all-to-all-start = ((bf16[32,32,128]{2,1,0:T(8,128)(2,1)}), bf16[32,32,128]{2,1,0:T(8,128)(2,1)S(1)}, u32[]{:S(2)}, u32[]{:S(2)}) async-start(bf16[32,32,128]{2,1,0:T(8,128)(2,1)} %get-tuple-element.98), calls=%async_computation | async-start | bytes 524288 | tf_op jit(solution)/shard_map/all_to_all | solution.py:640
  83.9 3.6 %collective-permute-start.27 = (f32[1,32]{1,0:T(1,128)S(1)}, f32[1,32]{1,0:T(1,128)S(1)}, u32[]{:S(2)}, u32[]{:S(2)}) collective-permute-start(f32[1,32]{1,0:T(1,128)S(1)} %slice.19), channel_id=1, source_target_pairs={{0,32},{32,0},{64,96},{96,64},{1,33},{33,1},{65,97},{97,65},{2,34}... | collective-permute-start | bytes 392 | tf_op jit(solution)/shard_map/ppermute | solution.py:549
